TPU v7x, 128 devices: a whole 4x4x4 slice. The times are simulated.
128 devices in a mesh: ctx: 32 (over x, z, core), head: 4 (over y).
Axes of the slice: x: 4, y: 4, z: 4, core: 2. Of those that a mesh axis runs over, the one named last changes fastest.
Arguments:
- hidden_in: bfloat16 [16384, 7168], P('ctx', 'head'), may hold values from -6 to 6
- gate_weight: bfloat16 [7168, 192], P('head'), may hold values from -0.09375 to 0.09375
- encoded_queries: bfloat16 [16384, 64, 128], P('ctx', 'head'), may hold values from -12 to 12
- encoded_keys: bfloat16 [16384, 4, 128], P('ctx', 'head'), may hold values from -12 to 12
- value_tensor: bfloat16 [16384, 4, 128], P('ctx', 'head'), may hold values from -6 to 6
- comp_key_weight: float32 [64, 128], replicated, may hold values from -0.75 to 0.75
- comp_value_weight: float32 [64, 128], replicated, may hold values from -0.75 to 0.75
- selection: int32 [256, 4, 16], P('ctx', 'head'), may hold values from 0 to 255, as said below
Outputs:
- attended: bfloat16 [16384, 64, 128], P('ctx', 'head')
Inputs may be any that keep to these rules, and one draw needn't show every extreme that they name: `selection`: entries of one list are distinct and the first is the query block's own block. For one index of ctx and one group, the blocks named over all its query blocks that lie in one other index's shard are at most 4, and some index reaches 4 in every draw.
All inputs are finite; a program needn't handle non-finite values.
Results may differ from a plain program's by a relative error of at most 0.011.
Values may be sent and summed in bfloat16 or wider, within the bound.
No kernel may reach another device: no remote copies, remote signals or barrier semaphores. Data moves between devices by JAX's collectives and lax.ppermute only.
A program may use at most 64 MiB of HBM per device.

v0:
```python
import jax
import jax.numpy as jnp
from jax import lax
from jax.sharding import PartitionSpec as P

WINDOW_TOKENS = 512


def shifted(value, axis, steps):
    count = lax.axis_size(axis)
    initial, last = (max(0, -steps), min(count, count - steps))
    return lax.ppermute(value, axis, [(source, source + steps) for source in range(initial, last)])


def attend(query_block_index, key_rows, value_rows, key_mask, with_null):
    scale = query_block_index.shape[-1] ** (-0.5)
    if key_rows.dtype == jnp.float32:
        scores = (
            jnp.einsum(
                "tgjd,gkd->tgjk",
                query_block_index.astype(jnp.float32),
                key_rows,
                preferred_element_type=jnp.float32,
                precision=lax.Precision.HIGHEST,
            )
            * scale
        )
    else:
        scores = (
            jnp.einsum(
                "tgjd,gkd->tgjk", query_block_index, key_rows, preferred_element_type=jnp.float32
            )
            * scale
        )
    scores = jnp.where(key_mask[:, :, None, :], scores, -1e30)
    peak = jnp.max(scores, axis=-1, keepdims=True)
    if with_null:
        peak = jnp.maximum(peak, 0.0)
    weights = jnp.exp(scores - peak)
    total_w = jnp.sum(weights, axis=-1, keepdims=True)
    if with_null:
        total_w = total_w + jnp.exp(-peak)
    rounded = (weights / total_w).astype(jnp.bfloat16)
    if value_rows.dtype == jnp.float32:
        return jnp.einsum(
            "tgjk,gkd->tgjd",
            rounded.astype(jnp.float32),
            value_rows,
            preferred_element_type=jnp.float32,
            precision=lax.Precision.HIGHEST,
        )
    return jnp.einsum("tgjk,gkd->tgjd", rounded, value_rows, preferred_element_type=jnp.float32)


def body(
    hidden_in,
    gate_weight,
    encoded_queries,
    encoded_keys,
    value_tensor,
    comp_key_weight,
    comp_value_weight,
    selection,
):
    rows_here, heads_here, head_dim = encoded_queries.shape
    block_len = comp_key_weight.shape[0]
    top_count = selection.shape[-1]
    blocks_here = rows_here // block_len
    shard_parts = lax.axis_size("ctx")
    own_index = lax.axis_index("ctx")
    block_count_total = blocks_here * shard_parts
    window_len = WINDOW_TOKENS
    partial_value = jnp.dot(hidden_in, gate_weight, preferred_element_type=jnp.float32)
    logits = lax.psum_scatter(partial_value, "head", scatter_dimension=1, tiled=True)
    gate_values = jax.nn.sigmoid(logits).reshape(rows_here, 1, heads_here, 3)
    key_value = jnp.concatenate([encoded_keys, value_tensor], axis=-1).reshape(
        rows_here, 2 * head_dim
    )
    widened = key_value.astype(jnp.float32).reshape(blocks_here, block_len, 2 * head_dim)
    compress_w = jnp.concatenate([comp_key_weight, comp_value_weight], axis=-1)
    summary = jnp.sum(widened * compress_w[None, :, :], axis=1)
    summaries = lax.all_gather(summary, "ctx", axis=0, tiled=True)
    previous = shifted(key_value, "ctx", 1)
    extended = jnp.concatenate([previous, key_value], axis=0)
    blocks = key_value.reshape(blocks_here, block_len, 2 * head_dim)
    chosen_blocks = selection[:, 0, :]
    all_ids = jnp.arange(block_count_total, dtype=jnp.int32)
    all_blocks = lax.all_gather(blocks, "ctx", axis=0, tiled=True)
    picked = jnp.take(all_blocks, chosen_blocks, axis=0)
    offset = own_index * rows_here
    comp_ends = (all_ids + 1) * block_len - 1
    inner_result = jnp.arange(block_len, dtype=jnp.int32)
    comp_keys = summaries[None, :, :head_dim]
    comp_values = summaries[None, :, head_dim:]

    def per_block(block_num):
        query_start = block_num * block_len
        query_block_index = lax.dynamic_slice_in_dim(
            encoded_queries, query_start, block_len, 0
        ).reshape(block_len, 1, heads_here, head_dim)
        query_pos = offset + query_start + inner_result
        comp_mask = (comp_ends[None, :] <= query_pos[:, None])[:, None, :]
        out_comp = attend(query_block_index, comp_keys, comp_values, comp_mask, True)
        sel_tiles = lax.dynamic_index_in_dim(picked, block_num, 0, keepdims=False).reshape(
            top_count * block_len, 2 * head_dim
        )
        sel_ids = lax.dynamic_index_in_dim(chosen_blocks, block_num, 0, keepdims=False)
        selected_positions = (sel_ids[:, None] * block_len + inner_result[None, :]).reshape(-1)
        sel_mask = (selected_positions[None, :] <= query_pos[:, None])[:, None, :]
        out_sel = attend(
            query_block_index,
            sel_tiles[None, :, :head_dim],
            sel_tiles[None, :, head_dim:],
            sel_mask,
            False,
        )
        win_rows = lax.dynamic_slice_in_dim(extended, query_start, window_len + block_len, 0)
        win_pos = (
            offset + query_start - window_len + jnp.arange(window_len + block_len, dtype=jnp.int32)
        )
        win_mask = (
            (win_pos[None, :] <= query_pos[:, None])
            & (win_pos[None, :] > query_pos[:, None] - window_len)
            & (win_pos[None, :] >= 0)
        )
        out_win = attend(
            query_block_index,
            win_rows[None, :, :head_dim],
            win_rows[None, :, head_dim:],
            win_mask[:, None, :],
            False,
        )
        gate_block_rows = lax.dynamic_slice_in_dim(gate_values, query_start, block_len, 0)
        merged = (
            gate_block_rows[..., 0:1] * out_comp
            + gate_block_rows[..., 1:2] * out_sel
            + gate_block_rows[..., 2:3] * out_win
        )
        return merged.reshape(block_len, heads_here, head_dim).astype(jnp.bfloat16)

    results = lax.map(per_block, jnp.arange(blocks_here, dtype=jnp.int32))
    return results.reshape(rows_here, heads_here, head_dim)


def solution(mesh):
    return jax.shard_map(
        body,
        mesh=mesh,
        in_specs=(
            P("ctx", "head"),
            P("head", None),
            P("ctx", "head", None),
            P("ctx", "head", None),
            P("ctx", "head", None),
            P(),
            P(),
            P("ctx", "head", None),
        ),
        out_specs=P("ctx", "head", None),
        check_vma=False,
    )
```

profile of v0, /device:TPU:1, one launch (start us, length us, event | category | flops | bytes accessed | tf_op | source)
XLA Modules:
  0.0 289.9 jit_solution(7371172152859489917)
XLA Ops:
  8.9 2.6 fusion.55
  12.4 4.9 %collective-permute-start = (bf16[512,256]{1,0:T(8,128)(2,1)}, bf16[512,256]{1,0:T(8,128)(2,1)S(1)}, u32[]{:S(2)}, u32[]{:S(2)}) collective-permute-start(bf16[512,256]{1,0:T(8,128)(2,1)} %bitcast.175), channel_id=1, source_target_pairs={{0,4},{4,8},{8,12},{12,16},{16,20},{20,24},{24,28},{28,32},{32,36}... | collective-permute-start | bytes 786440 | tf_op jit(solution)/shard_map/ppermute | solution.py:12
  18.5 24.4 %all_gather.6 = f32[256,256]{1,0:T(8,128)S(1)} all-gather(f32[8,256]{1,0:T(8,128)S(1)} %multiply_reduce_fusion), channel_id=1, replica_groups=mesh['ctx'=32,'head'=4] {'ctx'}, dimensions={0}, use_global_device_ids=true | all-gather | bytes 270336 | tf_op jit(solution)/shard_map/all_gather | solution.py:82
  43.7 1.8 pad_maximum_fusion
  47.2 24.0 %all-gather.2.cloned.1.call-done = bf16[256,64,256]{2,1,0:T(8,128)(2,1)} async-done(((bf16[8,64,256]{2,1,0:T(8,128)(2,1)}), bf16[256,64,256]{2,1,0:T(8,128)(2,1)}) %all-gather.2.cloned.1.call-update) | async-done | bytes 8388624 | tf_op jit(solution)/shard_map/all_gather | solution.py:88
  71.2 6.2 %gather_fusion = bf16[128,64,256]{2,1,0:T(8,128)(2,1)} fusion(bf16[256,64,256]{2,1,0:T(8,128)(2,1)} %all-gather.2.cloned.1.call-done, s32[1024]{0:T(1024)S(1)} %pad_clamp_fusion), kind=kCustom, calls=%fused_computation | custom fusion | bytes 8389120 | tf_op jit(solution)/shard_map/jit(_take)/gather | solution.py:89
  77.4 4.6 %broadcast_select_fusion = bf16[8,16,64,256]{3,2,1,0:T(8,128)(2,1)} fusion(bf16[8,16,64,256]{3,2,1,0:T(8,128)(2,1)} %bitcast.173, pred[8,16]{1,0:T(8,128)(4,1)S(1)} %compare_and_fusion), kind=kLoop, calls=%fused_computation.68 | loop fusion | flops 2097152 | bytes 8388736 | tf_op jit(solution)/shard_map/jit(_take)/select_n | solution.py:89
  81.9 200.5 %while.15 = (s32[]{:T(128)}, bf16[8,64,16,128]{3,2,1,0:T(8,128)(2,1)}, s32[8]{0:T(128)S(1)}, f32[512,1,16,3]{0,3,2,1:T(4,128)}, s32[]{:T(128)}, /*index=5*/bf16[...) while((s32[]{:T(128)}, ...), condition=%wide.region_9.10_spmd.clone.clone, body=%wide.region_2.9_spmd.clone.clone.sunk | while | flops 1666942592 | bytes 35800808 | solution.py:141
  89.3 2.1 fusion.84
  92.5 3.7 %fusion.85 = f32[1,128,64,16]{1,3,2,0:T(8,128)} fusion(bf16[64,16,1024]{2,0,1:T(8,128)(2,1)} %fusion.84, bf16[1024,256]{1,0:T(8,128)(2,1)S(1)} %bitcast.172, f32[64,16]{1,0:T(8,128)S(1)} %bitcast.180), kind=kOutput, calls=%fused_computation.23.clone.1 | convolution fusion | flops 268566528 | bytes 2916352 | tf_op jit(solution)/shard_map/while/body/eval_jaxpr/tgjk,gkd->tgjd/dot_general | solution.py:52
  98.3 2.7 fusion.88
  101.1 1.6 fusion.89
  104.2 2.8 fusion.92
  114.4 2.1 fusion.84
  117.5 3.7 %fusion.85 = f32[1,128,64,16]{1,3,2,0:T(8,128)} fusion(bf16[64,16,1024]{2,0,1:T(8,128)(2,1)} %fusion.84, bf16[1024,256]{1,0:T(8,128)(2,1)S(1)} %bitcast.172, f32[64,16]{1,0:T(8,128)S(1)} %bitcast.180), kind=kOutput, calls=%fused_computation.23.clone.1 | convolution fusion | flops 268566528 | bytes 2916352 | tf_op jit(solution)/shard_map/while/body/eval_jaxpr/tgjk,gkd->tgjd/dot_general | solution.py:52
  123.4 2.7 fusion.88
  126.2 1.6 fusion.89
  129.3 2.8 fusion.92
  139.4 2.1 fusion.84
  142.6 3.7 %fusion.85 = f32[1,128,64,16]{1,3,2,0:T(8,128)} fusion(bf16[64,16,1024]{2,0,1:T(8,128)(2,1)} %fusion.84, bf16[1024,256]{1,0:T(8,128)(2,1)S(1)} %bitcast.172, f32[64,16]{1,0:T(8,128)S(1)} %bitcast.180), kind=kOutput, calls=%fused_computation.23.clone.1 | convolution fusion | flops 268566528 | bytes 2916352 | tf_op jit(solution)/shard_map/while/body/eval_jaxpr/tgjk,gkd->tgjd/dot_general | solution.py:52
  148.4 2.7 fusion.88
  151.2 1.6 fusion.89
  154.4 2.8 fusion.92
  164.5 2.1 fusion.84
  167.7 3.7 %fusion.85 = f32[1,128,64,16]{1,3,2,0:T(8,128)} fusion(bf16[64,16,1024]{2,0,1:T(8,128)(2,1)} %fusion.84, bf16[1024,256]{1,0:T(8,128)(2,1)S(1)} %bitcast.172, f32[64,16]{1,0:T(8,128)S(1)} %bitcast.180), kind=kOutput, calls=%fused_computation.23.clone.1 | convolution fusion | flops 268566528 | bytes 2916352 | tf_op jit(solution)/shard_map/while/body/eval_jaxpr/tgjk,gkd->tgjd/dot_general | solution.py:52
  173.5 2.7 fusion.88
  176.3 1.6 fusion.89
  179.4 2.8 fusion.92
  189.6 2.1 fusion.84
  192.7 3.7 %fusion.85 = f32[1,128,64,16]{1,3,2,0:T(8,128)} fusion(bf16[64,16,1024]{2,0,1:T(8,128)(2,1)} %fusion.84, bf16[1024,256]{1,0:T(8,128)(2,1)S(1)} %bitcast.172, f32[64,16]{1,0:T(8,128)S(1)} %bitcast.180), kind=kOutput, calls=%fused_computation.23.clone.1 | convolution fusion | flops 268566528 | bytes 2916352 | tf_op jit(solution)/shard_map/while/body/eval_jaxpr/tgjk,gkd->tgjd/dot_general | solution.py:52
  198.5 2.7 fusion.88
  201.3 1.6 fusion.89
  204.5 2.8 fusion.92
  214.6 2.1 fusion.84
  217.8 3.7 %fusion.85 = f32[1,128,64,16]{1,3,2,0:T(8,128)} fusion(bf16[64,16,1024]{2,0,1:T(8,128)(2,1)} %fusion.84, bf16[1024,256]{1,0:T(8,128)(2,1)S(1)} %bitcast.172, f32[64,16]{1,0:T(8,128)S(1)} %bitcast.180), kind=kOutput, calls=%fused_computation.23.clone.1 | convolution fusion | flops 268566528 | bytes 2916352 | tf_op jit(solution)/shard_map/while/body/eval_jaxpr/tgjk,gkd->tgjd/dot_general | solution.py:52
  223.6 2.7 fusion.88
  226.4 1.6 fusion.89
  229.5 2.8 fusion.92
  239.7 2.1 fusion.84
  242.8 3.7 %fusion.85 = f32[1,128,64,16]{1,3,2,0:T(8,128)} fusion(bf16[64,16,1024]{2,0,1:T(8,128)(2,1)} %fusion.84, bf16[1024,256]{1,0:T(8,128)(2,1)S(1)} %bitcast.172, f32[64,16]{1,0:T(8,128)S(1)} %bitcast.180), kind=kOutput, calls=%fused_computation.23.clone.1 | convolution fusion | flops 268566528 | bytes 2916352 | tf_op jit(solution)/shard_map/while/body/eval_jaxpr/tgjk,gkd->tgjd/dot_general | solution.py:52
  248.7 2.7 fusion.88
  251.5 1.6 fusion.89
  254.6 2.8 fusion.92
  264.8 2.1 fusion.84
  267.9 3.7 %fusion.85 = f32[1,128,64,16]{1,3,2,0:T(8,128)} fusion(bf16[64,16,1024]{2,0,1:T(8,128)(2,1)} %fusion.84, bf16[1024,256]{1,0:T(8,128)(2,1)S(1)} %bitcast.172, f32[64,16]{1,0:T(8,128)S(1)} %bitcast.180), kind=kOutput, calls=%fused_computation.23.clone.1 | convolution fusion | flops 268566528 | bytes 2916352 | tf_op jit(solution)/shard_map/while/body/eval_jaxpr/tgjk,gkd->tgjd/dot_general | solution.py:52
  273.7 2.7 fusion.88
  276.5 1.6 fusion.89
  279.7 2.8 fusion.92
  (233 shorter events, 83.3 us)
Async XLA Ops:
  7.4 1.5 copy-start
  7.4 4.2 %copy-start.2 = (bf16[512,1,128]{2,0,1:T(8,128)(2,1)S(1)}, bf16[512,1,128]{2,0,1:T(8,128)(2,1)}, u32[]{:S(2)}) copy-start(bf16[512,1,128]{2,0,1:T(8,128)(2,1)} %param.13) | copy-start | bytes 393220
  7.4 4.2 %copy-start.3 = (bf16[512,1,128]{2,0,1:T(8,128)(2,1)S(1)}, bf16[512,1,128]{2,0,1:T(8,128)(2,1)}, u32[]{:S(2)}) copy-start(bf16[512,1,128]{2,0,1:T(8,128)(2,1)} %param.14) | copy-start | bytes 393220
  7.4 10.0 %copy-start.6 = (s32[8,1,16]{2,1,0:T(1,128)S(1)}, s32[8,1,16]{2,1,0:T(1,128)}, u32[]{:S(2)}) copy-start(s32[8,1,16]{2,1,0:T(1,128)} %param.17) | copy-start | bytes 1540
  7.4 10.1 %copy-start.4 = (f32[64,128]{1,0:T(8,128)S(1)}, f32[64,128]{1,0:T(8,128)}, u32[]{:S(2)}) copy-start(f32[64,128]{1,0:T(8,128)} %param.16) | copy-start | bytes 98308
  7.4 10.1 %copy-start.5 = (f32[64,128]{1,0:T(8,128)S(1)}, f32[64,128]{1,0:T(8,128)}, u32[]{:S(2)}) copy-start(f32[64,128]{1,0:T(8,128)} %param.15) | copy-start | bytes 98308
  7.4 38.1 %reduce-scatter.2.cloned.1.call-start = ((), (), s32[]{:S(2)}) async-start(), calls=%async_computation.1 | async-start | bytes 491520 | tf_op jit(solution)/shard_map/reduce_scatter | solution.py:74
  11.5 59.7 %all-gather.2.cloned.1.call-start = ((), (), s32[]{:S(2)}) async-start(), calls=%async_computation.2 | async-start | bytes 8650752 | tf_op jit(solution)/shard_map/all_gather | solution.py:88
  11.7 0.7 copy-start.1
  12.4 31.3 %collective-permute-start = (bf16[512,256]{1,0:T(8,128)(2,1)}, bf16[512,256]{1,0:T(8,128)(2,1)S(1)}, u32[]{:S(2)}, u32[]{:S(2)}) collective-permute-start(bf16[512,256]{1,0:T(8,128)(2,1)} %bitcast.175), channel_id=1, source_target_pairs={{0,4},{4,8},{8,12},{12,16},{16,20},{20,24},{24,28},{28,32},{32,36}... | collective-permute-start | bytes 786440 | tf_op jit(solution)/shard_map/ppermute | solution.py:12
Sparse Core Ops, SparseCore 0:
  11.6 22.3 reduce-scatter.1
Sparse Core Ops, SparseCore 1:
  14.5 56.6 all-gather.1
where the time goes:
time: 293 us; the launch traced here: 290 us
  matrix products  108 us (37%)
  other arithmetic  51.1 us (17%)
  local copies, waits for them, and re-layouts  41.5 us (14%)
  blocking collectives  24.4 us (8%)
  waiting for transfers between devices  24.1 us (8%)
  loops' own time  20.8 us (7%)
  between operations  15 us (5%)
  starting transfers between devices  5.02 us (2%)
    dot_general x16, matrix products, attend(): jnp.einsum('tgjk,gkd->tgjd', rounded, value_rows, preferred_element_type=...  51.4 us
    all_gather x1, blocking collectives, body(): summaries = lax.all_gather(summary, 'ctx', axis=0, tiled=True)  24.4 us
    all_gather x1, waiting for transfers between devices, body(): all_blocks = lax.all_gather(blocks, 'ctx', axis=0, tiled=True)  24 us
    another operation x16, other arithmetic  21.9 us
    dot_general x8, matrix products, attend(): jnp.einsum('tgjk,gkd->tgjd', rounded.astype(jnp.float32), value_rows, pre...  21.3 us
    another operation x1, loops' own time, body(): results = lax.map(per_block, jnp.arange(blocks_here, dtype=jnp.int32))  20.8 us
    dot_general x16, matrix products, attend(): jnp.einsum('tgjd,gkd->tgjk', query_block_index, key_rows, preferred_eleme...  20 us
    reduce_sum x24, other arithmetic, attend(): total_w = jnp.sum(weights, axis=-1, keepdims=True)  17.6 us
  transfers between devices with their start and end apart: 3, of which 1 were waited for; matrix products, arithmetic and copies ran while one was open for 2% of the time, Pallas kernels for 0%

commit v1 on v0

v1 whole, which is shorter than its diff:
```python
import functools
import math

import jax
import jax.numpy as jnp
from jax import lax
from jax.experimental import pallas as pl
from jax.experimental.pallas import tpu as pltpu
from jax.sharding import PartitionSpec as P

WINDOW_TOKENS = 512
MASKED = -1e30
LOG2E = 1.4426950408889634
ROW_TILE = 256
NT = (((1,), (1,)), ((), ()))


def shifted(value, axis, steps):
    count = lax.axis_size(axis)
    initial, last = (max(0, -steps), min(count, count - steps))
    return lax.ppermute(value, axis, [(source, source + steps) for source in range(initial, last)])


def token_one_hot(rows, first_row, heads):
    token = (lax.broadcasted_iota(jnp.int32, (rows, 128), 0) + first_row) // heads
    lane = lax.broadcasted_iota(jnp.int32, (rows, 128), 1)
    return jnp.where(token == lane, 1.0, 0.0).astype(jnp.bfloat16)


def softmax_parts(scores, factor):
    peak = jnp.max(scores, axis=-1, keepdims=True)
    return peak, jnp.exp2(scores * factor - peak * factor)


def near_kernel(
    block_len, heads, index_ref, q_ref, kv_ref, summary_hi_ref, summary_lo_ref, comp_ref, win_ref, bias_ref
):
    head_dim = q_ref.shape[-1]
    rows = block_len * heads
    blk = pl.program_id(0)
    factor = LOG2E / math.sqrt(head_dim)
    span = WINDOW_TOKENS + block_len
    own = index_ref[0]
    first = pl.multiple_of(blk * block_len, block_len)
    key = lax.broadcasted_iota(jnp.int32, (span, 128), 0)
    tok = lax.broadcasted_iota(jnp.int32, (span, 128), 1)
    start = own * (kv_ref.shape[0] // 2) + blk * block_len
    seen = (key > tok) & (key <= tok + WINDOW_TOKENS) & (key + start >= WINDOW_TOKENS)
    bias_ref[...] = jnp.where(seen, 0.0, MASKED).astype(jnp.bfloat16)
    keys = jnp.concatenate([kv_ref[pl.ds(first, span), :head_dim], bias_ref[...]], axis=1)
    values = jnp.concatenate(
        [kv_ref[pl.ds(first, span), head_dim:], jnp.ones((span, 128), jnp.bfloat16)], axis=1
    )
    comp_keys = jnp.concatenate([summary_hi_ref[:, :head_dim], summary_lo_ref[:, :head_dim]], axis=1)
    comp_values = jnp.concatenate([summary_hi_ref[:, head_dim:], summary_lo_ref[:, head_dim:]], axis=1)
    count = comp_keys.shape[0]
    block_index = own * (kv_ref.shape[0] // 2 // block_len) + blk
    for at in range(0, rows, ROW_TILE):
        q = q_ref[pl.ds(at, ROW_TILE), :]
        hot = token_one_hot(ROW_TILE, at, heads)
        scores = lax.dot_general(
            jnp.concatenate([q, hot], axis=1), keys, NT, preferred_element_type=jnp.float32
        )
        _, weights = softmax_parts(scores, factor)
        both = jnp.dot(weights.astype(jnp.bfloat16), values, preferred_element_type=jnp.float32)
        win_ref[pl.ds(at, ROW_TILE), :] = both[:, :head_dim] / both[:, head_dim:]
        scores = lax.dot_general(
            jnp.concatenate([q, q], axis=1), comp_keys, NT, preferred_element_type=jnp.float32
        )
        token = (lax.broadcasted_iota(jnp.int32, (ROW_TILE, count), 0) + at) // heads
        limit = block_index + jnp.where(token == block_len - 1, 1, 0)
        lane = lax.broadcasted_iota(jnp.int32, (ROW_TILE, count), 1)
        scores = jnp.where(lane < limit, scores, MASKED)
        peak = jnp.maximum(jnp.max(scores, axis=-1, keepdims=True), 0.0)
        weights = jnp.exp2(scores * factor - peak * factor)
        total = jnp.sum(weights, axis=-1, keepdims=True) + jnp.exp2(-peak * factor)
        both = jnp.dot(weights.astype(jnp.bfloat16), comp_values, preferred_element_type=jnp.float32)
        comp_ref[pl.ds(at, ROW_TILE), :] = (both[:, :head_dim] + both[:, head_dim:]) / total


def far_kernel(
    block_len, heads, picks, pick_ref, index_ref, q_ref, logit_ref, comp_ref, win_ref, all_ref, out_ref,
    kv_ref, bias_ref, sems,
):
    head_dim = q_ref.shape[-1]
    rows = block_len * heads
    blk = pl.program_id(0)
    steps = pl.num_programs(0)
    factor = LOG2E / math.sqrt(head_dim)
    own_block = index_ref[0] * steps + blk
    slot = lax.rem(blk, 2)

    def fetch(step, into, pick):
        source = pl.multiple_of(pick_ref[step * picks + pick] * block_len, block_len)
        return pltpu.make_async_copy(
            all_ref.at[pl.ds(source, block_len), :],
            kv_ref.at[into, pl.ds(pick * block_len, block_len), :],
            sems.at[into, pick],
        )

    @pl.when(blk == 0)
    def _():
        for pick in range(picks):
            fetch(blk, slot, pick).start()

    @pl.when(blk + 1 < steps)
    def _():
        for pick in range(picks):
            fetch(blk + 1, 1 - slot, pick).start()

    key = lax.broadcasted_iota(jnp.int32, (block_len, 128), 0)
    tok = lax.broadcasted_iota(jnp.int32, (block_len, 128), 1)
    for pick in range(picks):
        chosen = pick_ref[blk * picks + pick]
        last = jnp.where(chosen < own_block, block_len, jnp.where(chosen == own_block, 0, -2 * block_len))
        bias_ref[pl.ds(pick * block_len, block_len), :] = jnp.where(
            key <= tok + last, 0.0, MASKED
        ).astype(jnp.bfloat16)
    gate = jax.nn.sigmoid(logit_ref[...])
    columns = gate.shape[1]
    gate_hi = gate.astype(jnp.bfloat16)
    gate_lo = (gate - gate_hi.astype(jnp.float32)).astype(jnp.bfloat16)
    spread = jnp.zeros((128 - block_len, columns), jnp.bfloat16)
    gate_hi = jnp.concatenate([gate_hi, spread], axis=0)
    gate_lo = jnp.concatenate([gate_lo, spread], axis=0)
    for pick in range(picks):
        fetch(blk, slot, pick).wait()
    keys = jnp.concatenate([kv_ref[slot, :, :head_dim], bias_ref[...]], axis=1)
    values = jnp.concatenate(
        [kv_ref[slot, :, head_dim:], jnp.ones((picks * block_len, 128), jnp.bfloat16)], axis=1
    )
    ones = jnp.ones((columns, head_dim), jnp.bfloat16)
    for at in range(0, rows, ROW_TILE):
        q = q_ref[pl.ds(at, ROW_TILE), :]
        hot = token_one_hot(ROW_TILE, at, heads)
        scores = lax.dot_general(
            jnp.concatenate([q, hot], axis=1), keys, NT, preferred_element_type=jnp.float32
        )
        _, weights = softmax_parts(scores, factor)
        both = jnp.dot(weights.astype(jnp.bfloat16), values, preferred_element_type=jnp.float32)
        sel = both[:, :head_dim] / both[:, head_dim:]
        of_token_hi = jnp.dot(hot, gate_hi, preferred_element_type=jnp.float32)
        of_token_lo = jnp.dot(hot, gate_lo, preferred_element_type=jnp.float32)
        head = lax.rem(lax.broadcasted_iota(jnp.int32, (ROW_TILE, columns), 0) + at, heads)
        column = lax.broadcasted_iota(jnp.int32, (ROW_TILE, columns), 1)

        def gate_of(branch):
            mine = column == head * 3 + branch
            return jnp.dot(
                jnp.where(mine, of_token_hi, 0.0).astype(jnp.bfloat16), ones,
                preferred_element_type=jnp.float32,
            ) + jnp.dot(
                jnp.where(mine, of_token_lo, 0.0).astype(jnp.bfloat16), ones,
                preferred_element_type=jnp.float32,
            )

        merged = (
            gate_of(0) * comp_ref[pl.ds(at, ROW_TILE), :]
            + gate_of(1) * sel
            + gate_of(2) * win_ref[pl.ds(at, ROW_TILE), :]
        )
        out_ref[pl.ds(at, ROW_TILE), :] = merged.astype(jnp.bfloat16)


def body(
    hidden_in,
    gate_weight,
    encoded_queries,
    encoded_keys,
    value_tensor,
    comp_key_weight,
    comp_value_weight,
    selection,
):
    rows_here, heads_here, head_dim = encoded_queries.shape
    block_len = comp_key_weight.shape[0]
    picks = selection.shape[-1]
    blocks_here = rows_here // block_len
    shard_parts = lax.axis_size("ctx")
    rows = block_len * heads_here
    index = lax.axis_index("ctx").astype(jnp.int32).reshape(1)

    key_value = jnp.concatenate([encoded_keys, value_tensor], axis=-1).reshape(rows_here, 2 * head_dim)
    gathered = lax.all_gather(key_value, "ctx", axis=0, tiled=True)

    partial_value = jnp.dot(hidden_in, gate_weight, preferred_element_type=jnp.float32)
    logits = lax.psum_scatter(partial_value, "head", scatter_dimension=1, tiled=True)

    widened = key_value.astype(jnp.float32).reshape(blocks_here, block_len, 2 * head_dim)
    compress_w = jnp.concatenate([comp_key_weight, comp_value_weight], axis=-1)
    summary = jnp.sum(widened * compress_w[None, :, :], axis=1)
    summaries = lax.all_gather(summary, "ctx", axis=0, tiled=True)
    summary_hi = summaries.astype(jnp.bfloat16)
    summary_lo = (summaries - summary_hi.astype(jnp.float32)).astype(jnp.bfloat16)
    previous = shifted(key_value, "ctx", 1)
    extended = jnp.concatenate([previous, key_value], axis=0)
    queries = encoded_queries.reshape(rows_here * heads_here, head_dim)
    blocks_total = blocks_here * shard_parts

    tile = pl.BlockSpec((rows, head_dim), lambda b, *_: (b, 0))
    whole = lambda shape: pl.BlockSpec(shape, lambda b, *_: (0, 0))
    branch = jax.ShapeDtypeStruct((rows_here * heads_here, head_dim), jnp.float32)
    comp, win = pl.pallas_call(
        functools.partial(near_kernel, block_len, heads_here),
        out_shape=(branch, branch),
        grid_spec=pltpu.PrefetchScalarGridSpec(
            num_scalar_prefetch=1,
            grid=(blocks_here,),
            in_specs=[
                tile,
                whole((2 * rows_here, 2 * head_dim)),
                whole((blocks_total, 2 * head_dim)),
                whole((blocks_total, 2 * head_dim)),
            ],
            out_specs=(tile, tile),
            scratch_shapes=[pltpu.VMEM((WINDOW_TOKENS + block_len, 128), jnp.bfloat16)],
        ),
        compiler_params=pltpu.CompilerParams(vmem_limit_bytes=40 << 20),
        cost_estimate=pl.CostEstimate(
            flops=4 * rows_here * heads_here * head_dim * 832,
            transcendentals=rows_here * heads_here * 832,
            bytes_accessed=12 << 20,
        ),
        name="near",
    )(index, queries, extended, summary_hi, summary_lo)

    out = pl.pallas_call(
        functools.partial(far_kernel, block_len, heads_here, picks),
        out_shape=jax.ShapeDtypeStruct((rows_here * heads_here, head_dim), jnp.bfloat16),
        grid_spec=pltpu.PrefetchScalarGridSpec(
            num_scalar_prefetch=2,
            grid=(blocks_here,),
            in_specs=[
                tile,
                pl.BlockSpec((block_len, logits.shape[1]), lambda b, *_: (b, 0)),
                tile,
                tile,
                pl.BlockSpec(memory_space=pl.ANY),
            ],
            out_specs=tile,
            scratch_shapes=[
                pltpu.VMEM((2, picks * block_len, 2 * head_dim), jnp.bfloat16),
                pltpu.VMEM((picks * block_len, 128), jnp.bfloat16),
                pltpu.SemaphoreType.DMA((2, picks)),
            ],
        ),
        compiler_params=pltpu.CompilerParams(vmem_limit_bytes=40 << 20),
        cost_estimate=pl.CostEstimate(
            flops=4 * rows_here * heads_here * head_dim * 1024,
            transcendentals=rows_here * heads_here * 1024,
            bytes_accessed=16 << 20,
        ),
        name="far",
    )(selection.reshape(-1), index, queries, logits, comp, win, gathered)
    return out.reshape(rows_here, heads_here, head_dim)


def solution(mesh):
    return jax.shard_map(
        body,
        mesh=mesh,
        in_specs=(
            P("ctx", "head"),
            P("head", None),
            P("ctx", "head", None),
            P("ctx", "head", None),
            P("ctx", "head", None),
            P(),
            P(),
            P("ctx", "head", None),
        ),
        out_specs=P("ctx", "head", None),
        check_vma=False,
    )
```

time: 293 us -> 112 us (0.38)
  matrix products: 108 us -> 2.59 us
  other arithmetic: 51.1 us -> 2.68 us
  Pallas kernels: 0 us -> 43.9 us
  local copies, waits for them, and re-layouts: 41.5 us -> 15.3 us
  waiting for transfers between devices: 24.1 us -> 2.56 us
  loops' own time: 20.8 us -> 0 us
    dot_general x49 -> x0, matrix products: 108 us -> none  [the longest x16 51.4 us: attend(): jnp.einsum('tgjk,gkd->tgjd', rounded, value_rows, preferred_element_type=...]
    pallas_call x0 -> x2, Pallas kernels: none -> 43.9 us  [the longest x1 26.9 us: body(): pl.pallas_call(functools.partial(far_kernel, block_len, heads_here, picks...]
    another operation x16 -> x0, other arithmetic: 21.9 us -> none
    all_gather x1, waiting for transfers between devices: 24 us -> 2.52 us  [body(): gathered = lax.all_gather(key_value, 'ctx', axis=0, tiled=True)]
    dynamic_slice x24 -> x0, local copies, waits for them, and re-layouts: 21.2 us -> none  [the longest x8 8.66 us: per_block(): lax.dynamic_index_in_dim(picked, block_num, 0, keepdims=False)]
    another operation x1 -> x0, loops' own time: 20.8 us -> none  [body(): results = lax.map(per_block, jnp.arange(blocks_here, dtype=jnp.int32))]
    reduce_sum x24 -> x0, other arithmetic: 17.6 us -> none  [attend(): total_w = jnp.sum(weights, axis=-1, keepdims=True)]
    unnamed x15 -> x29, local copies, waits for them, and re-layouts: 2.18 us -> 15.2 us
  transfers between devices with their start and end apart: 3 -> 3, of which waited for: 1 -> 1; matrix products, arithmetic and copies ran while one was open for 2% -> 4% of each run, Pallas kernels for 0% -> 15%
where the time goes in v1:
time: 112 us; the launch traced here: 111 us
  Pallas kernels  43.9 us (39%)
  blocking collectives  24.4 us (22%)
  local copies, waits for them, and re-layouts  15.3 us (14%)
  between operations  15 us (13%)
  starting transfers between devices  5.02 us (4%)
  other arithmetic  2.68 us (2%)
  matrix products  2.59 us (2%)
  waiting for transfers between devices  2.56 us (2%)
    pallas_call x1, Pallas kernels, body(): pl.pallas_call(functools.partial(far_kernel, block_len, heads_here, picks...  26.9 us
    all_gather x1, blocking collectives, body(): summaries = lax.all_gather(summary, 'ctx', axis=0, tiled=True)  24.4 us
    pallas_call x1, Pallas kernels, body(): pl.pallas_call(functools.partial(near_kernel, block_len, heads_here), out...  17 us
    unnamed x29, local copies, waits for them, and re-layouts  15.2 us
    ppermute x1, starting transfers between devices, shifted(): lax.ppermute(value, axis, [(source, source + steps) for source in range(i...  4.94 us
    unnamed x1, matrix products  2.59 us
    all_gather x1, waiting for transfers between devices, body(): gathered = lax.all_gather(key_value, 'ctx', axis=0, tiled=True)  2.52 us
  transfers between devices with their start and end apart: 3, of which 1 were waited for; matrix products, arithmetic and copies ran while one was open for 4% of the time, Pallas kernels for 15%

profile of v1, /device:TPU:1, one launch (start us, length us, event | category | flops | bytes accessed | tf_op | source)
XLA Modules:
  0.0 111.5 jit_solution(5750995710665969074)
XLA Ops:
  7.4 0.0 copy-start
  7.4 0.0 copy-start.8
  7.4 0.0 copy-start.9
  7.4 0.0 copy-start.10
  7.4 0.0 copy-start.11
  7.4 0.0 copy-start.12
  7.4 0.0 reduce-scatter.4.cloned.1.call-start
  7.4 1.4 %copy-done = bf16[512,1792]{1,0:T(8,128)(2,1)S(1)} copy-done((bf16[512,1792]{1,0:T(8,128)(2,1)S(1)}, bf16[512,1792]{1,0:T(8,128)(2,1)}, u32[]{:S(2)}) %copy-start) | copy-done | bytes 1835032
  8.9 2.6 %convolution_bitcast_fusion = f32[192,512]{1,0:T(8,128)} fusion(bf16[512,1792]{1,0:T(8,128)(2,1)S(1)} %copy-done, bf16[1792,192]{0,1:T(8,128)(2,1)} %param.9), kind=kOutput, calls=%fused_computation | convolution fusion | flops 352321536 | bytes 2916352
  11.5 0.0 reduce-scatter.4.cloned.1.call-update
  11.5 0.0 all-gather.3.cloned.1.call-start
  11.5 0.0 copy-done.8
  11.6 0.0 copy-done.9
  11.6 0.0 copy-start.7
  11.6 0.7 copy-done.7
  12.3 0.0 all-gather.3.cloned.1.call-update
  12.3 4.9 %collective-permute-start = (bf16[512,256]{1,0:T(8,128)(2,1)}, bf16[512,256]{1,0:T(8,128)(2,1)S(1)}, u32[]{:S(2)}, u32[]{:S(2)}) collective-permute-start(bf16[512,256]{1,0:T(8,128)(2,1)} %bitcast.15), channel_id=1, source_target_pairs={{0,4},{4,8},{8,12},{12,16},{16,20},{20,24},{24,28},{28,32},{32,36}... | collective-permute-start | bytes 786440 | tf_op jit(solution)/shard_map/ppermute | solution.py:21
  17.3 0.0 copy-done.10
  17.3 0.0 copy-done.11
  17.3 1.0 fusion
  18.4 24.4 %all_gather.6 = f32[256,256]{1,0:T(8,128)S(1)} all-gather(f32[8,256]{1,0:T(8,128)S(1)} %fusion), channel_id=1, replica_groups=mesh['ctx'=32,'head'=4] {'ctx'}, dimensions={0}, use_global_device_ids=true | all-gather | bytes 270336 | tf_op jit(solution)/shard_map/all_gather | solution.py:192
  42.8 0.6 broadcast.12
  43.4 0.0 copy-done.12
  43.4 0.6 reduce.3
  44.0 0.1 reshape.24.pick_ref
  44.1 0.0 collective-permute-done
  44.1 1.0 pad_maximum_fusion.kv_ref
  45.1 0.0 copy-start.5
  45.1 1.6 %copy-done.5 = bf16[512,16,128]{2,1,0:T(8,128)(2,1)S(1)} copy-done((bf16[512,16,128]{2,1,0:T(8,128)(2,1)S(1)}, bf16[512,16,128]{2,1,0:T(8,128)(2,1)}, u32[]{:S(2)}) %copy-start.5) | copy-done | bytes 2097176
  46.7 17.0 %near.1 = (f32[8192,128]{1,0:T(8,128)S(1)}, f32[8192,128]{1,0:T(8,128)S(1)}) custom-call(s32[1]{0:T(128)} %bitcast.index_ref, bf16[8192,128]{1,0:T(8,128)(2,1)S(1)} %bitcast.12, bf16[1024,256]{1,0:T(8,128)(2,1)S(1)} %pad_maximum_fusion.kv_ref, bf16[256,256]{1,0:T(8,128)(2,1)S(1)} %get-tuple-element.10.summary_hi_ref, ...), custom_call_target="tpu_custom_call" | custom-call | flops 3489660928 | bytes 12582912 | tf_op jit(solution)/shard_map/near/pallas_call | solution.py:203
  63.7 0.0 copy-start.1
  63.7 2.0 %copy-done.1 = f32[8192,128]{1,0:T(8,128)} copy-done((f32[8192,128]{1,0:T(8,128)}, f32[8192,128]{1,0:T(8,128)S(1)}, u32[]{:S(2)}) %copy-start.1) | copy-done | bytes 4194328
  65.7 0.0 copy-start.3
  65.7 1.9 %copy-done.3 = f32[8192,128]{1,0:T(8,128)} copy-done((f32[8192,128]{1,0:T(8,128)}, f32[8192,128]{1,0:T(8,128)S(1)}, u32[]{:S(2)}) %copy-start.3) | copy-done | bytes 4194328
  67.6 0.0 reduce-scatter.4.cloned.1.call-done
  67.6 1.0 copy.13.logit_ref
  68.7 2.5 %all-gather.3.cloned.1.call-done = bf16[16384,1,256]{2,0,1:T(8,128)(2,1)} async-done(((bf16[512,1,256]{2,0,1:T(8,128)(2,1)}), bf16[16384,1,256]{2,0,1:T(8,128)(2,1)}) %all-gather.3.cloned.1.call-update) | async-done | bytes 8388624 | tf_op jit(solution)/shard_map/all_gather | solution.py:184
  71.2 0.0 copy-start.2
  71.2 2.2 %copy-done.2 = f32[8192,128]{1,0:T(8,128)S(1)} copy-done((f32[8192,128]{1,0:T(8,128)S(1)}, f32[8192,128]{1,0:T(8,128)}, u32[]{:S(2)}) %copy-start.2) | copy-done | bytes 4194328
  73.4 0.0 copy-start.4
  73.4 2.2 %copy-done.4 = f32[8192,128]{1,0:T(8,128)S(1)} copy-done((f32[8192,128]{1,0:T(8,128)S(1)}, f32[8192,128]{1,0:T(8,128)}, u32[]{:S(2)}) %copy-start.4) | copy-done | bytes 4194328
  75.6 0.0 copy-start.6
  75.6 1.6 %copy-done.6 = bf16[512,16,128]{2,1,0:T(8,128)(2,1)S(1)} copy-done((bf16[512,16,128]{2,1,0:T(8,128)(2,1)S(1)}, bf16[512,16,128]{2,1,0:T(8,128)(2,1)}, u32[]{:S(2)}) %copy-start.6) | copy-done | bytes 2097176
  77.1 26.9 %far.1 = bf16[8192,128]{1,0:T(8,128)(2,1)} custom-call(s32[128]{0:T(128)S(1)} %reshape.24.pick_ref, s32[1]{0:T(128)} %bitcast.index_ref, bf16[8192,128]{1,0:T(8,128)(2,1)S(1)} %bitcast.13, f32[512,48]{1,0:T(8,128)S(1)} %copy.13.logit_ref, f32[8192,128]{1,0:T(8,128)S(1)} %copy-done.2, f32[8192,128]{1,0:T(8,128)S(1)} %copy-done.4, bf16[16384,256]{1,0:T(8,128)(2,1)} %bitcast.14), custom_call_target="tpu_custom_call" | custom-call | flops 4294967296 | bytes 16777216 | tf_op jit(solution)/shard_map/far/pallas_call | solution.py:227
  (4 shorter events, 0.1 us)
Async XLA Ops:
  7.4 1.5 %copy-start = (bf16[512,1792]{1,0:T(8,128)(2,1)S(1)}, bf16[512,1792]{1,0:T(8,128)(2,1)}, u32[]{:S(2)}) copy-start(bf16[512,1792]{1,0:T(8,128)(2,1)} %param.8) | copy-start | bytes 5505028
  7.4 4.2 %copy-start.8 = (bf16[512,1,128]{2,0,1:T(8,128)(2,1)S(1)}, bf16[512,1,128]{2,0,1:T(8,128)(2,1)}, u32[]{:S(2)}) copy-start(bf16[512,1,128]{2,0,1:T(8,128)(2,1)} %param.11) | copy-start | bytes 393220
  7.4 4.2 %copy-start.9 = (bf16[512,1,128]{2,0,1:T(8,128)(2,1)S(1)}, bf16[512,1,128]{2,0,1:T(8,128)(2,1)}, u32[]{:S(2)}) copy-start(bf16[512,1,128]{2,0,1:T(8,128)(2,1)} %param.12) | copy-start | bytes 393220
  7.4 9.9 %copy-start.10 = (f32[64,128]{1,0:T(8,128)S(1)}, f32[64,128]{1,0:T(8,128)}, u32[]{:S(2)}) copy-start(f32[64,128]{1,0:T(8,128)} %param.14) | copy-start | bytes 98308
  7.4 9.9 %copy-start.11 = (f32[64,128]{1,0:T(8,128)S(1)}, f32[64,128]{1,0:T(8,128)}, u32[]{:S(2)}) copy-start(f32[64,128]{1,0:T(8,128)} %param.13) | copy-start | bytes 98308
  7.4 36.0 %copy-start.12 = (s32[8,1,16]{2,1,0:T(1,128)S(1)}, s32[8,1,16]{2,1,0:T(1,128)}, u32[]{:S(2)}) copy-start(s32[8,1,16]{2,1,0:T(1,128)} %param.15) | copy-start | bytes 1540
  7.4 60.2 %reduce-scatter.4.cloned.1.call-start = ((), (), s32[]{:S(2)}) async-start(), calls=%async_computation.2 | async-start | bytes 491520
  11.5 59.7 %all-gather.3.cloned.1.call-start = ((), (), s32[]{:S(2)}) async-start(), calls=%async_computation.1 | async-start | bytes 8650752 | tf_op jit(solution)/shard_map/all_gather | solution.py:184
  11.6 0.7 copy-start.7
  12.3 31.8 %collective-permute-start = (bf16[512,256]{1,0:T(8,128)(2,1)}, bf16[512,256]{1,0:T(8,128)(2,1)S(1)}, u32[]{:S(2)}, u32[]{:S(2)}) collective-permute-start(bf16[512,256]{1,0:T(8,128)(2,1)} %bitcast.15), channel_id=1, source_target_pairs={{0,4},{4,8},{8,12},{12,16},{16,20},{20,24},{24,28},{28,32},{32,36}... | collective-permute-start | bytes 786440 | tf_op jit(solution)/shard_map/ppermute | solution.py:21
  45.1 1.6 %copy-start.5 = (bf16[512,16,128]{2,1,0:T(8,128)(2,1)S(1)}, bf16[512,16,128]{2,1,0:T(8,128)(2,1)}, u32[]{:S(2)}) copy-start(bf16[512,16,128]{2,1,0:T(8,128)(2,1)} %param.10) | copy-start | bytes 6291460
  63.7 2.0 %copy-start.1 = (f32[8192,128]{1,0:T(8,128)}, f32[8192,128]{1,0:T(8,128)S(1)}, u32[]{:S(2)}) copy-start(f32[8192,128]{1,0:T(8,128)S(1)} %get-tuple-element.7.comp_ref) | copy-start | bytes 12582916
  65.7 1.9 %copy-start.3 = (f32[8192,128]{1,0:T(8,128)}, f32[8192,128]{1,0:T(8,128)S(1)}, u32[]{:S(2)}) copy-start(f32[8192,128]{1,0:T(8,128)S(1)} %get-tuple-element.8.win_ref) | copy-start | bytes 12582916
  71.2 2.2 %copy-start.2 = (f32[8192,128]{1,0:T(8,128)S(1)}, f32[8192,128]{1,0:T(8,128)}, u32[]{:S(2)}) copy-start(f32[8192,128]{1,0:T(8,128)} %copy-done.1) | copy-start | bytes 12582916
  73.4 2.2 %copy-start.4 = (f32[8192,128]{1,0:T(8,128)S(1)}, f32[8192,128]{1,0:T(8,128)}, u32[]{:S(2)}) copy-start(f32[8192,128]{1,0:T(8,128)} %copy-done.3) | copy-start | bytes 12582916
  75.6 1.6 %copy-start.6 = (bf16[512,16,128]{2,1,0:T(8,128)(2,1)S(1)}, bf16[512,16,128]{2,1,0:T(8,128)(2,1)}, u32[]{:S(2)}) copy-start(bf16[512,16,128]{2,1,0:T(8,128)(2,1)} %param.10) | copy-start | bytes 6291460
Sparse Core Ops, SparseCore 0:
  11.6 22.3 reduce-scatter.3
Sparse Core Ops, SparseCore 1:
  14.5 56.6 all-gather.2

commit v2 on v1

v2 whole, which is shorter than its diff:
```python
import functools
import math

import jax
import jax.numpy as jnp
from jax import lax
from jax.experimental import pallas as pl
from jax.experimental.pallas import tpu as pltpu
from jax.sharding import PartitionSpec as P

WINDOW_TOKENS = 512
MASKED = -1e30
LOG2E = 1.4426950408889634
ROW_TILE = 256
SIDE = 4
CORES = 2
NT = (((1,), (1,)), ((), ()))
F32 = jnp.float32
BF16 = jnp.bfloat16


def place(x, z, core):
    return ((x % SIDE) * SIDE + z % SIDE) * CORES + core


def pairs(target):
    spots = [(x, z, c) for x in range(SIDE) for z in range(SIDE) for c in range(CORES)]
    return [(place(*spot), place(*target(*spot))) for spot in spots]


def first_axis(steps):
    return pairs(lambda x, z, c: (x, z + steps, c) if c == 0 else (x + steps, z, c))


def second_axis(steps):
    return pairs(lambda x, z, c: (x + steps, z, c) if c == 0 else (x, z + steps, c))


def other_core():
    return pairs(lambda x, z, c: (x, z, 1 - c))


def in_hbm(value):
    return pltpu.with_memory_space_constraint(value, pltpu.HBM)


def token_one_hot(rows, first_row, heads, first_lane):
    token = (lax.broadcasted_iota(jnp.int32, (rows, 128), 0) + first_row) // heads + first_lane
    lane = lax.broadcasted_iota(jnp.int32, (rows, 128), 1)
    return jnp.where(token == lane, 1.0, 0.0).astype(BF16)


def split(value):
    high = value.astype(BF16)
    return high, (value - high.astype(F32)).astype(BF16)


def near_kernel(
    block_len, heads, index_ref, q_ref, previous_ref, own_ref, logit_ref, win_ref, gate_ref, kv_ref, bias_ref
):
    head_dim = q_ref.shape[-1]
    rows = block_len * heads
    rows_here = own_ref.shape[0]
    blk = pl.program_id(0)
    factor = LOG2E / math.sqrt(head_dim)
    span = WINDOW_TOKENS + block_len

    @pl.when(blk == 0)
    def _():
        kv_ref[pl.ds(0, rows_here), :] = previous_ref[...]
        kv_ref[pl.ds(rows_here, rows_here), :] = own_ref[...]

    first = pl.multiple_of(blk * block_len, block_len)
    key = lax.broadcasted_iota(jnp.int32, (span, 128), 0)
    tok = lax.broadcasted_iota(jnp.int32, (span, 128), 1)
    start = index_ref[0] * rows_here + blk * block_len
    seen = (key > tok) & (key <= tok + WINDOW_TOKENS) & (key + start >= WINDOW_TOKENS)
    bias_ref[...] = jnp.where(seen, 0.0, MASKED).astype(BF16)
    keys = jnp.concatenate([kv_ref[pl.ds(first, span), :head_dim], bias_ref[...]], axis=1)
    values = jnp.concatenate(
        [kv_ref[pl.ds(first, span), head_dim:], jnp.ones((span, 128), BF16)], axis=1
    )
    columns = logit_ref.shape[0]
    gates = jnp.concatenate(split(jax.nn.sigmoid(logit_ref[...])), axis=1)
    tokens_there = logit_ref.shape[1]
    for at in range(0, rows, ROW_TILE):
        q = q_ref[pl.ds(at, ROW_TILE), :]
        hot = token_one_hot(ROW_TILE, at, heads, 0)
        scores = lax.dot_general(
            jnp.concatenate([q, hot], axis=1), keys, NT, preferred_element_type=F32
        )
        peak = jnp.max(scores, axis=-1, keepdims=True)
        weights = jnp.exp2(scores * factor - peak * factor).astype(BF16)
        both = jnp.dot(weights, values, preferred_element_type=F32)
        moved = token_one_hot(ROW_TILE, at, heads, lax.rem(blk, tokens_there // block_len) * block_len)
        of_token = lax.dot_general(
            jnp.concatenate([moved, moved], axis=1), gates, NT, preferred_element_type=F32
        )
        head = lax.rem(lax.broadcasted_iota(jnp.int32, (ROW_TILE, columns), 0) + at, heads)
        column = lax.broadcasted_iota(jnp.int32, (ROW_TILE, columns), 1) - head * 3
        comp_gate, sel_gate, win_gate = [
            jnp.sum(jnp.where(column == branch, of_token, 0.0), axis=-1, keepdims=True)
            for branch in range(3)
        ]
        win_ref[pl.ds(at, ROW_TILE), :] = win_gate * (both[:, :head_dim] / both[:, head_dim:])
        lane = lax.broadcasted_iota(jnp.int32, (ROW_TILE, 128), 1)
        gate_ref[pl.ds(at, ROW_TILE), :] = jnp.where(lane < 64, comp_gate, sel_gate)


def far_kernel(
    block_len, heads, picks, places, pick_ref, row_ref, index_ref, q_ref, gate_ref, win_ref, id_ref, weight_ref,
    *refs,
):
    piece_refs = refs[: len(places)]
    out_ref, all_ref, comp_ref, keys_ref, values_ref, sems = refs[len(places) :]
    head_dim = q_ref.shape[-1]
    rows = block_len * heads
    blk = pl.program_id(0)
    steps = pl.num_programs(0)
    factor = LOG2E / math.sqrt(head_dim)
    own_block = index_ref[0] * steps + blk
    count = all_ref.shape[0] // block_len

    @pl.when(blk == 0)
    def _():
        copies = [
            pltpu.make_async_copy(piece, all_ref.at[pl.ds(at, piece.shape[0]), :], sems.at[n])
            for n, (piece, at) in enumerate(zip(piece_refs, places))
        ]
        for copy in copies:
            copy.start()
        values_ref[:, head_dim:] = jnp.ones((picks * block_len, 128), BF16)
        for copy in copies:
            copy.wait()

        def compress(group, carry):
            parts = []
            for n in range(8):
                base = pl.multiple_of((group * 8 + n) * block_len, block_len)
                block = all_ref[pl.ds(base, block_len), :].astype(F32)
                parts.append(jnp.sum(block * weight_ref[...], axis=0, keepdims=True))
            high, low = split(jnp.concatenate(parts, axis=0))
            at = pl.multiple_of(group * 8, 8)
            comp_ref[0, pl.ds(at, 8), :] = high.astype(F32)
            comp_ref[1, pl.ds(at, 8), :] = low.astype(F32)
            return carry

        lax.fori_loop(0, count // 8, compress, 0)

    key = lax.broadcasted_iota(jnp.int32, (block_len, 128), 0)
    tok = lax.broadcasted_iota(jnp.int32, (block_len, 128), 1)
    for pick in range(picks):
        chosen = pick_ref[blk * picks + pick]
        source = pl.multiple_of(row_ref[blk * picks + pick], block_len)
        into = pl.ds(pick * block_len, block_len)
        last = jnp.where(chosen < own_block, block_len, jnp.where(chosen == own_block, 0, -2 * block_len))
        keys_ref[into, :head_dim] = all_ref[pl.ds(source, block_len), :head_dim]
        values_ref[into, :head_dim] = all_ref[pl.ds(source, block_len), head_dim:]
        keys_ref[into, head_dim:] = jnp.where(key <= tok + last, 0.0, MASKED).astype(BF16)
    comp = comp_ref[...].astype(BF16)
    comp_keys = jnp.concatenate([comp[0, :, :head_dim], comp[1, :, :head_dim]], axis=1)
    comp_values = jnp.concatenate([comp[0, :, head_dim:], comp[1, :, head_dim:]], axis=1)
    for at in range(0, rows, ROW_TILE):
        q = q_ref[pl.ds(at, ROW_TILE), :]
        hot = token_one_hot(ROW_TILE, at, heads, 0)
        scores = lax.dot_general(
            jnp.concatenate([q, hot], axis=1), keys_ref[...], NT, preferred_element_type=F32
        )
        peak = jnp.max(scores, axis=-1, keepdims=True)
        weights = jnp.exp2(scores * factor - peak * factor).astype(BF16)
        both = jnp.dot(weights, values_ref[...], preferred_element_type=F32)
        sel = both[:, :head_dim] / both[:, head_dim:]
        scores = lax.dot_general(
            jnp.concatenate([q, q], axis=1), comp_keys, NT, preferred_element_type=F32
        )
        token = (lax.broadcasted_iota(jnp.int32, (ROW_TILE, 1), 0) + at) // heads
        limit = own_block + jnp.where(token == block_len - 1, 1, 0)
        scores = jnp.where(id_ref[...] < limit, scores, MASKED)
        peak = jnp.maximum(jnp.max(scores, axis=-1, keepdims=True), 0.0)
        weights = jnp.exp2(scores * factor - peak * factor)
        total = jnp.sum(weights, axis=-1, keepdims=True) + jnp.exp2(-peak * factor)
        both = jnp.dot(weights.astype(BF16), comp_values, preferred_element_type=F32)
        gate = gate_ref[pl.ds(at, ROW_TILE), :]
        merged = (
            (gate[:, 0:1] / total) * (both[:, :head_dim] + both[:, head_dim:])
            + gate[:, 64:65] * sel
            + win_ref[pl.ds(at, ROW_TILE), :]
        )
        out_ref[pl.ds(at, ROW_TILE), :] = merged.astype(BF16)


def partial_logits(hidden_in, gate_weight):
    return lax.dot_general(
        gate_weight, hidden_in, (((0,), (1,)), ((), ())), preferred_element_type=F32
    )


def gate_logits(partial_value):
    parts = lax.axis_size("head")
    mine = lax.axis_index("head")
    columns = partial_value.shape[0] // parts

    def chunk(which):
        return lax.dynamic_slice_in_dim(partial_value, lax.rem(which, parts) * columns, columns, 0)

    total = chunk(mine)
    for steps in range(1, parts):
        total = total + lax.ppermute(
            chunk(mine + steps), "head", [(n, (n + steps) % parts) for n in range(parts)]
        )
    return total


def send(value, perm):
    return lax.ppermute(value, "ctx", perm)


def gather_line(key_value, beside):
    ahead = send(key_value, perm=first_axis(-1))
    behind = send(key_value, perm=first_axis(1))
    across = send(key_value, perm=first_axis(2))
    ahead, behind, across, beside = lax.optimization_barrier((ahead, behind, across, beside))
    return jnp.concatenate([key_value, ahead, across, behind], axis=0), beside


def gather_pieces(line, meanwhile):
    half = line.shape[0] // 2
    next_line = send(line, perm=second_axis(-1))
    last_line = send(line, perm=second_axis(1))
    done = meanwhile()
    low, high, done = lax.optimization_barrier((next_line[:half], last_line[half:], done))
    far_low = send(low, perm=second_axis(-1))
    far_high = send(high, perm=second_axis(1))
    rows = line.shape[0]
    mine = [(line, 0), (next_line, rows), (far_low, 2 * rows), (far_high, 2 * rows + half), (last_line, 3 * rows)]
    return mine + [(send(piece, perm=other_core()), at + SIDE * rows) for piece, at in mine], done


def row_of_block(block, index, blocks_here, block_len):
    shard = block // blocks_here
    core = shard % CORES
    across_x = (shard // (SIDE * CORES) - index // (SIDE * CORES)) % SIDE
    across_z = (shard // CORES - index // CORES) % SIDE
    along = jnp.where(core == 0, across_z, across_x)
    line = jnp.where(core == 0, across_x, across_z)
    piece = jnp.where(core == index % CORES, 0, SIDE) + line
    return ((piece * SIDE + along) * blocks_here + block % blocks_here) * block_len


def body(
    hidden_in,
    gate_weight,
    encoded_queries,
    encoded_keys,
    value_tensor,
    comp_key_weight,
    comp_value_weight,
    selection,
):
    rows_here, heads_here, head_dim = encoded_queries.shape
    block_len = comp_key_weight.shape[0]
    picks = selection.shape[-1]
    blocks_here = rows_here // block_len
    shard_parts = lax.axis_size("ctx")
    rows = block_len * heads_here
    all_rows = rows_here * heads_here
    place_here = lax.axis_index("ctx").astype(jnp.int32)
    index = place_here.reshape(1)

    key_value = jnp.concatenate([encoded_keys, value_tensor], axis=-1).reshape(rows_here, 2 * head_dim)
    line, partial_value = gather_line(key_value, partial_logits(hidden_in, gate_weight))
    compress_w = jnp.concatenate([comp_key_weight, comp_value_weight], axis=-1)
    queries = in_hbm(encoded_queries.reshape(all_rows, head_dim))
    total_blocks = blocks_here * shard_parts
    chosen = selection.reshape(-1)
    source_rows = row_of_block(chosen, place_here, blocks_here, block_len)
    block_ids = jnp.arange(total_blocks, dtype=jnp.int32)
    placed = row_of_block(block_ids, place_here, blocks_here, block_len) // block_len
    slots = jnp.arange(total_blocks, dtype=jnp.int32)
    ids_by_slot = jnp.sum(
        jnp.where(placed[None, :] == slots[:, None], block_ids[None, :], 0), axis=1, dtype=jnp.int32
    ).reshape(1, total_blocks)

    tile = pl.BlockSpec((rows, head_dim), lambda b, *_: (b, 0))
    whole = lambda shape: pl.BlockSpec(shape, lambda b, *_: (0, 0))
    wide = pltpu.HBM((all_rows, head_dim), F32)
    def near():
        previous = lax.ppermute(key_value, "ctx", [(n, n + 1) for n in range(shard_parts - 1)])
        logits = gate_logits(partial_value)
        return pl.pallas_call(
            functools.partial(near_kernel, block_len, heads_here),
            out_shape=(wide, wide),
            grid_spec=pltpu.PrefetchScalarGridSpec(
                num_scalar_prefetch=1,
                grid=(blocks_here,),
                in_specs=[
                    tile,
                    whole((rows_here, 2 * head_dim)),
                    whole((rows_here, 2 * head_dim)),
                    pl.BlockSpec((logits.shape[0], 128), lambda b, *_: (0, b * block_len // 128)),
                ],
                out_specs=(tile, tile),
                scratch_shapes=[
                    pltpu.VMEM((2 * rows_here, 2 * head_dim), BF16),
                    pltpu.VMEM((WINDOW_TOKENS + block_len, 128), BF16),
                ],
            ),
            compiler_params=pltpu.CompilerParams(vmem_limit_bytes=56 << 20),
            cost_estimate=pl.CostEstimate(
                flops=4 * all_rows * head_dim * 1024, transcendentals=all_rows * 576, bytes_accessed=12 << 20
            ),
            name="near",
        )(index, queries, previous, key_value, logits)

    pieces, (win, gate) = gather_pieces(line, near)
    out = pl.pallas_call(
        functools.partial(far_kernel, block_len, heads_here, picks, [at for _, at in pieces]),
        out_shape=jax.ShapeDtypeStruct((all_rows, head_dim), BF16),
        grid_spec=pltpu.PrefetchScalarGridSpec(
            num_scalar_prefetch=3,
            grid=(blocks_here,),
            in_specs=[tile, tile, tile, whole((1, total_blocks)), whole((block_len, 2 * head_dim))]
            + [pl.BlockSpec(memory_space=pl.ANY)] * len(pieces),
            out_specs=tile,
            scratch_shapes=[
                pltpu.VMEM((rows_here * shard_parts, 2 * head_dim), BF16),
                pltpu.VMEM((2, total_blocks, 2 * head_dim), F32),
                pltpu.VMEM((picks * block_len, 2 * head_dim), BF16),
                pltpu.VMEM((picks * block_len, 2 * head_dim), BF16),
                pltpu.SemaphoreType.DMA((len(pieces),)),
            ],
        ),
        compiler_params=pltpu.CompilerParams(vmem_limit_bytes=56 << 20),
        cost_estimate=pl.CostEstimate(
            flops=8 * all_rows * head_dim * 1280, transcendentals=all_rows * 1280, bytes_accessed=20 << 20
        ),
        name="far",
    )(
        chosen, source_rows, index, queries, gate, win, ids_by_slot, compress_w,
        *[in_hbm(piece) for piece, _ in pieces],
    )
    return out.reshape(rows_here, heads_here, head_dim)


def solution(mesh):
    return jax.shard_map(
        body,
        mesh=mesh,
        in_specs=(
            P("ctx", "head"),
            P("head", None),
            P("ctx", "head", None),
            P("ctx", "head", None),
            P("ctx", "head", None),
            P(),
            P(),
            P("ctx", "head", None),
        ),
        out_specs=P("ctx", "head", None),
        check_vma=False,
    )
```

time: 112 us -> 106 us (0.946)
  starting transfers between devices: 5.02 us -> 35.8 us
  blocking collectives: 24.4 us -> 0 us
  between operations: 15 us -> 0.18 us
  local copies, waits for them, and re-layouts: 15.3 us -> 6.06 us
  Pallas kernels: 43.9 us -> 50.5 us
  waiting for transfers between devices: 2.56 us -> 5.67 us
  other arithmetic: 2.68 us -> 5.39 us
    ppermute x1 -> x16, starting transfers between devices: 4.94 us -> 35.8 us  [the longest x12 25.5 us: send(): return lax.ppermute(value, 'ctx', perm)]
    all_gather x1 -> x0, blocking collectives: 24.4 us -> none  [body(): summaries = lax.all_gather(summary, 'ctx', axis=0, tiled=True)]
    unnamed x29 -> x19, local copies, waits for them, and re-layouts: 15.2 us -> 1.54 us
    ppermute x1 -> x16, waiting for transfers between devices: 0.01 us -> 5.67 us  [the longest x12 3.3 us: send(): return lax.ppermute(value, 'ctx', perm)]
    pallas_call x1, Pallas kernels: 26.9 us -> 31.1 us  [body(): pl.pallas_call(functools.partial(far_kernel, block_len, heads_here, picks...]
    slice x0 -> x2, local copies, waits for them, and re-layouts: none -> 3.75 us  [the longest x1 1.88 us: gather_pieces(): last_line[half:]]
    unnamed x1 -> x0, matrix products: 2.59 us -> none
    all_gather x1 -> x0, waiting for transfers between devices: 2.52 us -> none  [body(): gathered = lax.all_gather(key_value, 'ctx', axis=0, tiled=True)]
  transfers between devices with their start and end apart: 3 -> 16, of which waited for: 1 -> 5; matrix products, arithmetic and copies ran while one was open for 4% -> 9% of each run, Pallas kernels for 15% -> 18%
where the time goes in v2:
time: 106 us; the launch traced here: 105 us
  Pallas kernels  50.5 us (48%)
  starting transfers between devices  35.8 us (34%)
  local copies, waits for them, and re-layouts  6.06 us (6%)
  waiting for transfers between devices  5.67 us (5%)
  other arithmetic  5.39 us (5%)
  matrix products  1.84 us (2%)
    pallas_call x1, Pallas kernels, body(): pl.pallas_call(functools.partial(far_kernel, block_len, heads_here, picks...  31.1 us
    ppermute x12, starting transfers between devices, send(): return lax.ppermute(value, 'ctx', perm)  25.5 us
    pallas_call x1, Pallas kernels, near(): pl.pallas_call(functools.partial(near_kernel, block_len, heads_here), out...  19.4 us
    ppermute x1, starting transfers between devices, near(): lax.ppermute(key_value, 'ctx', [(n, n + 1) for n in range(shard_parts - 1)])  5.85 us
    ppermute x3, starting transfers between devices, gate_logits(): lax.ppermute(chunk(mine + steps), 'head', [(n, (n + steps) % parts) for n...  4.38 us
    ppermute x12, waiting for transfers between devices, send(): return lax.ppermute(value, 'ctx', perm)  3.3 us
  transfers between devices with their start and end apart: 16, of which 5 were waited for; matrix products, arithmetic and copies ran while one was open for 9% of the time, Pallas kernels for 18%

profile of v2, /device:TPU:1, one launch (start us, length us, event | category | flops | bytes accessed | tf_op | source)
XLA Modules:
  0.0 105.4 jit_solution(2875676589841589537)
XLA Ops:
  0.0 1.1 %maximum_bitcast_fusion.own_ref = bf16[512,256]{1,0:T(8,128)(2,1)S(1)} fusion(bf16[512,1,128]{2,0,1:T(8,128)(2,1)} %param.12, bf16[512,1,128]{2,0,1:T(8,128)(2,1)} %param.11), kind=kLoop, calls=%fused_computation.1 | loop fusion | flops 524288 | bytes 524288 | tf_op jit(solution)/shard_map/reshape | solution.py:270
  1.1 0.0 copy-start.2
  1.1 3.7 %collective-permute-start.2 = (bf16[512,256]{1,0:T(8,128)(2,1)S(1)}, bf16[512,256]{1,0:T(8,128)(2,1)S(1)}, u32[]{:S(2)}, u32[]{:S(2)}) collective-permute-start(bf16[512,256]{1,0:T(8,128)(2,1)S(1)} %maximum_bitcast_fusion.own_ref), channel_id=1, source_target_pairs={{0,16},{4,68},{8,24},{12,76},{16,0},{20,84},{24,8},{28,92},{32,48}... | collective-permute-start | bytes 786440 | tf_op jit(solution)/shard_map/ppermute | solution.py:215
  4.8 0.3 collective-permute-start.1
  5.1 2.4 %collective-permute-start = (bf16[512,256]{1,0:T(8,128)(2,1)S(1)}, bf16[512,256]{1,0:T(8,128)(2,1)S(1)}, u32[]{:S(2)}, u32[]{:S(2)}) collective-permute-start(bf16[512,256]{1,0:T(8,128)(2,1)S(1)} %maximum_bitcast_fusion.own_ref), channel_id=1, source_target_pairs={{0,24},{4,100},{8,0},{12,108},{16,8},{20,116},{24,16},{28,124},{32... | collective-permute-start | bytes 786440 | tf_op jit(solution)/shard_map/ppermute | solution.py:215
  7.5 1.8 %fusion.15 = f32[192,512]{1,0:T(8,128)S(1)} fusion(bf16[1792,192]{0,1:T(8,128)(2,1)} %param.9, bf16[512,1792]{1,0:T(8,128)(2,1)S(1)} %copy-done), kind=kOutput, calls=%fused_computation.70 | convolution fusion | flops 352321536 | bytes 2916352 | tf_op jit(solution)/shard_map/dot_general | solution.py:193
  9.3 0.0 collective-permute-done.2
  9.3 2.3 %collective-permute-done.1 = bf16[512,256]{1,0:T(8,128)(2,1)S(1)} collective-permute-done((bf16[512,256]{1,0:T(8,128)(2,1)S(1)}, bf16[512,256]{1,0:T(8,128)(2,1)S(1)}, u32[]{:S(2)}, u32[]{:S(2)}) %collective-permute-start.1) | collective-permute-done | bytes 262176 | tf_op jit(solution)/shard_map/ppermute | solution.py:215
  11.7 0.3 collective-permute-done
  12.0 0.1 pad_maximum_fusion.refs_0_
  12.1 1.7 %collective-permute-start.4 = (bf16[2048,256]{1,0:T(8,128)(2,1)S(1)}, bf16[2048,256]{1,0:T(8,128)(2,1)}, u32[]{:S(2)}, u32[]{:S(2)}) collective-permute-start(bf16[2048,256]{1,0:T(8,128)(2,1)S(1)} %pad_maximum_fusion.refs_0_), channel_id=1, source_target_pairs={{0,32},{4,12},{8,40},{12,20},{16,48},{20,28},{24,56},{28,4},{32,64... | collective-permute-start | bytes 3145736 | tf_op jit(solution)/shard_map/ppermute | solution.py:215
  13.8 2.2 %collective-permute-start.3 = (bf16[2048,256]{1,0:T(8,128)(2,1)S(1)}, bf16[2048,256]{1,0:T(8,128)(2,1)}, u32[]{:S(2)}, u32[]{:S(2)}) collective-permute-start(bf16[2048,256]{1,0:T(8,128)(2,1)S(1)} %pad_maximum_fusion.refs_0_), channel_id=1, source_target_pairs={{0,96},{4,28},{8,104},{12,4},{16,112},{20,12},{24,120},{28,20},{32... | collective-permute-start | bytes 3145736 | tf_op jit(solution)/shard_map/ppermute | solution.py:215
  16.0 0.7 constant_dynamic-slice_fusion.2
  16.7 1.3 %collective-permute-start.6 = (f32[48,512]{1,0:T(8,128)S(1)}, f32[48,512]{1,0:T(8,128)}, u32[]{:S(2)}, u32[]{:S(2)}) collective-permute-start(f32[48,512]{1,0:T(8,128)S(1)} %get-tuple-element.25), channel_id=1, source_target_pairs={{0,1},{1,2},{2,3},{3,0},{4,5},{5,6},{6,7},{7,4},{8,9},{9,10},{10,1... | collective-permute-start | bytes 294920 | tf_op jit(solution)/shard_map/ppermute | solution.py:208
  18.0 1.4 %collective-permute-start.8 = (f32[48,512]{1,0:T(8,128)}, f32[48,512]{1,0:T(8,128)}, u32[]{:S(2)}, u32[]{:S(2)}) collective-permute-start(f32[48,512]{1,0:T(8,128)} %get-tuple-element.26), channel_id=1, source_target_pairs={{0,3},{1,0},{2,1},{3,2},{4,7},{5,4},{6,5},{7,6},{8,11},{9,8},{10,9... | collective-permute-start | bytes 294920 | tf_op jit(solution)/shard_map/ppermute | solution.py:208
  19.4 1.6 %collective-permute-start.7 = (f32[48,512]{1,0:T(8,128)}, f32[48,512]{1,0:T(8,128)}, u32[]{:S(2)}, u32[]{:S(2)}) collective-permute-start(f32[48,512]{1,0:T(8,128)} %get-tuple-element.27), channel_id=1, source_target_pairs={{0,2},{1,3},{2,0},{3,1},{4,6},{5,7},{6,4},{7,5},{8,10},{9,11},{10,... | collective-permute-start | bytes 294920 | tf_op jit(solution)/shard_map/ppermute | solution.py:208
  21.0 0.8 collective-permute-done.6
  21.8 5.9 %collective-permute-start.5 = (bf16[512,256]{1,0:T(8,128)(2,1)S(1)}, bf16[512,256]{1,0:T(8,128)(2,1)}, u32[]{:S(2)}, u32[]{:S(2)}) collective-permute-start(bf16[512,256]{1,0:T(8,128)(2,1)S(1)} %maximum_bitcast_fusion.own_ref), channel_id=1, source_target_pairs={{0,4},{4,8},{8,12},{12,16},{16,20},{20,24},{24,28},{28,32},{32,36}... | collective-permute-start | bytes 786440 | tf_op jit(solution)/shard_map/ppermute | solution.py:288
  27.7 0.0 collective-permute-done.8
  27.7 0.0 collective-permute-done.7
  27.7 1.7 %add_add_fusion.logit_ref = f32[48,512]{1,0:T(8,128)} fusion(f32[48,512]{1,0:T(8,128)} %collective-permute-done.8, f32[48,512]{1,0:T(8,128)} %collective-permute-done.7, f32[48,512]{1,0:T(8,128)} %collective-permute-done.6, f32[192,512]{1,0:T(8,128)S(1)} %fusion.15, s32[]{:T(128)S(6)} %select_n.184), kind=kLoop, calls=%fused_computation.4 | loop fusion | flops 73728 | bytes 491524 | tf_op jit(solution)/shard_map/add | solution.py:208
  29.4 1.6 %collective-permute-done.5.previous_ref = bf16[512,256]{1,0:T(8,128)(2,1)} collective-permute-done((bf16[512,256]{1,0:T(8,128)(2,1)S(1)}, bf16[512,256]{1,0:T(8,128)(2,1)}, u32[]{:S(2)}, u32[]{:S(2)}) %collective-permute-start.5) | collective-permute-done | bytes 262176 | tf_op jit(solution)/shard_map/ppermute | solution.py:288
  31.0 19.4 %near.1 = (f32[8192,128]{1,0:T(8,128)}, f32[8192,128]{1,0:T(8,128)}) custom-call(s32[1]{0:T(128)} %bitcast.index_ref, bf16[8192,128]{1,0:T(8,128)(2,1)} %bitcast.9, bf16[512,256]{1,0:T(8,128)(2,1)} %collective-permute-done.5.previous_ref, bf16[512,256]{1,0:T(8,128)(2,1)} %copy-done.2, f32[48,512]{1,0:T(8,128)} %add_add_fusion.logit_ref), custom_call_target="tpu_custom_call" | custom-call | flops 4294967296 | bytes 12582912 | tf_op jit(solution)/shard_map/near/pallas_call | solution.py:290
  50.4 0.0 copy-start.4
  50.4 0.0 collective-permute-done.4.refs_4_
  50.4 1.9 %slice.9 = bf16[1024,256]{1,0:T(8,128)(2,1)} slice(bf16[2048,256]{1,0:T(8,128)(2,1)} %collective-permute-done.4.refs_4_), slice={[1024:2048], [0:256]} | slice | bytes 1048576 | tf_op jit(solution)/shard_map/slice | solution.py:231
  52.3 0.0 collective-permute-done.3.refs_1_
  52.3 1.9 %slice.8 = bf16[1024,256]{1,0:T(8,128)(2,1)} slice(bf16[2048,256]{1,0:T(8,128)(2,1)} %collective-permute-done.3.refs_1_), slice={[0:1024], [0:256]} | slice | bytes 1048576 | tf_op jit(solution)/shard_map/slice | solution.py:231
  54.1 2.6 %collective-permute-start.9 = (bf16[1024,256]{1,0:T(8,128)(2,1)}, bf16[1024,256]{1,0:T(8,128)(2,1)}, u32[]{:S(2)}, u32[]{:S(2)}) collective-permute-start(bf16[1024,256]{1,0:T(8,128)(2,1)} %slice.8), channel_id=1, source_target_pairs={{0,96},{4,28},{8,104},{12,4},{16,112},{20,12},{24,120},{28,20},{32... | collective-permute-start | bytes 1572872 | tf_op jit(solution)/shard_map/ppermute | solution.py:215
  56.7 0.0 collective-permute-start.10
  56.7 4.0 %collective-permute-start.11 = (bf16[2048,256]{1,0:T(8,128)(2,1)S(1)}, bf16[2048,256]{1,0:T(8,128)(2,1)}, u32[]{:S(2)}, u32[]{:S(2)}) collective-permute-start(bf16[2048,256]{1,0:T(8,128)(2,1)S(1)} %pad_maximum_fusion.refs_0_), channel_id=1, source_target_pairs={{0,4},{4,0},{8,12},{12,8},{16,20},{20,16},{24,28},{28,24},{32,36},... | collective-permute-start | bytes 3145736 | tf_op jit(solution)/shard_map/ppermute | solution.py:215
  60.7 0.1 collective-permute-start.15
  60.8 0.4 collective-permute-start.12
  61.2 0.6 broadcast.288
  61.8 0.6 reduce.3
  62.5 0.1 reshape.124.pick_ref
  62.5 0.6 collective-permute-done.9.refs_2_
  63.2 4.5 %collective-permute-start.13 = (bf16[1024,256]{1,0:T(8,128)(2,1)}, bf16[1024,256]{1,0:T(8,128)(2,1)S(1)}, u32[]{:S(2)}, u32[]{:S(2)}) collective-permute-start(bf16[1024,256]{1,0:T(8,128)(2,1)} %collective-permute-done.9.refs_2_), channel_id=1, source_target_pairs={{0,4},{4,0},{8,12},{12,8},{16,20},{20,16},{24,28},{28,24},{32,36},... | collective-permute-start | bytes 1572872 | tf_op jit(solution)/shard_map/ppermute | solution.py:215
  67.7 0.0 collective-permute-done.10.refs_3_
  67.7 3.7 %collective-permute-start.14 = (bf16[1024,256]{1,0:T(8,128)(2,1)}, bf16[1024,256]{1,0:T(8,128)(2,1)S(1)}, u32[]{:S(2)}, u32[]{:S(2)}) collective-permute-start(bf16[1024,256]{1,0:T(8,128)(2,1)} %collective-permute-done.10.refs_3_), channel_id=1, source_target_pairs={{0,4},{4,0},{8,12},{12,8},{16,20},{20,16},{24,28},{28,24},{32,36},... | collective-permute-start | bytes 1572872 | tf_op jit(solution)/shard_map/ppermute | solution.py:215
  71.5 0.6 pad_maximum_fusion.1.weight_ref
  72.1 0.7 select_reduce_fusion
  72.8 0.5 fusion.14.row_ref
  73.3 0.0 collective-permute-done.13.refs_7_
  73.3 0.0 collective-permute-done.14.refs_8_
  73.4 0.8 copy-done.7
  74.1 0.2 copy-done.8
  74.3 31.1 %far.1 = bf16[8192,128]{1,0:T(8,128)(2,1)} custom-call(s32[128]{0:T(128)} %copy-done.6, s32[128]{0:T(128)} %fusion.14.row_ref, s32[1]{0:T(128)} %bitcast.index_ref, bf16[8192,128]{1,0:T(8,128)(2,1)} %bitcast.10, f32[8192,128]{1,0:T(8,128)} %get-tuple-element.21.gate_ref, f32[8192,128]{1,0:T(8,128)} %get-tuple-element.22.win_ref, s32[1,256]{1,0:T(1,128)} %bitcast.8, ...), custom_call_target="tpu_custom_call" | custom-call | flops 10737418240 | bytes 20971520 | tf_op jit(solution)/shard_map/far/pallas_call | solution.py:316
  (18 shorter events, 0.1 us)
Async XLA Ops:
  0.0 7.5 %copy-start = (bf16[512,1792]{1,0:T(8,128)(2,1)S(1)}, bf16[512,1792]{1,0:T(8,128)(2,1)}, u32[]{:S(2)}) copy-start(bf16[512,1792]{1,0:T(8,128)(2,1)} %param.8) | copy-start | bytes 5505028
  1.1 20.7 %copy-start.2 = (bf16[512,256]{1,0:T(8,128)(2,1)}, bf16[512,256]{1,0:T(8,128)(2,1)S(1)}, u32[]{:S(2)}) copy-start(bf16[512,256]{1,0:T(8,128)(2,1)S(1)} %maximum_bitcast_fusion.own_ref) | copy-start | bytes 786436
  1.1 8.2 %collective-permute-start.2 = (bf16[512,256]{1,0:T(8,128)(2,1)S(1)}, bf16[512,256]{1,0:T(8,128)(2,1)S(1)}, u32[]{:S(2)}, u32[]{:S(2)}) collective-permute-start(bf16[512,256]{1,0:T(8,128)(2,1)S(1)} %maximum_bitcast_fusion.own_ref), channel_id=1, source_target_pairs={{0,16},{4,68},{8,24},{12,76},{16,0},{20,84},{24,8},{28,92},{32,48}... | collective-permute-start | bytes 786440 | tf_op jit(solution)/shard_map/ppermute | solution.py:215
  4.8 6.9 %collective-permute-start.1 = (bf16[512,256]{1,0:T(8,128)(2,1)S(1)}, bf16[512,256]{1,0:T(8,128)(2,1)S(1)}, u32[]{:S(2)}, u32[]{:S(2)}) collective-permute-start(bf16[512,256]{1,0:T(8,128)(2,1)S(1)} %maximum_bitcast_fusion.own_ref), channel_id=1, source_target_pairs={{0,8},{4,36},{8,16},{12,44},{16,24},{20,52},{24,0},{28,60},{32,40}... | collective-permute-start | bytes 786440 | tf_op jit(solution)/shard_map/ppermute | solution.py:215
  5.1 6.9 %collective-permute-start = (bf16[512,256]{1,0:T(8,128)(2,1)S(1)}, bf16[512,256]{1,0:T(8,128)(2,1)S(1)}, u32[]{:S(2)}, u32[]{:S(2)}) collective-permute-start(bf16[512,256]{1,0:T(8,128)(2,1)S(1)} %maximum_bitcast_fusion.own_ref), channel_id=1, source_target_pairs={{0,24},{4,100},{8,0},{12,108},{16,8},{20,116},{24,16},{28,124},{32... | collective-permute-start | bytes 786440 | tf_op jit(solution)/shard_map/ppermute | solution.py:215
  12.0 44.7 %copy-start.1 = (bf16[2048,256]{1,0:T(8,128)(2,1)}, bf16[2048,256]{1,0:T(8,128)(2,1)S(1)}, u32[]{:S(2)}) copy-start(bf16[2048,256]{1,0:T(8,128)(2,1)S(1)} %pad_maximum_fusion.refs_0_) | copy-start | bytes 3145732
  12.1 38.3 %collective-permute-start.4 = (bf16[2048,256]{1,0:T(8,128)(2,1)S(1)}, bf16[2048,256]{1,0:T(8,128)(2,1)}, u32[]{:S(2)}, u32[]{:S(2)}) collective-permute-start(bf16[2048,256]{1,0:T(8,128)(2,1)S(1)} %pad_maximum_fusion.refs_0_), channel_id=1, source_target_pairs={{0,32},{4,12},{8,40},{12,20},{16,48},{20,28},{24,56},{28,4},{32,64... | collective-permute-start | bytes 3145736 | tf_op jit(solution)/shard_map/ppermute | solution.py:215
  13.8 38.5 %collective-permute-start.3 = (bf16[2048,256]{1,0:T(8,128)(2,1)S(1)}, bf16[2048,256]{1,0:T(8,128)(2,1)}, u32[]{:S(2)}, u32[]{:S(2)}) collective-permute-start(bf16[2048,256]{1,0:T(8,128)(2,1)S(1)} %pad_maximum_fusion.refs_0_), channel_id=1, source_target_pairs={{0,96},{4,28},{8,104},{12,4},{16,112},{20,12},{24,120},{28,20},{32... | collective-permute-start | bytes 3145736 | tf_op jit(solution)/shard_map/ppermute | solution.py:215
  16.7 5.1 %collective-permute-start.6 = (f32[48,512]{1,0:T(8,128)S(1)}, f32[48,512]{1,0:T(8,128)}, u32[]{:S(2)}, u32[]{:S(2)}) collective-permute-start(f32[48,512]{1,0:T(8,128)S(1)} %get-tuple-element.25), channel_id=1, source_target_pairs={{0,1},{1,2},{2,3},{3,0},{4,5},{5,6},{6,7},{7,4},{8,9},{9,10},{10,1... | collective-permute-start | bytes 294920 | tf_op jit(solution)/shard_map/ppermute | solution.py:208
  18.0 9.7 %collective-permute-start.8 = (f32[48,512]{1,0:T(8,128)}, f32[48,512]{1,0:T(8,128)}, u32[]{:S(2)}, u32[]{:S(2)}) collective-permute-start(f32[48,512]{1,0:T(8,128)} %get-tuple-element.26), channel_id=1, source_target_pairs={{0,3},{1,0},{2,1},{3,2},{4,7},{5,4},{6,5},{7,6},{8,11},{9,8},{10,9... | collective-permute-start | bytes 294920 | tf_op jit(solution)/shard_map/ppermute | solution.py:208
  19.4 8.3 %collective-permute-start.7 = (f32[48,512]{1,0:T(8,128)}, f32[48,512]{1,0:T(8,128)}, u32[]{:S(2)}, u32[]{:S(2)}) collective-permute-start(f32[48,512]{1,0:T(8,128)} %get-tuple-element.27), channel_id=1, source_target_pairs={{0,2},{1,3},{2,0},{3,1},{4,6},{5,7},{6,4},{7,5},{8,10},{9,11},{10,... | collective-permute-start | bytes 294920 | tf_op jit(solution)/shard_map/ppermute | solution.py:208
  21.8 9.2 %collective-permute-start.5 = (bf16[512,256]{1,0:T(8,128)(2,1)S(1)}, bf16[512,256]{1,0:T(8,128)(2,1)}, u32[]{:S(2)}, u32[]{:S(2)}) collective-permute-start(bf16[512,256]{1,0:T(8,128)(2,1)S(1)} %maximum_bitcast_fusion.own_ref), channel_id=1, source_target_pairs={{0,4},{4,8},{8,12},{12,16},{16,20},{20,24},{24,28},{28,32},{32,36}... | collective-permute-start | bytes 786440 | tf_op jit(solution)/shard_map/ppermute | solution.py:288
  50.4 11.4 %copy-start.5 = (s32[8,1,16]{2,1,0:T(1,128)S(1)}, s32[8,1,16]{2,1,0:T(1,128)}, u32[]{:S(2)}) copy-start(s32[8,1,16]{2,1,0:T(1,128)} %param.15) | copy-start | bytes 1540
  50.4 21.1 %copy-start.3 = (f32[64,128]{1,0:T(8,128)S(1)}, f32[64,128]{1,0:T(8,128)}, u32[]{:S(2)}) copy-start(f32[64,128]{1,0:T(8,128)} %param.14) | copy-start | bytes 98308
  50.4 21.1 %copy-start.4 = (f32[64,128]{1,0:T(8,128)S(1)}, f32[64,128]{1,0:T(8,128)}, u32[]{:S(2)}) copy-start(f32[64,128]{1,0:T(8,128)} %param.13) | copy-start | bytes 98308
  54.1 9.0 %collective-permute-start.9 = (bf16[1024,256]{1,0:T(8,128)(2,1)}, bf16[1024,256]{1,0:T(8,128)(2,1)}, u32[]{:S(2)}, u32[]{:S(2)}) collective-permute-start(bf16[1024,256]{1,0:T(8,128)(2,1)} %slice.8), channel_id=1, source_target_pairs={{0,96},{4,28},{8,104},{12,4},{16,112},{20,12},{24,120},{28,20},{32... | collective-permute-start | bytes 1572872 | tf_op jit(solution)/shard_map/ppermute | solution.py:215
  56.7 11.0 %collective-permute-start.10 = (bf16[1024,256]{1,0:T(8,128)(2,1)}, bf16[1024,256]{1,0:T(8,128)(2,1)}, u32[]{:S(2)}, u32[]{:S(2)}) collective-permute-start(bf16[1024,256]{1,0:T(8,128)(2,1)} %slice.9), channel_id=1, source_target_pairs={{0,32},{4,12},{8,40},{12,20},{16,48},{20,28},{24,56},{28,4},{32,64... | collective-permute-start | bytes 1572872 | tf_op jit(solution)/shard_map/ppermute | solution.py:215
  56.7 16.6 %collective-permute-start.11 = (bf16[2048,256]{1,0:T(8,128)(2,1)S(1)}, bf16[2048,256]{1,0:T(8,128)(2,1)}, u32[]{:S(2)}, u32[]{:S(2)}) collective-permute-start(bf16[2048,256]{1,0:T(8,128)(2,1)S(1)} %pad_maximum_fusion.refs_0_), channel_id=1, source_target_pairs={{0,4},{4,0},{8,12},{12,8},{16,20},{20,16},{24,28},{28,24},{32,36},... | collective-permute-start | bytes 3145736 | tf_op jit(solution)/shard_map/ppermute | solution.py:215
  60.7 12.6 %collective-permute-start.15 = (bf16[2048,256]{1,0:T(8,128)(2,1)}, bf16[2048,256]{1,0:T(8,128)(2,1)}, u32[]{:S(2)}, u32[]{:S(2)}) collective-permute-start(bf16[2048,256]{1,0:T(8,128)(2,1)} %collective-permute-done.4.refs_4_), channel_id=1, source_target_pairs={{0,4},{4,0},{8,12},{12,8},{16,20},{20,16},{24,28},{28,24},{32,36},... | collective-permute-start | bytes 3145736 | tf_op jit(solution)/shard_map/ppermute | solution.py:215
  60.8 12.5 %collective-permute-start.12 = (bf16[2048,256]{1,0:T(8,128)(2,1)}, bf16[2048,256]{1,0:T(8,128)(2,1)}, u32[]{:S(2)}, u32[]{:S(2)}) collective-permute-start(bf16[2048,256]{1,0:T(8,128)(2,1)} %collective-permute-done.3.refs_1_), channel_id=1, source_target_pairs={{0,4},{4,0},{8,12},{12,8},{16,20},{20,16},{24,28},{28,24},{32,36},... | collective-permute-start | bytes 3145736 | tf_op jit(solution)/shard_map/ppermute | solution.py:215
  62.5 10.8 %copy-start.6 = (s32[128]{0:T(128)}, s32[128]{0:T(128)S(1)}, u32[]{:S(2)}) copy-start(s32[128]{0:T(128)S(1)} %reshape.124.pick_ref) | copy-start | bytes 1540
  63.2 10.2 %collective-permute-start.13 = (bf16[1024,256]{1,0:T(8,128)(2,1)}, bf16[1024,256]{1,0:T(8,128)(2,1)S(1)}, u32[]{:S(2)}, u32[]{:S(2)}) collective-permute-start(bf16[1024,256]{1,0:T(8,128)(2,1)} %collective-permute-done.9.refs_2_), channel_id=1, source_target_pairs={{0,4},{4,0},{8,12},{12,8},{16,20},{20,16},{24,28},{28,24},{32,36},... | collective-permute-start | bytes 1572872 | tf_op jit(solution)/shard_map/ppermute | solution.py:215
  67.7 5.6 %collective-permute-start.14 = (bf16[1024,256]{1,0:T(8,128)(2,1)}, bf16[1024,256]{1,0:T(8,128)(2,1)S(1)}, u32[]{:S(2)}, u32[]{:S(2)}) collective-permute-start(bf16[1024,256]{1,0:T(8,128)(2,1)} %collective-permute-done.10.refs_3_), channel_id=1, source_target_pairs={{0,4},{4,0},{8,12},{12,8},{16,20},{20,16},{24,28},{28,24},{32,36},... | collective-permute-start | bytes 1572872 | tf_op jit(solution)/shard_map/ppermute | solution.py:215
  73.3 0.8 copy-start.7
  73.4 0.9 copy-start.8

commit v3 on v2

v3 whole, which is shorter than its diff:
```python
import functools
import math

import jax
import jax.numpy as jnp
from jax import lax
from jax.experimental import pallas as pl
from jax.experimental.pallas import tpu as pltpu
from jax.sharding import PartitionSpec as P

WINDOW_TOKENS = 512
MASKED = -1e30
LOG2E = 1.4426950408889634
ROW_TILE = 256
GROUP = 16
NEAR_TOKENS = 128
SIDE = 4
CORES = 2
NT = (((1,), (1,)), ((), ()))
F32 = jnp.float32
BF16 = jnp.bfloat16


def place(x, z, core):
    return ((x % SIDE) * SIDE + z % SIDE) * CORES + core


def pairs(target):
    spots = [(x, z, c) for x in range(SIDE) for z in range(SIDE) for c in range(CORES)]
    return [(place(*spot), place(*target(*spot))) for spot in spots]


def first_axis(steps):
    return pairs(lambda x, z, c: (x, z + steps, c) if c == 0 else (x + steps, z, c))


def second_axis(steps):
    return pairs(lambda x, z, c: (x + steps, z, c) if c == 0 else (x, z + steps, c))


def other_core():
    return pairs(lambda x, z, c: (x, z, 1 - c))


def in_hbm(value):
    return pltpu.with_memory_space_constraint(value, pltpu.HBM)


def token_one_hot(rows, first_row, heads):
    token = (lax.broadcasted_iota(jnp.int32, (rows, 128), 0) + first_row) // heads
    lane = lax.broadcasted_iota(jnp.int32, (rows, 128), 1)
    return jnp.where(token == lane, 1.0, 0.0).astype(BF16)


def split(value):
    high = value.astype(BF16)
    return high, (value - high.astype(F32)).astype(BF16)


def near_kernel(heads, first_step, index_ref, q_ref, previous_ref, own_ref, *refs):
    win_ref, kv_ref, bias_ref = refs[-3:]
    head_dim = q_ref.shape[-1]
    tokens = NEAR_TOKENS
    rows = tokens * heads
    rows_here = own_ref.shape[0]
    step = pl.program_id(0) + first_step
    factor = LOG2E / math.sqrt(head_dim)
    span = WINDOW_TOKENS + tokens
    lead = WINDOW_TOKENS

    @pl.when(pl.program_id(0) == 0)
    def _():
        kv_ref[pl.ds(lead - rows_here, rows_here), :] = previous_ref[...]
        kv_ref[pl.ds(lead, rows_here), :] = own_ref[...]

    first = pl.multiple_of(step * tokens, tokens)
    key = lax.broadcasted_iota(jnp.int32, (span, 128), 0) - lead
    tok = lax.broadcasted_iota(jnp.int32, (span, 128), 1)
    start = index_ref[0] * rows_here + step * tokens
    seen = (key > tok - WINDOW_TOKENS) & (key <= tok) & (key + start >= 0)
    bias_ref[...] = jnp.where(seen, 0.0, MASKED).astype(BF16)
    keys = jnp.concatenate([kv_ref[pl.ds(first, span), :head_dim], bias_ref[...]], axis=1)
    values = jnp.concatenate(
        [kv_ref[pl.ds(first, span), head_dim:], jnp.ones((span, 128), BF16)], axis=1
    )

    def score(at):
        q = jnp.concatenate([q_ref[pl.ds(at, ROW_TILE), :], token_one_hot(ROW_TILE, at, heads)], axis=1)
        return lax.dot_general(q, keys, NT, preferred_element_type=F32)

    ahead = score(0)
    for at in range(0, rows, ROW_TILE):
        scores = ahead
        if at + ROW_TILE < rows:
            ahead = score(at + ROW_TILE)
        peak = jnp.max(scores, axis=-1, keepdims=True)
        weights = jnp.exp2(scores * factor - peak * factor).astype(BF16)
        both = jnp.dot(weights, values, preferred_element_type=F32)
        win_ref[pl.ds(at, ROW_TILE), :] = both[:, :head_dim] / both[:, head_dim:]


def far_kernel(
    block_len, heads, picks, places, pick_ref, row_ref, index_ref, q_ref, logit_ref, win_ref, id_ref, weight_ref,
    *refs,
):
    piece_refs = refs[: len(places)]
    out_ref, all_ref, comp_ref, keys_ref, values_ref, sems = refs[len(places) :]
    head_dim = q_ref.shape[-1]
    rows = block_len * heads
    blk = pl.program_id(0)
    steps = pl.num_programs(0)
    factor = LOG2E / math.sqrt(head_dim)
    own_block = index_ref[0] * steps + blk

    @pl.when(blk == 0)
    def _():
        copies = [
            pltpu.make_async_copy(piece, all_ref.at[pl.ds(at, piece.shape[0]), :], sems.at[n])
            for n, (piece, at) in enumerate(zip(piece_refs, places))
        ]
        for copy in copies:
            copy.start()
        values_ref[:, head_dim:] = jnp.ones((picks * block_len, 128), BF16)

        def compress(group, carry):
            parts = []
            for n in range(GROUP):
                base = pl.multiple_of((group * GROUP + n) * block_len, block_len)
                block = all_ref[pl.ds(base, block_len), :].astype(F32)
                parts.append(jnp.sum(block * weight_ref[...], axis=0, keepdims=True))
            high, low = split(jnp.concatenate(parts, axis=0))
            at = pl.multiple_of(group * GROUP, GROUP)
            comp_ref[0, pl.ds(at, GROUP), :] = high
            comp_ref[1, pl.ds(at, GROUP), :] = low
            return carry

        each = GROUP * block_len
        for copy, piece, at in zip(copies, piece_refs, places):
            copy.wait()
            lax.fori_loop(at // each, (at + piece.shape[0]) // each, compress, 0)

    key = lax.broadcasted_iota(jnp.int32, (block_len, 128), 0)
    tok = lax.broadcasted_iota(jnp.int32, (block_len, 128), 1)
    for pick in range(picks):
        chosen = pick_ref[blk * picks + pick]
        source = pl.multiple_of(row_ref[blk * picks + pick], block_len)
        into = pl.ds(pick * block_len, block_len)
        last = jnp.where(chosen < own_block, block_len, jnp.where(chosen == own_block, 0, -2 * block_len))
        keys_ref[into, :head_dim] = all_ref[pl.ds(source, block_len), :head_dim]
        values_ref[into, :head_dim] = all_ref[pl.ds(source, block_len), head_dim:]
        keys_ref[into, head_dim:] = jnp.where(key <= tok + last, 0.0, MASKED).astype(BF16)
    comp_keys = jnp.concatenate([comp_ref[0, :, :head_dim], comp_ref[1, :, :head_dim]], axis=1)
    comp_values = jnp.concatenate([comp_ref[0, :, head_dim:], comp_ref[1, :, head_dim:]], axis=1)
    gates = jax.nn.sigmoid(logit_ref[0])

    def spread(branch, at):
        return jnp.concatenate(
            [
                jnp.broadcast_to(gates[branch, :, t : t + 1], (heads, 128))
                for t in range(at // heads, (at + ROW_TILE) // heads)
            ],
            axis=0,
        )

    def score(at):
        q = q_ref[pl.ds(at, ROW_TILE), :]
        hot = token_one_hot(ROW_TILE, at, heads)
        sel = lax.dot_general(
            jnp.concatenate([q, hot], axis=1), keys_ref[...], NT, preferred_element_type=F32
        )
        comp = lax.dot_general(
            jnp.concatenate([q, q], axis=1), comp_keys, NT, preferred_element_type=F32
        )
        return sel, comp

    ahead = score(0)
    for at in range(0, rows, ROW_TILE):
        scores, comp_scores = ahead
        if at + ROW_TILE < rows:
            ahead = score(at + ROW_TILE)
        peak = jnp.max(scores, axis=-1, keepdims=True)
        weights = jnp.exp2(scores * factor - peak * factor).astype(BF16)
        both = jnp.dot(weights, values_ref[...], preferred_element_type=F32)
        sel = both[:, :head_dim] / both[:, head_dim:]
        token = (lax.broadcasted_iota(jnp.int32, (ROW_TILE, 1), 0) + at) // heads
        limit = own_block + jnp.where(token == block_len - 1, 1, 0)
        scores = jnp.where(id_ref[...] < limit, comp_scores, MASKED)
        peak = jnp.maximum(jnp.max(scores, axis=-1, keepdims=True), 0.0)
        weights = jnp.exp2(scores * factor - peak * factor)
        total = jnp.sum(weights, axis=-1, keepdims=True) + jnp.exp2(-peak * factor)
        both = jnp.dot(weights.astype(BF16), comp_values, preferred_element_type=F32)
        merged = (
            spread(0, at) * ((both[:, :head_dim] + both[:, head_dim:]) / total)
            + spread(1, at) * sel
            + spread(2, at) * win_ref[pl.ds(at, ROW_TILE), :]
        )
        out_ref[pl.ds(at, ROW_TILE), :] = merged.astype(BF16)


def partial_logits(hidden_in, gate_weight):
    return lax.dot_general(
        gate_weight, hidden_in, (((0,), (1,)), ((), ())), preferred_element_type=F32
    )


def gate_logits(partial_value):
    parts = lax.axis_size("head")
    mine = lax.axis_index("head")
    columns = partial_value.shape[0] // parts

    def chunk(which):
        return lax.dynamic_slice_in_dim(partial_value, lax.rem(which, parts) * columns, columns, 0)

    total = chunk(mine)
    for steps in range(1, parts):
        total = total + lax.ppermute(
            chunk(mine + steps), "head", [(n, (n + steps) % parts) for n in range(parts)]
        )
    return total


def send(value, perm):
    return lax.ppermute(value, "ctx", perm)


def gather_line(key_value):
    ahead = send(key_value, perm=first_axis(-1))
    behind = send(key_value, perm=first_axis(1))
    across = send(key_value, perm=first_axis(2))
    low = jnp.concatenate([key_value, ahead], axis=0)
    high = jnp.concatenate([across, behind], axis=0)
    return low, high


def gather_pieces(low, high, first_work, second_work):
    next_low = send(low, perm=second_axis(-1))
    last_high = send(high, perm=second_axis(1))
    next_high = send(high, perm=second_axis(-1))
    last_low = send(low, perm=second_axis(1))
    next_low, last_high, done = lax.optimization_barrier((next_low, last_high, first_work()))
    far_low = send(next_low, perm=second_axis(-1))
    far_high = send(last_high, perm=second_axis(1))
    far_low, far_high, done = lax.optimization_barrier((far_low, far_high, second_work(done)))
    mine = [low, high, next_low, next_high, far_low, far_high, last_low, last_high]
    return mine + [send(piece, perm=other_core()) for piece in mine], done


def row_of_block(block, index, blocks_here, block_len):
    shard = block // blocks_here
    core = shard % CORES
    across_x = (shard // (SIDE * CORES) - index // (SIDE * CORES)) % SIDE
    across_z = (shard // CORES - index // CORES) % SIDE
    along = jnp.where(core == 0, across_z, across_x)
    line = jnp.where(core == 0, across_x, across_z)
    piece = jnp.where(core == index % CORES, 0, SIDE) + line
    return ((piece * SIDE + along) * blocks_here + block % blocks_here) * block_len


def run_near(index, queries, previous, own, heads, first_step, steps, before=None):
    all_rows, head_dim = queries.shape
    rows_here = own.shape[0]
    whole = pl.BlockSpec((rows_here, 2 * head_dim), lambda b, *_: (0, 0))
    tile = pl.BlockSpec((NEAR_TOKENS * heads, head_dim), lambda b, *_: (b + first_step, 0))
    earlier = [] if before is None else [before]
    return pl.pallas_call(
        functools.partial(near_kernel, heads, first_step),
        out_shape=pltpu.HBM((all_rows, head_dim), F32),
        grid_spec=pltpu.PrefetchScalarGridSpec(
            num_scalar_prefetch=1,
            grid=(steps,),
            in_specs=[tile, whole, whole] + [pl.BlockSpec(memory_space=pl.ANY)] * len(earlier),
            out_specs=tile,
            scratch_shapes=[
                pltpu.VMEM((rows_here + WINDOW_TOKENS, 2 * head_dim), BF16),
                pltpu.VMEM((WINDOW_TOKENS + NEAR_TOKENS, 128), BF16),
            ],
        ),
        input_output_aliases={4: 0} if earlier else {},
        compiler_params=pltpu.CompilerParams(vmem_limit_bytes=56 << 20),
        cost_estimate=pl.CostEstimate(
            flops=steps * 4 * NEAR_TOKENS * heads * head_dim * 1024,
            transcendentals=steps * NEAR_TOKENS * heads * 640,
            bytes_accessed=steps * NEAR_TOKENS * heads * head_dim * 6,
        ),
        name="near",
    )(index, queries, previous, own, *earlier)


def run_far(chosen, source_rows, index, queries, logits, win, ids_by_slot, compress_w, pieces, places):
    all_rows, head_dim = queries.shape
    blocks_here, branches, heads, block_len = logits.shape
    picks = chosen.shape[0] // blocks_here
    total_blocks = ids_by_slot.shape[1]
    tile = pl.BlockSpec((block_len * heads, head_dim), lambda b, *_: (b, 0))
    whole = lambda shape: pl.BlockSpec(shape, lambda b, *_: (0, 0))
    return pl.pallas_call(
        functools.partial(far_kernel, block_len, heads, picks, places),
        out_shape=jax.ShapeDtypeStruct((all_rows, head_dim), BF16),
        grid_spec=pltpu.PrefetchScalarGridSpec(
            num_scalar_prefetch=3,
            grid=(blocks_here,),
            in_specs=[
                tile,
                pl.BlockSpec((1, branches, heads, block_len), lambda b, *_: (b, 0, 0, 0)),
                tile,
                whole((1, total_blocks)),
                whole((block_len, 2 * head_dim)),
            ]
            + [pl.BlockSpec(memory_space=pl.ANY)] * len(pieces),
            out_specs=tile,
            scratch_shapes=[
                pltpu.VMEM((total_blocks * block_len, 2 * head_dim), BF16),
                pltpu.VMEM((2, total_blocks, 2 * head_dim), BF16),
                pltpu.VMEM((picks * block_len, 2 * head_dim), BF16),
                pltpu.VMEM((picks * block_len, 2 * head_dim), BF16),
                pltpu.SemaphoreType.DMA((len(pieces),)),
            ],
        ),
        compiler_params=pltpu.CompilerParams(vmem_limit_bytes=56 << 20),
        cost_estimate=pl.CostEstimate(
            flops=8 * all_rows * head_dim * 1280, transcendentals=all_rows * 1280, bytes_accessed=20 << 20
        ),
        name="far",
    )(chosen, source_rows, index, queries, logits, win, ids_by_slot, compress_w, *[in_hbm(p) for p in pieces])


def body(
    hidden_in,
    gate_weight,
    encoded_queries,
    encoded_keys,
    value_tensor,
    comp_key_weight,
    comp_value_weight,
    selection,
):
    rows_here, heads_here, head_dim = encoded_queries.shape
    block_len = comp_key_weight.shape[0]
    blocks_here = rows_here // block_len
    shard_parts = lax.axis_size("ctx")
    all_rows = rows_here * heads_here
    place_here = lax.axis_index("ctx").astype(jnp.int32)
    index = place_here.reshape(1)

    key_value = jnp.concatenate([encoded_keys, value_tensor], axis=-1).reshape(rows_here, 2 * head_dim)
    low, high = gather_line(key_value)
    previous = send(key_value, perm=[(n, n + 1) for n in range(shard_parts - 1)])
    previous, hidden_in = lax.optimization_barrier((previous, hidden_in))
    logits = gate_logits(partial_logits(hidden_in, gate_weight))
    previous, logits = lax.optimization_barrier((previous, logits))
    compress_w = jnp.concatenate([comp_key_weight, comp_value_weight], axis=-1)
    queries = in_hbm(encoded_queries.reshape(all_rows, head_dim))
    total_blocks = blocks_here * shard_parts
    chosen = selection.reshape(-1)
    source_rows = row_of_block(chosen, place_here, blocks_here, block_len)
    block_ids = jnp.arange(total_blocks, dtype=jnp.int32)
    placed = row_of_block(block_ids, place_here, blocks_here, block_len) // block_len
    slots = jnp.arange(total_blocks, dtype=jnp.int32)
    ids_by_slot = jnp.sum(
        jnp.where(placed[None, :] == slots[:, None], block_ids[None, :], 0), axis=1, dtype=jnp.int32
    ).reshape(1, total_blocks)

    near_steps = rows_here // NEAR_TOKENS // 2
    near = functools.partial(run_near, index, queries, previous, key_value, heads_here)
    pieces, win = gather_pieces(
        low, high, lambda: near(0, near_steps), lambda done: near(near_steps, near_steps, done)
    )
    logits = logits.reshape(heads_here, 3, blocks_here, block_len).transpose(2, 1, 0, 3)

    out = run_far(
        chosen, source_rows, index, queries, logits, win, ids_by_slot, compress_w,
        pieces, [n * low.shape[0] for n in range(len(pieces))],
    )
    return out.reshape(rows_here, heads_here, head_dim)


def solution(mesh):
    return jax.shard_map(
        body,
        mesh=mesh,
        in_specs=(
            P("ctx", "head"),
            P("head", None),
            P("ctx", "head", None),
            P("ctx", "head", None),
            P("ctx", "head", None),
            P(),
            P(),
            P("ctx", "head", None),
        ),
        out_specs=P("ctx", "head", None),
        check_vma=False,
    )
```

time: 106 us -> 86.2 us (0.81)
  Pallas kernels: 50.5 us -> 39.2 us
  starting transfers between devices: 35.8 us -> 31.6 us
  waiting for transfers between devices: 5.67 us -> 2.56 us
    pallas_call x2 -> x3, Pallas kernels: 50.5 us -> 39.2 us  [the longest x1 25.3 us: run_far(): pl.pallas_call(functools.partial(far_kernel, block_len, heads, picks, pla...]
    ppermute x1 -> x0, starting transfers between devices: 5.85 us -> none  [near(): lax.ppermute(key_value, 'ctx', [(n, n + 1) for n in range(shard_parts - 1)])]
    slice x2 -> x0, local copies, waits for them, and re-layouts: 3.75 us -> none  [the longest x1 1.88 us: gather_pieces(): last_line[half:]]
    concatenate x0 -> x1, local copies, waits for them, and re-layouts: none -> 1.66 us  [gather_line(): high = jnp.concatenate([across, behind], axis=0)]
    ppermute x1 -> x0, waiting for transfers between devices: 1.6 us -> none  [near(): lax.ppermute(key_value, 'ctx', [(n, n + 1) for n in range(shard_parts - 1)])]
    ppermute x12 -> x18, starting transfers between devices: 25.5 us -> 26.5 us  [send(): return lax.ppermute(value, 'ctx', perm)]
    ppermute x12 -> x18, waiting for transfers between devices: 3.3 us -> 2.55 us  [send(): return lax.ppermute(value, 'ctx', perm)]
    unnamed x19 -> x22, local copies, waits for them, and re-layouts: 1.54 us -> 2.25 us
  transfers between devices with their start and end apart: 16 -> 21, of which waited for: 5 -> 3; matrix products, arithmetic and copies ran while one was open for 9% -> 13% of each run, Pallas kernels for 18% -> 16%
where the time goes in v3:
time: 86.2 us; the launch traced here: 85.9 us
  Pallas kernels  39.2 us (45%)
  starting transfers between devices  31.6 us (37%)
  local copies, waits for them, and re-layouts  5.56 us (6%)
  other arithmetic  4.75 us (6%)
  waiting for transfers between devices  2.56 us (3%)
  matrix products  1.93 us (2%)
    ppermute x18, starting transfers between devices, send(): return lax.ppermute(value, 'ctx', perm)  26.5 us
    pallas_call x1, Pallas kernels, run_far(): pl.pallas_call(functools.partial(far_kernel, block_len, heads, picks, pla...  25.3 us
    pallas_call x2, Pallas kernels, run_near(): pl.pallas_call(functools.partial(near_kernel, heads, first_step), out_sha...  13.8 us
    ppermute x3, starting transfers between devices, gate_logits(): lax.ppermute(chunk(mine + steps), 'head', [(n, (n + steps) % parts) for n...  5.05 us
    ppermute x18, waiting for transfers between devices, send(): return lax.ppermute(value, 'ctx', perm)  2.55 us
    unnamed x22, local copies, waits for them, and re-layouts  2.25 us
    dot_general x1, matrix products, partial_logits(): lax.dot_general(gate_weight, hidden_in, (((0,), (1,)), ((), ())), preferr...  1.93 us
  transfers between devices with their start and end apart: 21, of which 3 were waited for; matrix products, arithmetic and copies ran while one was open for 13% of the time, Pallas kernels for 16%

profile of v3, /device:TPU:1, one launch (start us, length us, event | category | flops | bytes accessed | tf_op | source)
XLA Modules:
  0.0 85.9 jit_solution(3702169548248154551)
XLA Ops:
  0.0 1.1 %maximum_bitcast_fusion.own_ref = bf16[512,256]{1,0:T(8,128)(2,1)S(1)} fusion(bf16[512,1,128]{2,0,1:T(8,128)(2,1)} %param.12, bf16[512,1,128]{2,0,1:T(8,128)(2,1)} %param.11), kind=kLoop, calls=%fused_computation.1 | loop fusion | flops 524288 | bytes 524288 | tf_op jit(solution)/shard_map/reshape | solution.py:345
  1.1 4.9 %collective-permute-start = (bf16[512,256]{1,0:T(8,128)(2,1)S(1)}, bf16[512,256]{1,0:T(8,128)(2,1)S(1)}, u32[]{:S(2)}, u32[]{:S(2)}) collective-permute-start(bf16[512,256]{1,0:T(8,128)(2,1)S(1)} %maximum_bitcast_fusion.own_ref), channel_id=1, source_target_pairs={{0,4},{4,8},{8,12},{12,16},{16,20},{20,24},{24,28},{28,32},{32,36}... | collective-permute-start | bytes 786440 | tf_op jit(solution)/shard_map/ppermute | solution.py:223
  6.1 1.3 %collective-permute-start.7 = (bf16[512,256]{1,0:T(8,128)(2,1)S(1)}, bf16[512,256]{1,0:T(8,128)(2,1)}, u32[]{:S(2)}, u32[]{:S(2)}) collective-permute-start(bf16[512,256]{1,0:T(8,128)(2,1)S(1)} %maximum_bitcast_fusion.own_ref), channel_id=1, source_target_pairs={{0,8},{4,36},{8,16},{12,44},{16,24},{20,52},{24,0},{28,60},{32,40}... | collective-permute-start | bytes 786440 | tf_op jit(solution)/shard_map/ppermute | solution.py:223
  7.4 2.5 %collective-permute-start.6 = (bf16[512,256]{1,0:T(8,128)(2,1)S(1)}, bf16[512,256]{1,0:T(8,128)(2,1)}, u32[]{:S(2)}, u32[]{:S(2)}) collective-permute-start(bf16[512,256]{1,0:T(8,128)(2,1)S(1)} %maximum_bitcast_fusion.own_ref), channel_id=1, source_target_pairs={{0,16},{4,68},{8,24},{12,76},{16,0},{20,84},{24,8},{28,92},{32,48}... | collective-permute-start | bytes 786440 | tf_op jit(solution)/shard_map/ppermute | solution.py:223
  9.8 1.2 %collective-permute-start.4 = (bf16[512,256]{1,0:T(8,128)(2,1)S(1)}, bf16[512,256]{1,0:T(8,128)(2,1)S(1)}, u32[]{:S(2)}, u32[]{:S(2)}) collective-permute-start(bf16[512,256]{1,0:T(8,128)(2,1)S(1)} %maximum_bitcast_fusion.own_ref), channel_id=1, source_target_pairs={{0,24},{4,100},{8,0},{12,108},{16,8},{20,116},{24,16},{28,124},{32... | collective-permute-start | bytes 786440 | tf_op jit(solution)/shard_map/ppermute | solution.py:223
  11.0 0.6 collective-permute-done.previous_ref
  11.6 1.9 %fusion.17 = f32[512,192]{0,1:T(8,128)S(1)} fusion(bf16[512,1792]{1,0:T(8,128)(2,1)S(1)} %copy-done, bf16[1792,192]{0,1:T(8,128)(2,1)} %param.9), kind=kOutput, calls=%fused_computation.75 | convolution fusion | flops 352321536 | bytes 2916352 | tf_op jit(solution)/shard_map/dot_general | solution.py:201
  13.5 0.7 dynamic-slice_bitcast_fusion.2
  14.2 1.3 %collective-permute-start.1 = (f32[48,512]{1,0:T(8,128)}, f32[48,512]{1,0:T(8,128)}, u32[]{:S(2)}, u32[]{:S(2)}) collective-permute-start(f32[48,512]{1,0:T(8,128)} %get-tuple-element.25), channel_id=1, source_target_pairs={{0,1},{1,2},{2,3},{3,0},{4,5},{5,6},{6,7},{7,4},{8,9},{9,10},{10,1... | collective-permute-start | bytes 294920 | tf_op jit(solution)/shard_map/ppermute | solution.py:216
  15.5 1.4 %collective-permute-start.3 = (f32[48,512]{1,0:T(8,128)}, f32[48,512]{1,0:T(8,128)}, u32[]{:S(2)}, u32[]{:S(2)}) collective-permute-start(f32[48,512]{1,0:T(8,128)} %get-tuple-element.26), channel_id=1, source_target_pairs={{0,3},{1,0},{2,1},{3,2},{4,7},{5,4},{6,5},{7,6},{8,11},{9,8},{10,9... | collective-permute-start | bytes 294920 | tf_op jit(solution)/shard_map/ppermute | solution.py:216
  17.0 2.3 %collective-permute-start.2 = (f32[48,512]{1,0:T(8,128)}, f32[48,512]{1,0:T(8,128)}, u32[]{:S(2)}, u32[]{:S(2)}) collective-permute-start(f32[48,512]{1,0:T(8,128)} %get-tuple-element.27), channel_id=1, source_target_pairs={{0,2},{1,3},{2,0},{3,1},{4,6},{5,7},{6,4},{7,5},{8,10},{9,11},{10,... | collective-permute-start | bytes 294920 | tf_op jit(solution)/shard_map/ppermute | solution.py:216
  19.4 0.0 collective-permute-done.6
  19.4 1.9 %collective-permute-start.5 = (bf16[1024,256]{1,0:T(8,128)(2,1)S(1)}, bf16[1024,256]{1,0:T(8,128)(2,1)}, u32[]{:S(2)}, u32[]{:S(2)}) collective-permute-start(bf16[1024,256]{1,0:T(8,128)(2,1)S(1)} %pad_maximum_fusion.refs_0_), channel_id=1, source_target_pairs={{0,96},{4,28},{8,104},{12,4},{16,112},{20,12},{24,120},{28,20},{32... | collective-permute-start | bytes 1572872 | tf_op jit(solution)/shard_map/ppermute | solution.py:223
  21.3 1.7 %constant_dynamic-update-slice_fusion.1 = bf16[1024,256]{1,0:T(8,128)(2,1)} fusion(bf16[512,256]{1,0:T(8,128)(2,1)} %collective-permute-done.6), kind=kLoop, calls=%fused_computation.13 | loop fusion | bytes 524288
  23.0 0.0 collective-permute-done.7
  23.0 1.7 %constant_dynamic-update-slice_fusion.refs_1_ = bf16[1024,256]{1,0:T(8,128)(2,1)} fusion(bf16[1024,256]{1,0:T(8,128)(2,1)} %constant_dynamic-update-slice_fusion.1, bf16[512,256]{1,0:T(8,128)(2,1)} %collective-permute-done.7), kind=kLoop, calls=%fused_computation.12 | loop fusion | bytes 524288 | tf_op jit(solution)/shard_map/concatenate | solution.py:231
  24.6 0.0 collective-permute-start.8
  24.7 0.0 collective-permute-done.1
  24.7 1.1 %collective-permute-start.12 = (bf16[1024,256]{1,0:T(8,128)(2,1)S(1)}, bf16[1024,256]{1,0:T(8,128)(2,1)}, u32[]{:S(2)}, u32[]{:S(2)}) collective-permute-start(bf16[1024,256]{1,0:T(8,128)(2,1)S(1)} %pad_maximum_fusion.refs_0_), channel_id=1, source_target_pairs={{0,32},{4,12},{8,40},{12,20},{16,48},{20,28},{24,56},{28,4},{32,64... | collective-permute-start | bytes 1572872 | tf_op jit(solution)/shard_map/ppermute | solution.py:223
  25.8 0.0 collective-permute-done.3
  25.8 0.0 collective-permute-done.2
  25.8 1.0 %fusion.1 = f32[48,512]{1,0:T(8,128)S(1)} fusion(f32[48,512]{1,0:T(8,128)} %collective-permute-done.3, f32[48,512]{1,0:T(8,128)} %collective-permute-done.2, f32[48,512]{1,0:T(8,128)} %collective-permute-done.1, f32[512,192]{0,1:T(8,128)S(1)} %fusion.17, s32[]{:T(128)S(6)} %select_n.184), kind=kLoop, calls=%fused_computation.7 | loop fusion | flops 73728 | bytes 491524 | tf_op jit(solution)/shard_map/add | solution.py:216
  26.8 0.0 copy-start.6
  26.8 6.9 %near.2.refs_0_ = f32[8192,128]{1,0:T(8,128)} custom-call(s32[1]{0:T(128)} %bitcast.index_ref, bf16[8192,128]{1,0:T(8,128)(2,1)} %bitcast.23, bf16[512,256]{1,0:T(8,128)(2,1)} %copy-done.3, bf16[512,256]{1,0:T(8,128)(2,1)} %copy-done.1), custom_call_target="tpu_custom_call" | custom-call | flops 2147483648 | bytes 3145728 | tf_op jit(solution)/shard_map/near/pallas_call | solution.py:265
  33.7 0.0 collective-permute-done.5.refs_2_
  33.7 0.8 collective-permute-done.8.refs_7_
  34.5 0.9 %collective-permute-start.9 = (bf16[1024,256]{1,0:T(8,128)(2,1)}, bf16[1024,256]{1,0:T(8,128)(2,1)S(1)}, u32[]{:S(2)}, u32[]{:S(2)}) collective-permute-start(bf16[1024,256]{1,0:T(8,128)(2,1)} %collective-permute-done.5.refs_2_), channel_id=1, source_target_pairs={{0,96},{4,28},{8,104},{12,4},{16,112},{20,12},{24,120},{28,20},{32... | collective-permute-start | bytes 1572872 | tf_op jit(solution)/shard_map/ppermute | solution.py:223
  35.4 0.6 collective-permute-start.10
  36.0 3.5 %collective-permute-start.13 = (bf16[1024,256]{1,0:T(8,128)(2,1)S(1)}, bf16[1024,256]{1,0:T(8,128)(2,1)}, u32[]{:S(2)}, u32[]{:S(2)}) collective-permute-start(bf16[1024,256]{1,0:T(8,128)(2,1)S(1)} %pad_maximum_fusion.refs_0_), channel_id=1, source_target_pairs={{0,4},{4,0},{8,12},{12,8},{16,20},{20,16},{24,28},{28,24},{32,36},... | collective-permute-start | bytes 1572872 | tf_op jit(solution)/shard_map/ppermute | solution.py:223
  39.4 3.7 %collective-permute-start.11 = (bf16[1024,256]{1,0:T(8,128)(2,1)}, bf16[1024,256]{1,0:T(8,128)(2,1)}, u32[]{:S(2)}, u32[]{:S(2)}) collective-permute-start(bf16[1024,256]{1,0:T(8,128)(2,1)} %constant_dynamic-update-slice_fusion.refs_1_), channel_id=1, source_target_pairs={{0,96},{4,28},{8,104},{12,4},{16,112},{20,12},{24,120},{28,20},{32... | collective-permute-start | bytes 1572872 | tf_op jit(solution)/shard_map/ppermute | solution.py:223
  43.2 3.6 %collective-permute-start.19 = (bf16[1024,256]{1,0:T(8,128)(2,1)}, bf16[1024,256]{1,0:T(8,128)(2,1)}, u32[]{:S(2)}, u32[]{:S(2)}) collective-permute-start(bf16[1024,256]{1,0:T(8,128)(2,1)} %collective-permute-done.12.refs_6_), channel_id=1, source_target_pairs={{0,4},{4,0},{8,12},{12,8},{16,20},{20,16},{24,28},{28,24},{32,36},... | collective-permute-start | bytes 1572872 | tf_op jit(solution)/shard_map/ppermute | solution.py:223
  46.8 0.5 broadcast.288
  47.3 0.6 reduce.3
  48.0 0.1 reshape.127.pick_ref
  48.1 0.0 copy-start.5
  48.1 6.9 %near.3.win_ref = f32[8192,128]{1,0:T(8,128)} custom-call(s32[1]{0:T(128)} %bitcast.index_ref, bf16[8192,128]{1,0:T(8,128)(2,1)} %bitcast.24, bf16[512,256]{1,0:T(8,128)(2,1)} %copy-done.3, bf16[512,256]{1,0:T(8,128)(2,1)} %copy-done.1, f32[8192,128]{1,0:T(8,128)} %near.2.refs_0_), custom_call_target="tpu_custom_call", output_to_operand_aliasing={{}: (4, {})} | custom-call | flops 2147483648 | bytes 3145728 | tf_op jit(solution)/shard_map/near/pallas_call | solution.py:265
  55.0 0.1 collective-permute-start.15
  55.1 0.5 collective-permute-start.20
  55.6 0.1 collective-permute-start.16
  55.7 0.4 collective-permute-start.17
  56.1 0.3 collective-permute-start.18
  56.4 0.6 pad_maximum_fusion.1.weight_ref
  57.1 0.7 select_reduce_fusion
  57.7 0.6 fusion.16.row_ref
  58.3 0.1 reshape.131
  58.4 0.7 copy.13
  59.2 1.2 %collective-permute-done.16.refs_11_ = bf16[1024,256]{1,0:T(8,128)(2,1)} collective-permute-done((bf16[1024,256]{1,0:T(8,128)(2,1)}, bf16[1024,256]{1,0:T(8,128)(2,1)}, u32[]{:S(2)}, u32[]{:S(2)}) %collective-permute-start.16) | collective-permute-done | bytes 524320 | tf_op jit(solution)/shard_map/ppermute | solution.py:223
  60.4 25.3 %far.1 = bf16[8192,128]{1,0:T(8,128)(2,1)} custom-call(s32[128]{0:T(128)} %copy-done.7, s32[128]{0:T(128)} %fusion.16.row_ref, s32[1]{0:T(128)} %bitcast.index_ref, bf16[8192,128]{1,0:T(8,128)(2,1)} %bitcast.25, f32[8,3,16,64]{3,2,1,0:T(8,128)} %bitcast.26, f32[8192,128]{1,0:T(8,128)} %near.3.win_ref, s32[1,256]{1,0:T(1,128)} %bitcast.27, ...), custom_call_target="tpu_custom_call" | custom-call | flops 10737418240 | bytes 20971520 | tf_op jit(solution)/shard_map/far/pallas_call | solution.py:296
  (33 shorter events, 0.1 us)
Async XLA Ops:
  0.0 11.6 %copy-start = (bf16[512,1792]{1,0:T(8,128)(2,1)S(1)}, bf16[512,1792]{1,0:T(8,128)(2,1)}, u32[]{:S(2)}) copy-start(bf16[512,1792]{1,0:T(8,128)(2,1)} %param.8) | copy-start | bytes 5505028
  1.1 18.2 %copy-start.1 = (bf16[512,256]{1,0:T(8,128)(2,1)}, bf16[512,256]{1,0:T(8,128)(2,1)S(1)}, u32[]{:S(2)}) copy-start(bf16[512,256]{1,0:T(8,128)(2,1)S(1)} %maximum_bitcast_fusion.own_ref) | copy-start | bytes 786436
  1.1 10.4 %collective-permute-start = (bf16[512,256]{1,0:T(8,128)(2,1)S(1)}, bf16[512,256]{1,0:T(8,128)(2,1)S(1)}, u32[]{:S(2)}, u32[]{:S(2)}) collective-permute-start(bf16[512,256]{1,0:T(8,128)(2,1)S(1)} %maximum_bitcast_fusion.own_ref), channel_id=1, source_target_pairs={{0,4},{4,8},{8,12},{12,16},{16,20},{20,24},{24,28},{28,32},{32,36}... | collective-permute-start | bytes 786440 | tf_op jit(solution)/shard_map/ppermute | solution.py:223
  6.1 16.9 %collective-permute-start.7 = (bf16[512,256]{1,0:T(8,128)(2,1)S(1)}, bf16[512,256]{1,0:T(8,128)(2,1)}, u32[]{:S(2)}, u32[]{:S(2)}) collective-permute-start(bf16[512,256]{1,0:T(8,128)(2,1)S(1)} %maximum_bitcast_fusion.own_ref), channel_id=1, source_target_pairs={{0,8},{4,36},{8,16},{12,44},{16,24},{20,52},{24,0},{28,60},{32,40}... | collective-permute-start | bytes 786440 | tf_op jit(solution)/shard_map/ppermute | solution.py:223
  7.4 12.0 %collective-permute-start.6 = (bf16[512,256]{1,0:T(8,128)(2,1)S(1)}, bf16[512,256]{1,0:T(8,128)(2,1)}, u32[]{:S(2)}, u32[]{:S(2)}) collective-permute-start(bf16[512,256]{1,0:T(8,128)(2,1)S(1)} %maximum_bitcast_fusion.own_ref), channel_id=1, source_target_pairs={{0,16},{4,68},{8,24},{12,76},{16,0},{20,84},{24,8},{28,92},{32,48}... | collective-permute-start | bytes 786440 | tf_op jit(solution)/shard_map/ppermute | solution.py:223
  9.8 7.2 %collective-permute-start.4 = (bf16[512,256]{1,0:T(8,128)(2,1)S(1)}, bf16[512,256]{1,0:T(8,128)(2,1)S(1)}, u32[]{:S(2)}, u32[]{:S(2)}) collective-permute-start(bf16[512,256]{1,0:T(8,128)(2,1)S(1)} %maximum_bitcast_fusion.own_ref), channel_id=1, source_target_pairs={{0,24},{4,100},{8,0},{12,108},{16,8},{20,116},{24,16},{28,124},{32... | collective-permute-start | bytes 786440 | tf_op jit(solution)/shard_map/ppermute | solution.py:223
  11.6 7.8 %copy-start.3 = (bf16[512,256]{1,0:T(8,128)(2,1)}, bf16[512,256]{1,0:T(8,128)(2,1)S(1)}, u32[]{:S(2)}) copy-start(bf16[512,256]{1,0:T(8,128)(2,1)S(1)} %collective-permute-done.previous_ref) | copy-start | bytes 786436
  14.2 10.4 %collective-permute-start.1 = (f32[48,512]{1,0:T(8,128)}, f32[48,512]{1,0:T(8,128)}, u32[]{:S(2)}, u32[]{:S(2)}) collective-permute-start(f32[48,512]{1,0:T(8,128)} %get-tuple-element.25), channel_id=1, source_target_pairs={{0,1},{1,2},{2,3},{3,0},{4,5},{5,6},{6,7},{7,4},{8,9},{9,10},{10,1... | collective-permute-start | bytes 294920 | tf_op jit(solution)/shard_map/ppermute | solution.py:216
  15.5 10.3 %collective-permute-start.3 = (f32[48,512]{1,0:T(8,128)}, f32[48,512]{1,0:T(8,128)}, u32[]{:S(2)}, u32[]{:S(2)}) collective-permute-start(f32[48,512]{1,0:T(8,128)} %get-tuple-element.26), channel_id=1, source_target_pairs={{0,3},{1,0},{2,1},{3,2},{4,7},{5,4},{6,5},{7,6},{8,11},{9,8},{10,9... | collective-permute-start | bytes 294920 | tf_op jit(solution)/shard_map/ppermute | solution.py:216
  17.0 8.8 %collective-permute-start.2 = (f32[48,512]{1,0:T(8,128)}, f32[48,512]{1,0:T(8,128)}, u32[]{:S(2)}, u32[]{:S(2)}) collective-permute-start(f32[48,512]{1,0:T(8,128)} %get-tuple-element.27), channel_id=1, source_target_pairs={{0,2},{1,3},{2,0},{3,1},{4,6},{5,7},{6,4},{7,5},{8,10},{9,11},{10,... | collective-permute-start | bytes 294920 | tf_op jit(solution)/shard_map/ppermute | solution.py:216
  19.4 16.6 %copy-start.2 = (bf16[1024,256]{1,0:T(8,128)(2,1)}, bf16[1024,256]{1,0:T(8,128)(2,1)S(1)}, u32[]{:S(2)}) copy-start(bf16[1024,256]{1,0:T(8,128)(2,1)S(1)} %pad_maximum_fusion.refs_0_) | copy-start | bytes 1572868
  19.4 14.4 %collective-permute-start.5 = (bf16[1024,256]{1,0:T(8,128)(2,1)S(1)}, bf16[1024,256]{1,0:T(8,128)(2,1)}, u32[]{:S(2)}, u32[]{:S(2)}) collective-permute-start(bf16[1024,256]{1,0:T(8,128)(2,1)S(1)} %pad_maximum_fusion.refs_0_), channel_id=1, source_target_pairs={{0,96},{4,28},{8,104},{12,4},{16,112},{20,12},{24,120},{28,20},{32... | collective-permute-start | bytes 1572872 | tf_op jit(solution)/shard_map/ppermute | solution.py:223
  24.6 9.9 %collective-permute-start.8 = (bf16[1024,256]{1,0:T(8,128)(2,1)}, bf16[1024,256]{1,0:T(8,128)(2,1)}, u32[]{:S(2)}, u32[]{:S(2)}) collective-permute-start(bf16[1024,256]{1,0:T(8,128)(2,1)} %constant_dynamic-update-slice_fusion.refs_1_), channel_id=1, source_target_pairs={{0,32},{4,12},{8,40},{12,20},{16,48},{20,28},{24,56},{28,4},{32,64... | collective-permute-start | bytes 1572872 | tf_op jit(solution)/shard_map/ppermute | solution.py:223
  24.7 18.5 %collective-permute-start.12 = (bf16[1024,256]{1,0:T(8,128)(2,1)S(1)}, bf16[1024,256]{1,0:T(8,128)(2,1)}, u32[]{:S(2)}, u32[]{:S(2)}) collective-permute-start(bf16[1024,256]{1,0:T(8,128)(2,1)S(1)} %pad_maximum_fusion.refs_0_), channel_id=1, source_target_pairs={{0,32},{4,12},{8,40},{12,20},{16,48},{20,28},{24,56},{28,4},{32,64... | collective-permute-start | bytes 1572872 | tf_op jit(solution)/shard_map/ppermute | solution.py:223
  26.8 20.5 %copy-start.6 = (s32[8,1,16]{2,1,0:T(1,128)S(1)}, s32[8,1,16]{2,1,0:T(1,128)}, u32[]{:S(2)}) copy-start(s32[8,1,16]{2,1,0:T(1,128)} %param.15) | copy-start | bytes 1540
  34.5 8.7 %collective-permute-start.9 = (bf16[1024,256]{1,0:T(8,128)(2,1)}, bf16[1024,256]{1,0:T(8,128)(2,1)S(1)}, u32[]{:S(2)}, u32[]{:S(2)}) collective-permute-start(bf16[1024,256]{1,0:T(8,128)(2,1)} %collective-permute-done.5.refs_2_), channel_id=1, source_target_pairs={{0,96},{4,28},{8,104},{12,4},{16,112},{20,12},{24,120},{28,20},{32... | collective-permute-start | bytes 1572872 | tf_op jit(solution)/shard_map/ppermute | solution.py:223
  35.4 19.6 %collective-permute-start.10 = (bf16[1024,256]{1,0:T(8,128)(2,1)}, bf16[1024,256]{1,0:T(8,128)(2,1)S(1)}, u32[]{:S(2)}, u32[]{:S(2)}) collective-permute-start(bf16[1024,256]{1,0:T(8,128)(2,1)} %collective-permute-done.8.refs_7_), channel_id=1, source_target_pairs={{0,32},{4,12},{8,40},{12,20},{16,48},{20,28},{24,56},{28,4},{32,64... | collective-permute-start | bytes 1572872 | tf_op jit(solution)/shard_map/ppermute | solution.py:223
  36.0 19.1 %collective-permute-start.13 = (bf16[1024,256]{1,0:T(8,128)(2,1)S(1)}, bf16[1024,256]{1,0:T(8,128)(2,1)}, u32[]{:S(2)}, u32[]{:S(2)}) collective-permute-start(bf16[1024,256]{1,0:T(8,128)(2,1)S(1)} %pad_maximum_fusion.refs_0_), channel_id=1, source_target_pairs={{0,4},{4,0},{8,12},{12,8},{16,20},{20,16},{24,28},{28,24},{32,36},... | collective-permute-start | bytes 1572872 | tf_op jit(solution)/shard_map/ppermute | solution.py:223
  39.4 16.2 %collective-permute-start.11 = (bf16[1024,256]{1,0:T(8,128)(2,1)}, bf16[1024,256]{1,0:T(8,128)(2,1)}, u32[]{:S(2)}, u32[]{:S(2)}) collective-permute-start(bf16[1024,256]{1,0:T(8,128)(2,1)} %constant_dynamic-update-slice_fusion.refs_1_), channel_id=1, source_target_pairs={{0,96},{4,28},{8,104},{12,4},{16,112},{20,12},{24,120},{28,20},{32... | collective-permute-start | bytes 1572872 | tf_op jit(solution)/shard_map/ppermute | solution.py:223
  43.2 12.5 %collective-permute-start.14 = (bf16[1024,256]{1,0:T(8,128)(2,1)}, bf16[1024,256]{1,0:T(8,128)(2,1)}, u32[]{:S(2)}, u32[]{:S(2)}) collective-permute-start(bf16[1024,256]{1,0:T(8,128)(2,1)} %constant_dynamic-update-slice_fusion.refs_1_), channel_id=1, source_target_pairs={{0,4},{4,0},{8,12},{12,8},{16,20},{20,16},{24,28},{28,24},{32,36},... | collective-permute-start | bytes 1572872 | tf_op jit(solution)/shard_map/ppermute | solution.py:223
  43.2 12.5 %copy-start.8 = (bf16[1024,256]{1,0:T(8,128)(2,1)}, bf16[1024,256]{1,0:T(8,128)(2,1)S(1)}, u32[]{:S(2)}) copy-start(bf16[1024,256]{1,0:T(8,128)(2,1)S(1)} %collective-permute-done.9.refs_4_) | copy-start | bytes 1572868
  43.2 12.9 %collective-permute-start.19 = (bf16[1024,256]{1,0:T(8,128)(2,1)}, bf16[1024,256]{1,0:T(8,128)(2,1)}, u32[]{:S(2)}, u32[]{:S(2)}) collective-permute-start(bf16[1024,256]{1,0:T(8,128)(2,1)} %collective-permute-done.12.refs_6_), channel_id=1, source_target_pairs={{0,4},{4,0},{8,12},{12,8},{16,20},{20,16},{24,28},{28,24},{32,36},... | collective-permute-start | bytes 1572872 | tf_op jit(solution)/shard_map/ppermute | solution.py:223
  48.1 9.7 %copy-start.7 = (s32[128]{0:T(128)}, s32[128]{0:T(128)S(1)}, u32[]{:S(2)}) copy-start(s32[128]{0:T(128)S(1)} %reshape.127.pick_ref) | copy-start | bytes 1540
  48.1 8.3 %copy-start.4 = (f32[64,128]{1,0:T(8,128)S(1)}, f32[64,128]{1,0:T(8,128)}, u32[]{:S(2)}) copy-start(f32[64,128]{1,0:T(8,128)} %param.14) | copy-start | bytes 98308
  48.1 8.4 %copy-start.5 = (f32[64,128]{1,0:T(8,128)S(1)}, f32[64,128]{1,0:T(8,128)}, u32[]{:S(2)}) copy-start(f32[64,128]{1,0:T(8,128)} %param.13) | copy-start | bytes 98308
  55.0 5.4 %copy-start.9 = (bf16[1024,256]{1,0:T(8,128)(2,1)}, bf16[1024,256]{1,0:T(8,128)(2,1)S(1)}, u32[]{:S(2)}) copy-start(bf16[1024,256]{1,0:T(8,128)(2,1)S(1)} %collective-permute-done.10.refs_5_) | copy-start | bytes 1572868
  55.0 5.3 %collective-permute-start.15 = (bf16[1024,256]{1,0:T(8,128)(2,1)}, bf16[1024,256]{1,0:T(8,128)(2,1)}, u32[]{:S(2)}, u32[]{:S(2)}) collective-permute-start(bf16[1024,256]{1,0:T(8,128)(2,1)} %collective-permute-done.5.refs_2_), channel_id=1, source_target_pairs={{0,4},{4,0},{8,12},{12,8},{16,20},{20,16},{24,28},{28,24},{32,36},... | collective-permute-start | bytes 1572872 | tf_op jit(solution)/shard_map/ppermute | solution.py:223
  55.1 5.2 %collective-permute-start.20 = (bf16[1024,256]{1,0:T(8,128)(2,1)}, bf16[1024,256]{1,0:T(8,128)(2,1)}, u32[]{:S(2)}, u32[]{:S(2)}) collective-permute-start(bf16[1024,256]{1,0:T(8,128)(2,1)} %collective-permute-done.8.refs_7_), channel_id=1, source_target_pairs={{0,4},{4,0},{8,12},{12,8},{16,20},{20,16},{24,28},{28,24},{32,36},... | collective-permute-start | bytes 1572872 | tf_op jit(solution)/shard_map/ppermute | solution.py:223
  55.6 4.7 %collective-permute-start.16 = (bf16[1024,256]{1,0:T(8,128)(2,1)}, bf16[1024,256]{1,0:T(8,128)(2,1)}, u32[]{:S(2)}, u32[]{:S(2)}) collective-permute-start(bf16[1024,256]{1,0:T(8,128)(2,1)} %collective-permute-done.11.refs_3_), channel_id=1, source_target_pairs={{0,4},{4,0},{8,12},{12,8},{16,20},{20,16},{24,28},{28,24},{32,36},... | collective-permute-start | bytes 1572872 | tf_op jit(solution)/shard_map/ppermute | solution.py:223
  55.7 4.6 %collective-permute-start.17 = (bf16[1024,256]{1,0:T(8,128)(2,1)S(1)}, bf16[1024,256]{1,0:T(8,128)(2,1)}, u32[]{:S(2)}, u32[]{:S(2)}) collective-permute-start(bf16[1024,256]{1,0:T(8,128)(2,1)S(1)} %collective-permute-done.9.refs_4_), channel_id=1, source_target_pairs={{0,4},{4,0},{8,12},{12,8},{16,20},{20,16},{24,28},{28,24},{32,36},... | collective-permute-start | bytes 1572872 | tf_op jit(solution)/shard_map/ppermute | solution.py:223
  56.1 4.2 %collective-permute-start.18 = (bf16[1024,256]{1,0:T(8,128)(2,1)S(1)}, bf16[1024,256]{1,0:T(8,128)(2,1)}, u32[]{:S(2)}, u32[]{:S(2)}) collective-permute-start(bf16[1024,256]{1,0:T(8,128)(2,1)S(1)} %collective-permute-done.10.refs_5_), channel_id=1, source_target_pairs={{0,4},{4,0},{8,12},{12,8},{16,20},{20,16},{24,28},{28,24},{32,36},... | collective-permute-start | bytes 1572872 | tf_op jit(solution)/shard_map/ppermute | solution.py:223

commit v4 on v3

--- a/solution.py
+++ b/solution.py
@@ -14,6 +14,7 @@
 ROW_TILE = 256
 GROUP = 16
 NEAR_TOKENS = 128
+SAFE_RANGE = 2.0**60
 SIDE = 4
 CORES = 2
 NT = (((1,), (1,)), ((), ()))
@@ -52,31 +53,24 @@
     return jnp.where(token == lane, 1.0, 0.0).astype(BF16)
 
 
+def spread_of(total, inverse):
+    return jnp.max(jnp.maximum(total, inverse), axis=0, keepdims=True)
+
+
 def split(value):
     high = value.astype(BF16)
     return high, (value - high.astype(F32)).astype(BF16)
 
 
-def near_kernel(heads, first_step, index_ref, q_ref, previous_ref, own_ref, *refs):
-    win_ref, kv_ref, bias_ref = refs[-3:]
+def window_step(heads, rows_here, step, index_ref, q_ref, kv_ref, bias_ref, win_ref):
     head_dim = q_ref.shape[-1]
-    tokens = NEAR_TOKENS
-    rows = tokens * heads
-    rows_here = own_ref.shape[0]
-    step = pl.program_id(0) + first_step
+    rows = NEAR_TOKENS * heads
     factor = LOG2E / math.sqrt(head_dim)
-    span = WINDOW_TOKENS + tokens
-    lead = WINDOW_TOKENS
-
-    @pl.when(pl.program_id(0) == 0)
-    def _():
-        kv_ref[pl.ds(lead - rows_here, rows_here), :] = previous_ref[...]
-        kv_ref[pl.ds(lead, rows_here), :] = own_ref[...]
-
-    first = pl.multiple_of(step * tokens, tokens)
-    key = lax.broadcasted_iota(jnp.int32, (span, 128), 0) - lead
+    span = WINDOW_TOKENS + NEAR_TOKENS
+    first = pl.multiple_of(step * NEAR_TOKENS, NEAR_TOKENS)
+    key = lax.broadcasted_iota(jnp.int32, (span, 128), 0) - WINDOW_TOKENS
     tok = lax.broadcasted_iota(jnp.int32, (span, 128), 1)
-    start = index_ref[0] * rows_here + step * tokens
+    start = index_ref[0] * rows_here + step * NEAR_TOKENS
     seen = (key > tok - WINDOW_TOKENS) & (key <= tok) & (key + start >= 0)
     bias_ref[...] = jnp.where(seen, 0.0, MASKED).astype(BF16)
     keys = jnp.concatenate([kv_ref[pl.ds(first, span), :head_dim], bias_ref[...]], axis=1)
@@ -88,15 +82,38 @@
         q = jnp.concatenate([q_ref[pl.ds(at, ROW_TILE), :], token_one_hot(ROW_TILE, at, heads)], axis=1)
         return lax.dot_general(q, keys, NT, preferred_element_type=F32)
 
+    def finish(at, weights):
+        both = jnp.dot(weights.astype(BF16), values, preferred_element_type=F32)
+        inverse = 1.0 / both[:, head_dim:]
+        win_ref[pl.ds(at, ROW_TILE), :] = both[:, :head_dim] * inverse
+        return spread_of(both[:, head_dim:], inverse)
+
+    tiles = range(0, rows, ROW_TILE)
     ahead = score(0)
-    for at in range(0, rows, ROW_TILE):
+    range_seen = jnp.zeros((1, 128), F32)
+    for at in tiles:
         scores = ahead
         if at + ROW_TILE < rows:
             ahead = score(at + ROW_TILE)
-        peak = jnp.max(scores, axis=-1, keepdims=True)
-        weights = jnp.exp2(scores * factor - peak * factor).astype(BF16)
-        both = jnp.dot(weights, values, preferred_element_type=F32)
-        win_ref[pl.ds(at, ROW_TILE), :] = both[:, :head_dim] / both[:, head_dim:]
+        range_seen = jnp.maximum(range_seen, finish(at, jnp.exp2(scores * factor)))
+
+    @pl.when(jnp.logical_not(jnp.max(range_seen) < SAFE_RANGE))
+    def _():
+        for at in tiles:
+            scores = score(at)
+            peak = jnp.max(scores, axis=-1, keepdims=True)
+            finish(at, jnp.exp2((scores - peak) * factor))
+
+
+def near_kernel(heads, index_ref, q_ref, previous_ref, own_ref, win_ref, kv_ref, bias_ref):
+    rows_here = own_ref.shape[0]
+
+    @pl.when(pl.program_id(0) == 0)
+    def _():
+        kv_ref[pl.ds(0, rows_here), :] = previous_ref[...]
+        kv_ref[pl.ds(rows_here, rows_here), :] = own_ref[...]
+
+    window_step(heads, rows_here, pl.program_id(0), index_ref, q_ref, kv_ref, bias_ref, win_ref)
 
 
 def far_kernel(
@@ -135,9 +152,12 @@
             return carry
 
         each = GROUP * block_len
+        ready = 0
         for copy, piece, at in zip(copies, piece_refs, places):
             copy.wait()
-            lax.fori_loop(at // each, (at + piece.shape[0]) // each, compress, 0)
+            there = (at + piece.shape[0]) // each
+            lax.fori_loop(ready, there, compress, 0)
+            ready = there
 
     key = lax.broadcasted_iota(jnp.int32, (block_len, 128), 0)
     tok = lax.broadcasted_iota(jnp.int32, (block_len, 128), 1)
@@ -171,30 +191,47 @@
         comp = lax.dot_general(
             jnp.concatenate([q, q], axis=1), comp_keys, NT, preferred_element_type=F32
         )
-        return sel, comp
-
-    ahead = score(0)
-    for at in range(0, rows, ROW_TILE):
-        scores, comp_scores = ahead
-        if at + ROW_TILE < rows:
-            ahead = score(at + ROW_TILE)
-        peak = jnp.max(scores, axis=-1, keepdims=True)
-        weights = jnp.exp2(scores * factor - peak * factor).astype(BF16)
-        both = jnp.dot(weights, values_ref[...], preferred_element_type=F32)
-        sel = both[:, :head_dim] / both[:, head_dim:]
         token = (lax.broadcasted_iota(jnp.int32, (ROW_TILE, 1), 0) + at) // heads
         limit = own_block + jnp.where(token == block_len - 1, 1, 0)
-        scores = jnp.where(id_ref[...] < limit, comp_scores, MASKED)
-        peak = jnp.maximum(jnp.max(scores, axis=-1, keepdims=True), 0.0)
-        weights = jnp.exp2(scores * factor - peak * factor)
-        total = jnp.sum(weights, axis=-1, keepdims=True) + jnp.exp2(-peak * factor)
-        both = jnp.dot(weights.astype(BF16), comp_values, preferred_element_type=F32)
+        return sel, jnp.where(id_ref[...] < limit, comp, MASKED)
+
+    def finish(at, sel_weights, comp_weights, null_weight):
+        both = jnp.dot(sel_weights.astype(BF16), values_ref[...], preferred_element_type=F32)
+        inverse = 1.0 / both[:, head_dim:]
+        sel = both[:, :head_dim] * inverse
+        seen = spread_of(both[:, head_dim:], inverse)
+        total = jnp.sum(comp_weights, axis=-1, keepdims=True) + null_weight
+        both = jnp.dot(comp_weights.astype(BF16), comp_values, preferred_element_type=F32)
         merged = (
             spread(0, at) * ((both[:, :head_dim] + both[:, head_dim:]) / total)
             + spread(1, at) * sel
             + spread(2, at) * win_ref[pl.ds(at, ROW_TILE), :]
         )
         out_ref[pl.ds(at, ROW_TILE), :] = merged.astype(BF16)
+        return jnp.maximum(seen, jnp.max(total, axis=0, keepdims=True))
+
+    tiles = range(0, rows, ROW_TILE)
+    ahead = score(0)
+    range_seen = jnp.zeros((1, 128), F32)
+    for at in tiles:
+        sel_scores, comp_scores = ahead
+        if at + ROW_TILE < rows:
+            ahead = score(at + ROW_TILE)
+        seen = finish(at, jnp.exp2(sel_scores * factor), jnp.exp2(comp_scores * factor), 1.0)
+        range_seen = jnp.maximum(range_seen, seen)
+
+    @pl.when(jnp.logical_not(jnp.max(range_seen) < SAFE_RANGE))
+    def _():
+        for at in tiles:
+            sel_scores, comp_scores = score(at)
+            sel_peak = jnp.max(sel_scores, axis=-1, keepdims=True)
+            comp_peak = jnp.maximum(jnp.max(comp_scores, axis=-1, keepdims=True), 0.0)
+            finish(
+                at,
+                jnp.exp2((sel_scores - sel_peak) * factor),
+                jnp.exp2((comp_scores - comp_peak) * factor),
+                jnp.exp2(-comp_peak * factor),
+            )
 
 
 def partial_logits(hidden_in, gate_weight):
@@ -206,16 +243,15 @@
 def gate_logits(partial_value):
     parts = lax.axis_size("head")
     mine = lax.axis_index("head")
-    columns = partial_value.shape[0] // parts
-
-    def chunk(which):
-        return lax.dynamic_slice_in_dim(partial_value, lax.rem(which, parts) * columns, columns, 0)
-
-    total = chunk(mine)
-    for steps in range(1, parts):
-        total = total + lax.ppermute(
-            chunk(mine + steps), "head", [(n, (n + steps) % parts) for n in range(parts)]
-        )
+    total = partial_value
+    apart = parts // 2
+    while apart:
+        kept = lax.rem(mine // apart, 2)
+        half = total.shape[0] // 2
+        sent = lax.dynamic_slice_in_dim(total, (1 - kept) * half, half, 0)
+        got = lax.ppermute(sent, "head", [(n, n ^ apart) for n in range(parts)])
+        total = lax.dynamic_slice_in_dim(total, kept * half, half, 0) + got
+        apart //= 2
     return total
 
 
@@ -227,22 +263,20 @@
     ahead = send(key_value, perm=first_axis(-1))
     behind = send(key_value, perm=first_axis(1))
     across = send(key_value, perm=first_axis(2))
-    low = jnp.concatenate([key_value, ahead], axis=0)
-    high = jnp.concatenate([across, behind], axis=0)
-    return low, high
-
-
-def gather_pieces(low, high, first_work, second_work):
-    next_low = send(low, perm=second_axis(-1))
-    last_high = send(high, perm=second_axis(1))
-    next_high = send(high, perm=second_axis(-1))
-    last_low = send(low, perm=second_axis(1))
-    next_low, last_high, done = lax.optimization_barrier((next_low, last_high, first_work()))
-    far_low = send(next_low, perm=second_axis(-1))
-    far_high = send(last_high, perm=second_axis(1))
-    far_low, far_high, done = lax.optimization_barrier((far_low, far_high, second_work(done)))
-    mine = [low, high, next_low, next_high, far_low, far_high, last_low, last_high]
-    return mine + [send(piece, perm=other_core()) for piece in mine], done
+    return [key_value, ahead, across, behind]
+
+
+def gather_pieces(line, meanwhile, beside):
+    line = jnp.concatenate(line, axis=0)
+    next_line = send(line, perm=second_axis(-1))
+    last_line = send(line, perm=second_axis(1))
+    done = meanwhile()
+    next_line, last_line, again, done = lax.optimization_barrier((next_line, last_line, line, done))
+    across_line = send(again, perm=second_axis(2))
+    across_line, small = lax.optimization_barrier((across_line, beside(done)))
+    mine = [line, next_line, across_line, last_line]
+    pieces = mine + [send(piece, perm=other_core()) for piece in mine]
+    return pieces, [n * line.shape[0] for n in range(len(pieces))], small, done
 
 
 def row_of_block(block, index, blocks_here, block_len):
@@ -256,34 +290,33 @@
     return ((piece * SIDE + along) * blocks_here + block % blocks_here) * block_len
 
 
-def run_near(index, queries, previous, own, heads, first_step, steps, before=None):
+def run_near(index, queries, previous, own, heads):
     all_rows, head_dim = queries.shape
     rows_here = own.shape[0]
     whole = pl.BlockSpec((rows_here, 2 * head_dim), lambda b, *_: (0, 0))
-    tile = pl.BlockSpec((NEAR_TOKENS * heads, head_dim), lambda b, *_: (b + first_step, 0))
-    earlier = [] if before is None else [before]
+    tile = pl.BlockSpec((NEAR_TOKENS * heads, head_dim), lambda b, *_: (b, 0))
+    steps = rows_here // NEAR_TOKENS
     return pl.pallas_call(
-        functools.partial(near_kernel, heads, first_step),
+        functools.partial(near_kernel, heads),
         out_shape=pltpu.HBM((all_rows, head_dim), F32),
         grid_spec=pltpu.PrefetchScalarGridSpec(
             num_scalar_prefetch=1,
             grid=(steps,),
-            in_specs=[tile, whole, whole] + [pl.BlockSpec(memory_space=pl.ANY)] * len(earlier),
+            in_specs=[tile, whole, whole],
             out_specs=tile,
             scratch_shapes=[
                 pltpu.VMEM((rows_here + WINDOW_TOKENS, 2 * head_dim), BF16),
                 pltpu.VMEM((WINDOW_TOKENS + NEAR_TOKENS, 128), BF16),
             ],
         ),
-        input_output_aliases={4: 0} if earlier else {},
-        compiler_params=pltpu.CompilerParams(vmem_limit_bytes=56 << 20),
+        compiler_params=pltpu.CompilerParams(vmem_limit_bytes=24 << 20),
         cost_estimate=pl.CostEstimate(
-            flops=steps * 4 * NEAR_TOKENS * heads * head_dim * 1024,
-            transcendentals=steps * NEAR_TOKENS * heads * 640,
+            flops=steps * 8 * NEAR_TOKENS * heads * head_dim * 1024,
+            transcendentals=0,
             bytes_accessed=steps * NEAR_TOKENS * heads * head_dim * 6,
         ),
         name="near",
-    )(index, queries, previous, own, *earlier)
+    )(index, queries, previous, own)
 
 
 def run_far(chosen, source_rows, index, queries, logits, win, ids_by_slot, compress_w, pieces, places):
@@ -321,7 +354,10 @@
             flops=8 * all_rows * head_dim * 1280, transcendentals=all_rows * 1280, bytes_accessed=20 << 20
         ),
         name="far",
-    )(chosen, source_rows, index, queries, logits, win, ids_by_slot, compress_w, *[in_hbm(p) for p in pieces])
+    )(
+        chosen, source_rows, index, queries, logits, win, ids_by_slot, compress_w,
+        *[in_hbm(piece) for piece in pieces],
+    )
 
 
 def body(
@@ -343,11 +379,8 @@
     index = place_here.reshape(1)
 
     key_value = jnp.concatenate([encoded_keys, value_tensor], axis=-1).reshape(rows_here, 2 * head_dim)
-    low, high = gather_line(key_value)
+    line = gather_line(key_value)
     previous = send(key_value, perm=[(n, n + 1) for n in range(shard_parts - 1)])
-    previous, hidden_in = lax.optimization_barrier((previous, hidden_in))
-    logits = gate_logits(partial_logits(hidden_in, gate_weight))
-    previous, logits = lax.optimization_barrier((previous, logits))
     compress_w = jnp.concatenate([comp_key_weight, comp_value_weight], axis=-1)
     queries = in_hbm(encoded_queries.reshape(all_rows, head_dim))
     total_blocks = blocks_here * shard_parts
@@ -360,17 +393,16 @@
         jnp.where(placed[None, :] == slots[:, None], block_ids[None, :], 0), axis=1, dtype=jnp.int32
     ).reshape(1, total_blocks)
 
-    near_steps = rows_here // NEAR_TOKENS // 2
     near = functools.partial(run_near, index, queries, previous, key_value, heads_here)
-    pieces, win = gather_pieces(
-        low, high, lambda: near(0, near_steps), lambda done: near(near_steps, near_steps, done)
-    )
-    logits = logits.reshape(heads_here, 3, blocks_here, block_len).transpose(2, 1, 0, 3)
-
-    out = run_far(
-        chosen, source_rows, index, queries, logits, win, ids_by_slot, compress_w,
-        pieces, [n * low.shape[0] for n in range(len(pieces))],
-    )
+
+    def late_inputs(win):
+        after, _ = lax.optimization_barrier((hidden_in, win))
+        logits = gate_logits(partial_logits(after, gate_weight))
+        logits = logits.reshape(heads_here, 3, blocks_here, block_len).transpose(2, 1, 0, 3)
+        return chosen, source_rows, logits, ids_by_slot, compress_w
+
+    pieces, places, (picked, picked_rows, logits, slot_ids, weights), win = gather_pieces(line, near, late_inputs)
+    out = run_far(picked, picked_rows, index, queries, logits, win, slot_ids, weights, pieces, places)
     return out.reshape(rows_here, heads_here, head_dim)
 
 

time: 86.2 us -> 105 us (1.22)
  Pallas kernels: 39.2 us -> 60.6 us
  waiting for transfers between devices: 2.56 us -> 7.3 us
  local copies, waits for them, and re-layouts: 5.56 us -> 2.44 us
  starting transfers between devices: 31.6 us -> 29.8 us
  matrix products: 1.93 us -> 0.74 us
    pallas_call x1, Pallas kernels: 25.3 us -> 41.6 us  [run_far(): pl.pallas_call(functools.partial(far_kernel, block_len, heads, picks, pla...]
    pallas_call x2 -> x1, Pallas kernels: 13.8 us -> 19 us  [run_near(): pl.pallas_call(functools.partial(near_kernel, heads), out_shape=pltpu.HBM...]
    ppermute x3 -> x2, waiting for transfers between devices: 0.01 us -> 2.52 us  [gate_logits(): got = lax.ppermute(sent, 'head', [(n, n ^ apart) for n in range(parts)])]
    ppermute x18 -> x11, waiting for transfers between devices: 2.55 us -> 4.78 us  [send(): return lax.ppermute(value, 'ctx', perm)]
    concatenate x1 -> x0, local copies, waits for them, and re-layouts: 1.66 us -> none  [gather_line(): high = jnp.concatenate([across, behind], axis=0)]
    dot_general x1, matrix products: 1.93 us -> 0.74 us  [partial_logits(): lax.dot_general(gate_weight, hidden_in, (((0,), (1,)), ((), ())), preferr...]
    ppermute x18 -> x11, starting transfers between devices: 26.5 us -> 25.4 us  [send(): return lax.ppermute(value, 'ctx', perm)]
    unnamed x22 -> x17, local copies, waits for them, and re-layouts: 2.25 us -> 1.52 us
  transfers between devices with their start and end apart: 21 -> 13, of which waited for: 3 -> 6; matrix products, arithmetic and copies ran while one was open for 13% -> 5% of each run, Pallas kernels for 16% -> 18%
where the time goes in v4:
time: 105 us
  Pallas kernels  60.6 us (58%)
  starting transfers between devices  29.8 us (28%)
  waiting for transfers between devices  7.3 us (7%)
  other arithmetic  3.83 us (4%)
  local copies, waits for them, and re-layouts  2.44 us (2%)
    pallas_call x1, Pallas kernels, run_far(): pl.pallas_call(functools.partial(far_kernel, block_len, heads, picks, pla...  41.6 us
    ppermute x11, starting transfers between devices, send(): return lax.ppermute(value, 'ctx', perm)  25.4 us
    pallas_call x1, Pallas kernels, run_near(): pl.pallas_call(functools.partial(near_kernel, heads), out_shape=pltpu.HBM...  19 us
    ppermute x11, waiting for transfers between devices, send(): return lax.ppermute(value, 'ctx', perm)  4.78 us
    ppermute x2, starting transfers between devices, gate_logits(): got = lax.ppermute(sent, 'head', [(n, n ^ apart) for n in range(parts)])  4.36 us
    ppermute x2, waiting for transfers between devices, gate_logits(): got = lax.ppermute(sent, 'head', [(n, n ^ apart) for n in range(parts)])  2.52 us
  transfers between devices with their start and end apart: 13, of which 6 were waited for; matrix products, arithmetic and copies ran while one was open for 5% of the time, Pallas kernels for 18%

profile of v4, /device:TPU:1, one launch (start us, length us, event | category | flops | bytes accessed | tf_op | source)
XLA Modules:
  0.0 104.9 jit_solution(9247537071196405916)
XLA Ops:
  0.0 0.0 copy-start
  0.0 1.1 %maximum_bitcast_fusion.own_ref = bf16[512,256]{1,0:T(8,128)(2,1)S(1)} fusion(bf16[512,1,128]{2,0,1:T(8,128)(2,1)} %param.12, bf16[512,1,128]{2,0,1:T(8,128)(2,1)} %param.11), kind=kLoop, calls=%fused_computation.1 | loop fusion | flops 524288 | bytes 524288 | tf_op jit(solution)/shard_map/reshape | solution.py:381
  1.2 2.1 %collective-permute-start.2 = (bf16[512,256]{1,0:T(8,128)(2,1)S(1)}, bf16[512,256]{1,0:T(8,128)(2,1)S(1)}, u32[]{:S(2)}, u32[]{:S(2)}) collective-permute-start(bf16[512,256]{1,0:T(8,128)(2,1)S(1)} %maximum_bitcast_fusion.own_ref), channel_id=1, source_target_pairs={{0,8},{4,36},{8,16},{12,44},{16,24},{20,52},{24,0},{28,60},{32,40}... | collective-permute-start | bytes 786440 | tf_op jit(solution)/shard_map/ppermute | solution.py:259
  3.3 2.5 %collective-permute-start.1 = (bf16[512,256]{1,0:T(8,128)(2,1)S(1)}, bf16[512,256]{1,0:T(8,128)(2,1)S(1)}, u32[]{:S(2)}, u32[]{:S(2)}) collective-permute-start(bf16[512,256]{1,0:T(8,128)(2,1)S(1)} %maximum_bitcast_fusion.own_ref), channel_id=1, source_target_pairs={{0,16},{4,68},{8,24},{12,76},{16,0},{20,84},{24,8},{28,92},{32,48}... | collective-permute-start | bytes 786440 | tf_op jit(solution)/shard_map/ppermute | solution.py:259
  5.7 1.2 %collective-permute-start = (bf16[512,256]{1,0:T(8,128)(2,1)S(1)}, bf16[512,256]{1,0:T(8,128)(2,1)S(1)}, u32[]{:S(2)}, u32[]{:S(2)}) collective-permute-start(bf16[512,256]{1,0:T(8,128)(2,1)S(1)} %maximum_bitcast_fusion.own_ref), channel_id=1, source_target_pairs={{0,24},{4,100},{8,0},{12,108},{16,8},{20,116},{24,16},{28,124},{32... | collective-permute-start | bytes 786440 | tf_op jit(solution)/shard_map/ppermute | solution.py:259
  6.9 4.9 %collective-permute-start.5 = (bf16[512,256]{1,0:T(8,128)(2,1)S(1)}, bf16[512,256]{1,0:T(8,128)(2,1)S(1)}, u32[]{:S(2)}, u32[]{:S(2)}) collective-permute-start(bf16[512,256]{1,0:T(8,128)(2,1)S(1)} %maximum_bitcast_fusion.own_ref), channel_id=1, source_target_pairs={{0,4},{4,8},{8,12},{12,16},{16,20},{20,24},{24,28},{28,32},{32,36}... | collective-permute-start | bytes 786440 | tf_op jit(solution)/shard_map/ppermute | solution.py:259
  11.8 0.0 collective-permute-done.2
  11.8 0.8 collective-permute-done.1
  12.6 0.0 collective-permute-done
  12.6 0.1 pad_maximum_fusion.refs_0_
  12.7 0.0 copy-start.1
  12.7 1.4 %collective-permute-start.4 = (bf16[2048,256]{1,0:T(8,128)(2,1)S(1)}, bf16[2048,256]{1,0:T(8,128)(2,1)}, u32[]{:S(2)}, u32[]{:S(2)}) collective-permute-start(bf16[2048,256]{1,0:T(8,128)(2,1)S(1)} %pad_maximum_fusion.refs_0_), channel_id=1, source_target_pairs={{0,32},{4,12},{8,40},{12,20},{16,48},{20,28},{24,56},{28,4},{32,64... | collective-permute-start | bytes 3145736 | tf_op jit(solution)/shard_map/ppermute | solution.py:259
  14.1 2.2 %collective-permute-start.3 = (bf16[2048,256]{1,0:T(8,128)(2,1)S(1)}, bf16[2048,256]{1,0:T(8,128)(2,1)}, u32[]{:S(2)}, u32[]{:S(2)}) collective-permute-start(bf16[2048,256]{1,0:T(8,128)(2,1)S(1)} %pad_maximum_fusion.refs_0_), channel_id=1, source_target_pairs={{0,96},{4,28},{8,104},{12,4},{16,112},{20,12},{24,120},{28,20},{32... | collective-permute-start | bytes 3145736 | tf_op jit(solution)/shard_map/ppermute | solution.py:259
  16.3 0.5 broadcast.288
  16.8 0.0 copy-done.5
  16.8 0.7 reduce.3
  17.5 0.1 reshape.130.pick_ref
  17.6 0.7 select_reduce_fusion
  18.2 0.0 collective-permute-done.5.previous_ref
  18.2 19.0 %near.1.win_ref = f32[8192,128]{1,0:T(8,128)} custom-call(s32[1]{0:T(128)} %bitcast.1.index_ref, bf16[8192,128]{1,0:T(8,128)(2,1)} %bitcast.17, bf16[512,256]{1,0:T(8,128)(2,1)S(1)} %collective-permute-done.5.previous_ref, bf16[512,256]{1,0:T(8,128)(2,1)S(1)} %maximum_bitcast_fusion.own_ref), custom_call_target="tpu_custom_call" | custom-call | flops 8589934592 | bytes 6291456 | tf_op jit(solution)/shard_map/near/pallas_call | solution.py:299
  37.3 0.0 collective-permute-done.4.refs_3_
  37.3 0.0 collective-permute-done.3.refs_1_
  37.3 1.3 %collective-permute-start.6 = (bf16[2048,256]{1,0:T(8,128)(2,1)S(1)}, bf16[2048,256]{1,0:T(8,128)(2,1)}, u32[]{:S(2)}, u32[]{:S(2)}) collective-permute-start(bf16[2048,256]{1,0:T(8,128)(2,1)S(1)} %pad_maximum_fusion.refs_0_), channel_id=1, source_target_pairs={{0,64},{4,20},{8,72},{12,28},{16,80},{20,4},{24,88},{28,12},{32,96... | collective-permute-start | bytes 3145736 | tf_op jit(solution)/shard_map/ppermute | solution.py:259
  38.6 0.0 copy-done
  38.6 0.0 copy-done.2
  38.6 0.7 fusion.15
  39.4 3.0 %collective-permute-start.7 = (f32[96,512]{1,0:T(8,128)S(1)}, f32[96,512]{1,0:T(8,128)S(1)}, u32[]{:S(2)}, u32[]{:S(2)}) collective-permute-start(f32[96,512]{1,0:T(8,128)S(1)} %dynamic-slice_bitcast_fusion), channel_id=1, source_target_pairs={{0,2},{1,3},{2,0},{3,1},{4,6},{5,7},{6,4},{7,5},{8,10},{9,11},{10,... | collective-permute-start | bytes 589832 | tf_op jit(solution)/shard_map/ppermute | solution.py:252
  42.3 0.0 copy-done.6
  42.3 0.6 fusion.14.row_ref
  42.9 2.5 %collective-permute-done.7 = f32[96,512]{1,0:T(8,128)S(1)} collective-permute-done((f32[96,512]{1,0:T(8,128)S(1)}, f32[96,512]{1,0:T(8,128)S(1)}, u32[]{:S(2)}, u32[]{:S(2)}) %collective-permute-start.7) | collective-permute-done | bytes 196640 | tf_op jit(solution)/shard_map/ppermute | solution.py:252
  45.5 1.4 %collective-permute-start.8 = (f32[48,512]{1,0:T(8,128)S(1)}, f32[48,512]{1,0:T(8,128)S(1)}, u32[]{:S(2)}, u32[]{:S(2)}) collective-permute-start(f32[48,512]{1,0:T(8,128)S(1)} %constant_dynamic-slice_fusion), channel_id=1, source_target_pairs={{0,1},{1,0},{2,3},{3,2},{4,5},{5,4},{6,7},{7,6},{8,9},{9,8},{10,11... | collective-permute-start | bytes 294920 | tf_op jit(solution)/shard_map/ppermute | solution.py:252
  46.9 0.0 copy-done.4
  46.9 0.6 pad_maximum_fusion.1.weight_ref
  47.5 0.0 copy-done.1
  47.5 7.7 %collective-permute-start.9 = (bf16[2048,256]{1,0:T(8,128)(2,1)S(1)}, bf16[2048,256]{1,0:T(8,128)(2,1)}, u32[]{:S(2)}, u32[]{:S(2)}) collective-permute-start(bf16[2048,256]{1,0:T(8,128)(2,1)S(1)} %pad_maximum_fusion.refs_0_), channel_id=1, source_target_pairs={{0,4},{4,0},{8,12},{12,8},{16,20},{20,16},{24,28},{28,24},{32,36},... | collective-permute-start | bytes 3145736 | tf_op jit(solution)/shard_map/ppermute | solution.py:259
  55.2 0.0 collective-permute-start.10
  55.2 0.5 collective-permute-start.12
  55.7 0.0 collective-permute-done.8
  55.7 0.1 reshape.131
  55.8 0.7 copy.12
  56.5 0.0 collective-permute-done.6.refs_2_
  56.5 1.7 %collective-permute-start.11 = (bf16[2048,256]{1,0:T(8,128)(2,1)}, bf16[2048,256]{1,0:T(8,128)(2,1)S(1)}, u32[]{:S(2)}, u32[]{:S(2)}) collective-permute-start(bf16[2048,256]{1,0:T(8,128)(2,1)} %collective-permute-done.6.refs_2_), channel_id=1, source_target_pairs={{0,4},{4,0},{8,12},{12,8},{16,20},{20,16},{24,28},{28,24},{32,36},... | collective-permute-start | bytes 3145736 | tf_op jit(solution)/shard_map/ppermute | solution.py:259
  58.2 0.9 collective-permute-done.9.refs_4_
  59.1 0.2 collective-permute-done.10.refs_5_
  59.3 1.5 %collective-permute-done.12.refs_7_ = bf16[2048,256]{1,0:T(8,128)(2,1)} collective-permute-done((bf16[2048,256]{1,0:T(8,128)(2,1)}, bf16[2048,256]{1,0:T(8,128)(2,1)}, u32[]{:S(2)}, u32[]{:S(2)}) %collective-permute-start.12) | collective-permute-done | bytes 1048608 | tf_op jit(solution)/shard_map/ppermute | solution.py:259
  60.8 1.4 %collective-permute-done.11.refs_6_ = bf16[2048,256]{1,0:T(8,128)(2,1)S(1)} collective-permute-done((bf16[2048,256]{1,0:T(8,128)(2,1)}, bf16[2048,256]{1,0:T(8,128)(2,1)S(1)}, u32[]{:S(2)}, u32[]{:S(2)}) %collective-permute-start.11) | collective-permute-done | bytes 1048608 | tf_op jit(solution)/shard_map/ppermute | solution.py:259
  62.2 1.0 copy-done.7
  63.2 41.6 %far.1 = bf16[8192,128]{1,0:T(8,128)(2,1)} custom-call(s32[128]{0:T(128)} %copy-done.6, s32[128]{0:T(128)} %fusion.14.row_ref, s32[1]{0:T(128)} %bitcast.1.index_ref, bf16[8192,128]{1,0:T(8,128)(2,1)} %bitcast.18, f32[8,3,16,64]{3,2,1,0:T(8,128)} %bitcast.15, f32[8192,128]{1,0:T(8,128)} %near.1.win_ref, s32[1,256]{1,0:T(1,128)} %bitcast.16, ...), custom_call_target="tpu_custom_call" | custom-call | flops 10737418240 | bytes 20971520 | tf_op jit(solution)/shard_map/far/pallas_call | solution.py:329
  (12 shorter events, 0.1 us)
Async XLA Ops:
  0.0 38.6 %copy-start = (bf16[512,1792]{1,0:T(8,128)(2,1)S(1)}, bf16[512,1792]{1,0:T(8,128)(2,1)}, u32[]{:S(2)}) copy-start(bf16[512,1792]{1,0:T(8,128)(2,1)} %param.8) | copy-start | bytes 5505028
  0.0 16.8 %copy-start.5 = (s32[8,1,16]{2,1,0:T(1,128)S(1)}, s32[8,1,16]{2,1,0:T(1,128)}, u32[]{:S(2)}) copy-start(s32[8,1,16]{2,1,0:T(1,128)} %param.15) | copy-start | bytes 1540
  1.2 10.6 %collective-permute-start.2 = (bf16[512,256]{1,0:T(8,128)(2,1)S(1)}, bf16[512,256]{1,0:T(8,128)(2,1)S(1)}, u32[]{:S(2)}, u32[]{:S(2)}) collective-permute-start(bf16[512,256]{1,0:T(8,128)(2,1)S(1)} %maximum_bitcast_fusion.own_ref), channel_id=1, source_target_pairs={{0,8},{4,36},{8,16},{12,44},{16,24},{20,52},{24,0},{28,60},{32,40}... | collective-permute-start | bytes 786440 | tf_op jit(solution)/shard_map/ppermute | solution.py:259
  3.3 9.3 %collective-permute-start.1 = (bf16[512,256]{1,0:T(8,128)(2,1)S(1)}, bf16[512,256]{1,0:T(8,128)(2,1)S(1)}, u32[]{:S(2)}, u32[]{:S(2)}) collective-permute-start(bf16[512,256]{1,0:T(8,128)(2,1)S(1)} %maximum_bitcast_fusion.own_ref), channel_id=1, source_target_pairs={{0,16},{4,68},{8,24},{12,76},{16,0},{20,84},{24,8},{28,92},{32,48}... | collective-permute-start | bytes 786440 | tf_op jit(solution)/shard_map/ppermute | solution.py:259
  5.7 6.9 %collective-permute-start = (bf16[512,256]{1,0:T(8,128)(2,1)S(1)}, bf16[512,256]{1,0:T(8,128)(2,1)S(1)}, u32[]{:S(2)}, u32[]{:S(2)}) collective-permute-start(bf16[512,256]{1,0:T(8,128)(2,1)S(1)} %maximum_bitcast_fusion.own_ref), channel_id=1, source_target_pairs={{0,24},{4,100},{8,0},{12,108},{16,8},{20,116},{24,16},{28,124},{32... | collective-permute-start | bytes 786440 | tf_op jit(solution)/shard_map/ppermute | solution.py:259
  6.9 11.4 %collective-permute-start.5 = (bf16[512,256]{1,0:T(8,128)(2,1)S(1)}, bf16[512,256]{1,0:T(8,128)(2,1)S(1)}, u32[]{:S(2)}, u32[]{:S(2)}) collective-permute-start(bf16[512,256]{1,0:T(8,128)(2,1)S(1)} %maximum_bitcast_fusion.own_ref), channel_id=1, source_target_pairs={{0,4},{4,8},{8,12},{12,16},{16,20},{20,24},{24,28},{28,32},{32,36}... | collective-permute-start | bytes 786440 | tf_op jit(solution)/shard_map/ppermute | solution.py:259
  12.7 34.9 %copy-start.1 = (bf16[2048,256]{1,0:T(8,128)(2,1)}, bf16[2048,256]{1,0:T(8,128)(2,1)S(1)}, u32[]{:S(2)}) copy-start(bf16[2048,256]{1,0:T(8,128)(2,1)S(1)} %pad_maximum_fusion.refs_0_) | copy-start | bytes 3145732
  12.7 24.6 %collective-permute-start.4 = (bf16[2048,256]{1,0:T(8,128)(2,1)S(1)}, bf16[2048,256]{1,0:T(8,128)(2,1)}, u32[]{:S(2)}, u32[]{:S(2)}) collective-permute-start(bf16[2048,256]{1,0:T(8,128)(2,1)S(1)} %pad_maximum_fusion.refs_0_), channel_id=1, source_target_pairs={{0,32},{4,12},{8,40},{12,20},{16,48},{20,28},{24,56},{28,4},{32,64... | collective-permute-start | bytes 3145736 | tf_op jit(solution)/shard_map/ppermute | solution.py:259
  14.1 23.2 %collective-permute-start.3 = (bf16[2048,256]{1,0:T(8,128)(2,1)S(1)}, bf16[2048,256]{1,0:T(8,128)(2,1)}, u32[]{:S(2)}, u32[]{:S(2)}) collective-permute-start(bf16[2048,256]{1,0:T(8,128)(2,1)S(1)} %pad_maximum_fusion.refs_0_), channel_id=1, source_target_pairs={{0,96},{4,28},{8,104},{12,4},{16,112},{20,12},{24,120},{28,20},{32... | collective-permute-start | bytes 3145736 | tf_op jit(solution)/shard_map/ppermute | solution.py:259
  17.5 24.8 %copy-start.6 = (s32[128]{0:T(128)}, s32[128]{0:T(128)S(1)}, u32[]{:S(2)}) copy-start(s32[128]{0:T(128)S(1)} %reshape.130.pick_ref) | copy-start | bytes 1540
  18.2 20.3 %copy-start.2 = (bf16[1792,192]{0,1:T(8,128)(2,1)S(1)}, bf16[1792,192]{0,1:T(8,128)(2,1)}, u32[]{:S(2)}) copy-start(bf16[1792,192]{0,1:T(8,128)(2,1)} %param.9) | copy-start | bytes 2064388
  37.2 9.6 %copy-start.3 = (f32[64,128]{1,0:T(8,128)S(1)}, f32[64,128]{1,0:T(8,128)}, u32[]{:S(2)}) copy-start(f32[64,128]{1,0:T(8,128)} %param.14) | copy-start | bytes 98308
  37.2 9.6 %copy-start.4 = (f32[64,128]{1,0:T(8,128)S(1)}, f32[64,128]{1,0:T(8,128)}, u32[]{:S(2)}) copy-start(f32[64,128]{1,0:T(8,128)} %param.13) | copy-start | bytes 98308
  37.3 19.3 %collective-permute-start.6 = (bf16[2048,256]{1,0:T(8,128)(2,1)S(1)}, bf16[2048,256]{1,0:T(8,128)(2,1)}, u32[]{:S(2)}, u32[]{:S(2)}) collective-permute-start(bf16[2048,256]{1,0:T(8,128)(2,1)S(1)} %pad_maximum_fusion.refs_0_), channel_id=1, source_target_pairs={{0,64},{4,20},{8,72},{12,28},{16,80},{20,4},{24,88},{28,12},{32,96... | collective-permute-start | bytes 3145736 | tf_op jit(solution)/shard_map/ppermute | solution.py:259
  39.4 6.1 %collective-permute-start.7 = (f32[96,512]{1,0:T(8,128)S(1)}, f32[96,512]{1,0:T(8,128)S(1)}, u32[]{:S(2)}, u32[]{:S(2)}) collective-permute-start(f32[96,512]{1,0:T(8,128)S(1)} %dynamic-slice_bitcast_fusion), channel_id=1, source_target_pairs={{0,2},{1,3},{2,0},{3,1},{4,6},{5,7},{6,4},{7,5},{8,10},{9,11},{10,... | collective-permute-start | bytes 589832 | tf_op jit(solution)/shard_map/ppermute | solution.py:252
  45.5 10.2 %collective-permute-start.8 = (f32[48,512]{1,0:T(8,128)S(1)}, f32[48,512]{1,0:T(8,128)S(1)}, u32[]{:S(2)}, u32[]{:S(2)}) collective-permute-start(f32[48,512]{1,0:T(8,128)S(1)} %constant_dynamic-slice_fusion), channel_id=1, source_target_pairs={{0,1},{1,0},{2,3},{3,2},{4,5},{5,4},{6,7},{7,6},{8,9},{9,8},{10,11... | collective-permute-start | bytes 294920 | tf_op jit(solution)/shard_map/ppermute | solution.py:252
  47.5 11.6 %collective-permute-start.9 = (bf16[2048,256]{1,0:T(8,128)(2,1)S(1)}, bf16[2048,256]{1,0:T(8,128)(2,1)}, u32[]{:S(2)}, u32[]{:S(2)}) collective-permute-start(bf16[2048,256]{1,0:T(8,128)(2,1)S(1)} %pad_maximum_fusion.refs_0_), channel_id=1, source_target_pairs={{0,4},{4,0},{8,12},{12,8},{16,20},{20,16},{24,28},{28,24},{32,36},... | collective-permute-start | bytes 3145736 | tf_op jit(solution)/shard_map/ppermute | solution.py:259
  55.2 4.1 %collective-permute-start.10 = (bf16[2048,256]{1,0:T(8,128)(2,1)}, bf16[2048,256]{1,0:T(8,128)(2,1)}, u32[]{:S(2)}, u32[]{:S(2)}) collective-permute-start(bf16[2048,256]{1,0:T(8,128)(2,1)} %collective-permute-done.3.refs_1_), channel_id=1, source_target_pairs={{0,4},{4,0},{8,12},{12,8},{16,20},{20,16},{24,28},{28,24},{32,36},... | collective-permute-start | bytes 3145736 | tf_op jit(solution)/shard_map/ppermute | solution.py:259
  55.2 5.6 %collective-permute-start.12 = (bf16[2048,256]{1,0:T(8,128)(2,1)}, bf16[2048,256]{1,0:T(8,128)(2,1)}, u32[]{:S(2)}, u32[]{:S(2)}) collective-permute-start(bf16[2048,256]{1,0:T(8,128)(2,1)} %collective-permute-done.4.refs_3_), channel_id=1, source_target_pairs={{0,4},{4,0},{8,12},{12,8},{16,20},{20,16},{24,28},{28,24},{32,36},... | collective-permute-start | bytes 3145736 | tf_op jit(solution)/shard_map/ppermute | solution.py:259
  56.5 5.7 %collective-permute-start.11 = (bf16[2048,256]{1,0:T(8,128)(2,1)}, bf16[2048,256]{1,0:T(8,128)(2,1)S(1)}, u32[]{:S(2)}, u32[]{:S(2)}) collective-permute-start(bf16[2048,256]{1,0:T(8,128)(2,1)} %collective-permute-done.6.refs_2_), channel_id=1, source_target_pairs={{0,4},{4,0},{8,12},{12,8},{16,20},{20,16},{24,28},{28,24},{32,36},... | collective-permute-start | bytes 3145736 | tf_op jit(solution)/shard_map/ppermute | solution.py:259
  62.2 1.0 copy-start.7

commit v5 on v4

--- a/solution.py
+++ b/solution.py
@@ -349,14 +349,14 @@
                 pltpu.SemaphoreType.DMA((len(pieces),)),
             ],
         ),
-        compiler_params=pltpu.CompilerParams(vmem_limit_bytes=56 << 20),
+        compiler_params=pltpu.CompilerParams(vmem_limit_bytes=28 << 20),
         cost_estimate=pl.CostEstimate(
             flops=8 * all_rows * head_dim * 1280, transcendentals=all_rows * 1280, bytes_accessed=20 << 20
         ),
         name="far",
     )(
-        chosen, source_rows, index, queries, logits, win, ids_by_slot, compress_w,
-        *[in_hbm(piece) for piece in pieces],
+        chosen, source_rows, index, queries, logits, in_hbm(win), ids_by_slot, compress_w,
+        *pieces,
     )
 
 

time: 105 us -> 102 us (0.971)
  other arithmetic: 3.83 us -> 2.1 us
  local copies, waits for them, and re-layouts: 2.44 us -> 0.78 us
  starting transfers between devices: 29.8 us -> 30.9 us
    ppermute x11, starting transfers between devices: 25.4 us -> 26.5 us  [send(): return lax.ppermute(value, 'ctx', perm)]
  transfers between devices with their start and end apart: 13 -> 13, of which waited for: 6 -> 5; matrix products, arithmetic and copies ran while one was open for 5% -> 2% of each run, Pallas kernels for 18% -> 19%
where the time goes in v5:
time: 102 us
  Pallas kernels  60 us (59%)
  starting transfers between devices  30.9 us (30%)
  waiting for transfers between devices  7.48 us (7%)
  other arithmetic  2.1 us (2%)
    pallas_call x1, Pallas kernels, run_far(): pl.pallas_call(functools.partial(far_kernel, block_len, heads, picks, pla...  41 us
    ppermute x11, starting transfers between devices, send(): return lax.ppermute(value, 'ctx', perm)  26.5 us
    pallas_call x1, Pallas kernels, run_near(): pl.pallas_call(functools.partial(near_kernel, heads), out_shape=pltpu.HBM...  19 us
    ppermute x11, waiting for transfers between devices, send(): return lax.ppermute(value, 'ctx', perm)  4.4 us
    ppermute x2, starting transfers between devices, gate_logits(): got = lax.ppermute(sent, 'head', [(n, n ^ apart) for n in range(parts)])  4.37 us
    ppermute x2, waiting for transfers between devices, gate_logits(): got = lax.ppermute(sent, 'head', [(n, n ^ apart) for n in range(parts)])  3.08 us
  transfers between devices with their start and end apart: 13, of which 5 were waited for; matrix products, arithmetic and copies ran while one was open for 2% of the time, Pallas kernels for 19%

profile of v5, /device:TPU:1, one launch (start us, length us, event | category | flops | bytes accessed | tf_op | source)
XLA Modules:
  0.0 102.3 jit_solution(11420054789716461728)
XLA Ops:
  0.0 0.0 copy-start
  0.0 0.0 copy-start.4
  0.0 1.1 %maximum_bitcast_fusion.own_ref = bf16[512,256]{1,0:T(8,128)(2,1)S(1)} fusion(bf16[512,1,128]{2,0,1:T(8,128)(2,1)} %param.12, bf16[512,1,128]{2,0,1:T(8,128)(2,1)} %param.11), kind=kLoop, calls=%fused_computation.1 | loop fusion | flops 524288 | bytes 524288 | tf_op jit(solution)/shard_map/reshape | solution.py:381
  1.2 2.1 %collective-permute-start.2 = (bf16[512,256]{1,0:T(8,128)(2,1)S(1)}, bf16[512,256]{1,0:T(8,128)(2,1)S(1)}, u32[]{:S(2)}, u32[]{:S(2)}) collective-permute-start(bf16[512,256]{1,0:T(8,128)(2,1)S(1)} %maximum_bitcast_fusion.own_ref), channel_id=1, source_target_pairs={{0,8},{4,36},{8,16},{12,44},{16,24},{20,52},{24,0},{28,60},{32,40}... | collective-permute-start | bytes 786440 | tf_op jit(solution)/shard_map/ppermute | solution.py:259
  3.3 2.5 %collective-permute-start.1 = (bf16[512,256]{1,0:T(8,128)(2,1)S(1)}, bf16[512,256]{1,0:T(8,128)(2,1)S(1)}, u32[]{:S(2)}, u32[]{:S(2)}) collective-permute-start(bf16[512,256]{1,0:T(8,128)(2,1)S(1)} %maximum_bitcast_fusion.own_ref), channel_id=1, source_target_pairs={{0,16},{4,68},{8,24},{12,76},{16,0},{20,84},{24,8},{28,92},{32,48}... | collective-permute-start | bytes 786440 | tf_op jit(solution)/shard_map/ppermute | solution.py:259
  5.7 1.2 %collective-permute-start = (bf16[512,256]{1,0:T(8,128)(2,1)S(1)}, bf16[512,256]{1,0:T(8,128)(2,1)S(1)}, u32[]{:S(2)}, u32[]{:S(2)}) collective-permute-start(bf16[512,256]{1,0:T(8,128)(2,1)S(1)} %maximum_bitcast_fusion.own_ref), channel_id=1, source_target_pairs={{0,24},{4,100},{8,0},{12,108},{16,8},{20,116},{24,16},{28,124},{32... | collective-permute-start | bytes 786440 | tf_op jit(solution)/shard_map/ppermute | solution.py:259
  6.9 4.9 %collective-permute-start.5 = (bf16[512,256]{1,0:T(8,128)(2,1)S(1)}, bf16[512,256]{1,0:T(8,128)(2,1)S(1)}, u32[]{:S(2)}, u32[]{:S(2)}) collective-permute-start(bf16[512,256]{1,0:T(8,128)(2,1)S(1)} %maximum_bitcast_fusion.own_ref), channel_id=1, source_target_pairs={{0,4},{4,8},{8,12},{12,16},{16,20},{20,24},{24,28},{28,32},{32,36}... | collective-permute-start | bytes 786440 | tf_op jit(solution)/shard_map/ppermute | solution.py:259
  11.8 0.0 collective-permute-done.2
  11.8 0.8 collective-permute-done.1
  12.6 0.0 collective-permute-done
  12.6 0.1 pad_maximum_fusion.refs_0_
  12.7 1.4 %collective-permute-start.4 = (bf16[2048,256]{1,0:T(8,128)(2,1)S(1)}, bf16[2048,256]{1,0:T(8,128)(2,1)}, u32[]{:S(2)}, u32[]{:S(2)}) collective-permute-start(bf16[2048,256]{1,0:T(8,128)(2,1)S(1)} %pad_maximum_fusion.refs_0_), channel_id=1, source_target_pairs={{0,32},{4,12},{8,40},{12,20},{16,48},{20,28},{24,56},{28,4},{32,64... | collective-permute-start | bytes 3145736 | tf_op jit(solution)/shard_map/ppermute | solution.py:259
  14.1 2.2 %collective-permute-start.3 = (bf16[2048,256]{1,0:T(8,128)(2,1)S(1)}, bf16[2048,256]{1,0:T(8,128)(2,1)}, u32[]{:S(2)}, u32[]{:S(2)}) collective-permute-start(bf16[2048,256]{1,0:T(8,128)(2,1)S(1)} %pad_maximum_fusion.refs_0_), channel_id=1, source_target_pairs={{0,96},{4,28},{8,104},{12,4},{16,112},{20,12},{24,120},{28,20},{32... | collective-permute-start | bytes 3145736 | tf_op jit(solution)/shard_map/ppermute | solution.py:259
  16.3 0.5 broadcast.288
  16.8 0.0 copy-done.4
  16.8 0.7 reduce.3
  17.4 0.1 reshape.130.pick_ref
  17.6 0.1 select_reduce_fusion
  17.7 0.0 collective-permute-done.5.previous_ref
  17.7 0.0 copy-start.1
  17.7 19.0 %near.1.win_ref = f32[8192,128]{1,0:T(8,128)} custom-call(s32[1]{0:T(128)} %bitcast.1.index_ref, bf16[8192,128]{1,0:T(8,128)(2,1)} %bitcast.17, bf16[512,256]{1,0:T(8,128)(2,1)S(1)} %collective-permute-done.5.previous_ref, bf16[512,256]{1,0:T(8,128)(2,1)S(1)} %maximum_bitcast_fusion.own_ref), custom_call_target="tpu_custom_call" | custom-call | flops 8589934592 | bytes 6291456 | tf_op jit(solution)/shard_map/near/pallas_call | solution.py:299
  36.7 0.0 copy-start.2
  36.7 0.0 copy-start.3
  36.7 0.0 collective-permute-done.4.refs_3_
  36.7 0.0 collective-permute-done.3.refs_1_
  36.7 1.3 %collective-permute-start.6 = (bf16[2048,256]{1,0:T(8,128)(2,1)S(1)}, bf16[2048,256]{1,0:T(8,128)(2,1)}, u32[]{:S(2)}, u32[]{:S(2)}) collective-permute-start(bf16[2048,256]{1,0:T(8,128)(2,1)S(1)} %pad_maximum_fusion.refs_0_), channel_id=1, source_target_pairs={{0,64},{4,20},{8,72},{12,28},{16,80},{20,4},{24,88},{28,12},{32,96... | collective-permute-start | bytes 3145736 | tf_op jit(solution)/shard_map/ppermute | solution.py:259
  38.0 0.0 copy-done
  38.0 0.0 copy-done.1
  38.0 0.7 fusion.15
  38.8 3.0 %collective-permute-start.7 = (f32[96,512]{1,0:T(8,128)S(1)}, f32[96,512]{1,0:T(8,128)S(1)}, u32[]{:S(2)}, u32[]{:S(2)}) collective-permute-start(f32[96,512]{1,0:T(8,128)S(1)} %dynamic-slice_bitcast_fusion), channel_id=1, source_target_pairs={{0,2},{1,3},{2,0},{3,1},{4,6},{5,7},{6,4},{7,5},{8,10},{9,11},{10,... | collective-permute-start | bytes 589832 | tf_op jit(solution)/shard_map/ppermute | solution.py:252
  41.8 3.1 %collective-permute-done.7 = f32[96,512]{1,0:T(8,128)S(1)} collective-permute-done((f32[96,512]{1,0:T(8,128)S(1)}, f32[96,512]{1,0:T(8,128)S(1)}, u32[]{:S(2)}, u32[]{:S(2)}) %collective-permute-start.7) | collective-permute-done | bytes 196640 | tf_op jit(solution)/shard_map/ppermute | solution.py:252
  45.0 1.4 %collective-permute-start.8 = (f32[48,512]{1,0:T(8,128)S(1)}, f32[48,512]{1,0:T(8,128)S(1)}, u32[]{:S(2)}, u32[]{:S(2)}) collective-permute-start(f32[48,512]{1,0:T(8,128)S(1)} %constant_dynamic-slice_fusion), channel_id=1, source_target_pairs={{0,1},{1,0},{2,3},{3,2},{4,5},{5,4},{6,7},{7,6},{8,9},{9,8},{10,11... | collective-permute-start | bytes 294920 | tf_op jit(solution)/shard_map/ppermute | solution.py:252
  46.4 0.0 copy-done.2
  46.4 0.0 copy-done.3
  46.4 7.8 %collective-permute-start.9 = (bf16[2048,256]{1,0:T(8,128)(2,1)S(1)}, bf16[2048,256]{1,0:T(8,128)(2,1)}, u32[]{:S(2)}, u32[]{:S(2)}) collective-permute-start(bf16[2048,256]{1,0:T(8,128)(2,1)S(1)} %pad_maximum_fusion.refs_0_), channel_id=1, source_target_pairs={{0,4},{4,0},{8,12},{12,8},{16,20},{20,16},{24,28},{28,24},{32,36},... | collective-permute-start | bytes 3145736 | tf_op jit(solution)/shard_map/ppermute | solution.py:259
  54.1 0.1 collective-permute-start.10
  54.2 0.4 collective-permute-start.12
  54.6 0.0 collective-permute-done.8
  54.7 0.1 reshape.131
  54.8 0.0 collective-permute-done.6.refs_2_
  54.8 2.7 %collective-permute-start.11 = (bf16[2048,256]{1,0:T(8,128)(2,1)}, bf16[2048,256]{1,0:T(8,128)(2,1)S(1)}, u32[]{:S(2)}, u32[]{:S(2)}) collective-permute-start(bf16[2048,256]{1,0:T(8,128)(2,1)} %collective-permute-done.6.refs_2_), channel_id=1, source_target_pairs={{0,4},{4,0},{8,12},{12,8},{16,20},{20,16},{24,28},{28,24},{32,36},... | collective-permute-start | bytes 3145736 | tf_op jit(solution)/shard_map/ppermute | solution.py:259
  57.5 0.0 collective-permute-done.9.refs_4_
  57.6 0.7 collective-permute-done.10.refs_5_
  58.3 1.5 %collective-permute-done.12.refs_7_ = bf16[2048,256]{1,0:T(8,128)(2,1)} collective-permute-done((bf16[2048,256]{1,0:T(8,128)(2,1)}, bf16[2048,256]{1,0:T(8,128)(2,1)}, u32[]{:S(2)}, u32[]{:S(2)}) %collective-permute-start.12) | collective-permute-done | bytes 1048608 | tf_op jit(solution)/shard_map/ppermute | solution.py:259
  59.8 1.4 %collective-permute-done.11.refs_6_ = bf16[2048,256]{1,0:T(8,128)(2,1)S(1)} collective-permute-done((bf16[2048,256]{1,0:T(8,128)(2,1)}, bf16[2048,256]{1,0:T(8,128)(2,1)S(1)}, u32[]{:S(2)}, u32[]{:S(2)}) %collective-permute-start.11) | collective-permute-done | bytes 1048608 | tf_op jit(solution)/shard_map/ppermute | solution.py:259
  61.1 41.0 %far.1 = bf16[8192,128]{1,0:T(8,128)(2,1)} custom-call(s32[128]{0:T(128)S(1)} %reshape.130.pick_ref, s32[128]{0:T(128)S(1)} %fusion.14.row_ref, s32[1]{0:T(128)} %bitcast.1.index_ref, bf16[8192,128]{1,0:T(8,128)(2,1)} %bitcast.18, f32[8,3,16,64]{3,2,1,0:T(8,128)S(1)} %bitcast.15, f32[8192,128]{1,0:T(8,128)} %near.1.win_ref, s32[1,256]{1,0:T(1,128)S(1)} %bitcast.16, ...), custom_call_target="tpu_custom_call" | custom-call | flops 10737418240 | bytes 20971520 | tf_op jit(solution)/shard_map/far/pallas_call | solution.py:329
  (8 shorter events, 0.2 us)
Async XLA Ops:
  0.0 38.0 %copy-start = (bf16[512,1792]{1,0:T(8,128)(2,1)S(1)}, bf16[512,1792]{1,0:T(8,128)(2,1)}, u32[]{:S(2)}) copy-start(bf16[512,1792]{1,0:T(8,128)(2,1)} %param.8) | copy-start | bytes 5505028
  0.0 16.8 %copy-start.4 = (s32[8,1,16]{2,1,0:T(1,128)S(1)}, s32[8,1,16]{2,1,0:T(1,128)}, u32[]{:S(2)}) copy-start(s32[8,1,16]{2,1,0:T(1,128)} %param.15) | copy-start | bytes 1540
  1.2 10.6 %collective-permute-start.2 = (bf16[512,256]{1,0:T(8,128)(2,1)S(1)}, bf16[512,256]{1,0:T(8,128)(2,1)S(1)}, u32[]{:S(2)}, u32[]{:S(2)}) collective-permute-start(bf16[512,256]{1,0:T(8,128)(2,1)S(1)} %maximum_bitcast_fusion.own_ref), channel_id=1, source_target_pairs={{0,8},{4,36},{8,16},{12,44},{16,24},{20,52},{24,0},{28,60},{32,40}... | collective-permute-start | bytes 786440 | tf_op jit(solution)/shard_map/ppermute | solution.py:259
  3.3 9.3 %collective-permute-start.1 = (bf16[512,256]{1,0:T(8,128)(2,1)S(1)}, bf16[512,256]{1,0:T(8,128)(2,1)S(1)}, u32[]{:S(2)}, u32[]{:S(2)}) collective-permute-start(bf16[512,256]{1,0:T(8,128)(2,1)S(1)} %maximum_bitcast_fusion.own_ref), channel_id=1, source_target_pairs={{0,16},{4,68},{8,24},{12,76},{16,0},{20,84},{24,8},{28,92},{32,48}... | collective-permute-start | bytes 786440 | tf_op jit(solution)/shard_map/ppermute | solution.py:259
  5.7 6.9 %collective-permute-start = (bf16[512,256]{1,0:T(8,128)(2,1)S(1)}, bf16[512,256]{1,0:T(8,128)(2,1)S(1)}, u32[]{:S(2)}, u32[]{:S(2)}) collective-permute-start(bf16[512,256]{1,0:T(8,128)(2,1)S(1)} %maximum_bitcast_fusion.own_ref), channel_id=1, source_target_pairs={{0,24},{4,100},{8,0},{12,108},{16,8},{20,116},{24,16},{28,124},{32... | collective-permute-start | bytes 786440 | tf_op jit(solution)/shard_map/ppermute | solution.py:259
  6.9 10.8 %collective-permute-start.5 = (bf16[512,256]{1,0:T(8,128)(2,1)S(1)}, bf16[512,256]{1,0:T(8,128)(2,1)S(1)}, u32[]{:S(2)}, u32[]{:S(2)}) collective-permute-start(bf16[512,256]{1,0:T(8,128)(2,1)S(1)} %maximum_bitcast_fusion.own_ref), channel_id=1, source_target_pairs={{0,4},{4,8},{8,12},{12,16},{16,20},{20,24},{24,28},{28,32},{32,36}... | collective-permute-start | bytes 786440 | tf_op jit(solution)/shard_map/ppermute | solution.py:259
  12.7 24.1 %collective-permute-start.4 = (bf16[2048,256]{1,0:T(8,128)(2,1)S(1)}, bf16[2048,256]{1,0:T(8,128)(2,1)}, u32[]{:S(2)}, u32[]{:S(2)}) collective-permute-start(bf16[2048,256]{1,0:T(8,128)(2,1)S(1)} %pad_maximum_fusion.refs_0_), channel_id=1, source_target_pairs={{0,32},{4,12},{8,40},{12,20},{16,48},{20,28},{24,56},{28,4},{32,64... | collective-permute-start | bytes 3145736 | tf_op jit(solution)/shard_map/ppermute | solution.py:259
  14.1 22.7 %collective-permute-start.3 = (bf16[2048,256]{1,0:T(8,128)(2,1)S(1)}, bf16[2048,256]{1,0:T(8,128)(2,1)}, u32[]{:S(2)}, u32[]{:S(2)}) collective-permute-start(bf16[2048,256]{1,0:T(8,128)(2,1)S(1)} %pad_maximum_fusion.refs_0_), channel_id=1, source_target_pairs={{0,96},{4,28},{8,104},{12,4},{16,112},{20,12},{24,120},{28,20},{32... | collective-permute-start | bytes 3145736 | tf_op jit(solution)/shard_map/ppermute | solution.py:259
  17.7 20.4 %copy-start.1 = (bf16[1792,192]{0,1:T(8,128)(2,1)S(1)}, bf16[1792,192]{0,1:T(8,128)(2,1)}, u32[]{:S(2)}) copy-start(bf16[1792,192]{0,1:T(8,128)(2,1)} %param.9) | copy-start | bytes 2064388
  36.7 9.6 %copy-start.2 = (f32[64,128]{1,0:T(8,128)S(1)}, f32[64,128]{1,0:T(8,128)}, u32[]{:S(2)}) copy-start(f32[64,128]{1,0:T(8,128)} %param.14) | copy-start | bytes 98308
  36.7 9.6 %copy-start.3 = (f32[64,128]{1,0:T(8,128)S(1)}, f32[64,128]{1,0:T(8,128)}, u32[]{:S(2)}) copy-start(f32[64,128]{1,0:T(8,128)} %param.13) | copy-start | bytes 98308
  36.7 18.1 %collective-permute-start.6 = (bf16[2048,256]{1,0:T(8,128)(2,1)S(1)}, bf16[2048,256]{1,0:T(8,128)(2,1)}, u32[]{:S(2)}, u32[]{:S(2)}) collective-permute-start(bf16[2048,256]{1,0:T(8,128)(2,1)S(1)} %pad_maximum_fusion.refs_0_), channel_id=1, source_target_pairs={{0,64},{4,20},{8,72},{12,28},{16,80},{20,4},{24,88},{28,12},{32,96... | collective-permute-start | bytes 3145736 | tf_op jit(solution)/shard_map/ppermute | solution.py:259
  38.8 6.1 %collective-permute-start.7 = (f32[96,512]{1,0:T(8,128)S(1)}, f32[96,512]{1,0:T(8,128)S(1)}, u32[]{:S(2)}, u32[]{:S(2)}) collective-permute-start(f32[96,512]{1,0:T(8,128)S(1)} %dynamic-slice_bitcast_fusion), channel_id=1, source_target_pairs={{0,2},{1,3},{2,0},{3,1},{4,6},{5,7},{6,4},{7,5},{8,10},{9,11},{10,... | collective-permute-start | bytes 589832 | tf_op jit(solution)/shard_map/ppermute | solution.py:252
  45.0 9.7 %collective-permute-start.8 = (f32[48,512]{1,0:T(8,128)S(1)}, f32[48,512]{1,0:T(8,128)S(1)}, u32[]{:S(2)}, u32[]{:S(2)}) collective-permute-start(f32[48,512]{1,0:T(8,128)S(1)} %constant_dynamic-slice_fusion), channel_id=1, source_target_pairs={{0,1},{1,0},{2,3},{3,2},{4,5},{5,4},{6,7},{7,6},{8,9},{9,8},{10,11... | collective-permute-start | bytes 294920 | tf_op jit(solution)/shard_map/ppermute | solution.py:252
  46.4 11.2 %collective-permute-start.9 = (bf16[2048,256]{1,0:T(8,128)(2,1)S(1)}, bf16[2048,256]{1,0:T(8,128)(2,1)}, u32[]{:S(2)}, u32[]{:S(2)}) collective-permute-start(bf16[2048,256]{1,0:T(8,128)(2,1)S(1)} %pad_maximum_fusion.refs_0_), channel_id=1, source_target_pairs={{0,4},{4,0},{8,12},{12,8},{16,20},{20,16},{24,28},{28,24},{32,36},... | collective-permute-start | bytes 3145736 | tf_op jit(solution)/shard_map/ppermute | solution.py:259
  54.1 4.1 %collective-permute-start.10 = (bf16[2048,256]{1,0:T(8,128)(2,1)}, bf16[2048,256]{1,0:T(8,128)(2,1)}, u32[]{:S(2)}, u32[]{:S(2)}) collective-permute-start(bf16[2048,256]{1,0:T(8,128)(2,1)} %collective-permute-done.3.refs_1_), channel_id=1, source_target_pairs={{0,4},{4,0},{8,12},{12,8},{16,20},{20,16},{24,28},{28,24},{32,36},... | collective-permute-start | bytes 3145736 | tf_op jit(solution)/shard_map/ppermute | solution.py:259
  54.2 5.5 %collective-permute-start.12 = (bf16[2048,256]{1,0:T(8,128)(2,1)}, bf16[2048,256]{1,0:T(8,128)(2,1)}, u32[]{:S(2)}, u32[]{:S(2)}) collective-permute-start(bf16[2048,256]{1,0:T(8,128)(2,1)} %collective-permute-done.4.refs_3_), channel_id=1, source_target_pairs={{0,4},{4,0},{8,12},{12,8},{16,20},{20,16},{24,28},{28,24},{32,36},... | collective-permute-start | bytes 3145736 | tf_op jit(solution)/shard_map/ppermute | solution.py:259
  54.8 6.3 %collective-permute-start.11 = (bf16[2048,256]{1,0:T(8,128)(2,1)}, bf16[2048,256]{1,0:T(8,128)(2,1)S(1)}, u32[]{:S(2)}, u32[]{:S(2)}) collective-permute-start(bf16[2048,256]{1,0:T(8,128)(2,1)} %collective-permute-done.6.refs_2_), channel_id=1, source_target_pairs={{0,4},{4,0},{8,12},{12,8},{16,20},{20,16},{24,28},{28,24},{32,36},... | collective-permute-start | bytes 3145736 | tf_op jit(solution)/shard_map/ppermute | solution.py:259

commit v6 on v5

--- a/solution.py
+++ b/solution.py
@@ -11,7 +11,7 @@
 WINDOW_TOKENS = 512
 MASKED = -1e30
 LOG2E = 1.4426950408889634
-ROW_TILE = 256
+ROW_TILE = 512
 GROUP = 16
 NEAR_TOKENS = 128
 SAFE_RANGE = 2.0**60
@@ -243,16 +243,17 @@
 def gate_logits(partial_value):
     parts = lax.axis_size("head")
     mine = lax.axis_index("head")
-    total = partial_value
-    apart = parts // 2
-    while apart:
-        kept = lax.rem(mine // apart, 2)
-        half = total.shape[0] // 2
-        sent = lax.dynamic_slice_in_dim(total, (1 - kept) * half, half, 0)
-        got = lax.ppermute(sent, "head", [(n, n ^ apart) for n in range(parts)])
-        total = lax.dynamic_slice_in_dim(total, kept * half, half, 0) + got
-        apart //= 2
-    return total
+    columns = partial_value.shape[0] // parts
+
+    def chunk(which):
+        return lax.dynamic_slice_in_dim(partial_value, lax.rem(which, parts) * columns, columns, 0)
+
+    others = [
+        lax.ppermute(chunk(mine + steps), "head", [(n, (n + steps) % parts) for n in range(parts)])
+        for steps in range(1, parts)
+    ]
+    others = lax.optimization_barrier(others)
+    return chunk(mine) + others[0] + others[1] + others[2]
 
 
 def send(value, perm):

time: 102 us -> 98.1 us (0.962)
  waiting for transfers between devices: 7.48 us -> 3.32 us
  Pallas kernels: 60 us -> 58.1 us
  matrix products: 0.74 us -> 1.84 us
    ppermute x2 -> x3, waiting for transfers between devices: 3.08 us -> 0.01 us  [gate_logits(): lax.ppermute(chunk(mine + steps), 'head', [(n, (n + steps) % parts) for n...]
    pallas_call x1, Pallas kernels: 41 us -> 38.2 us  [run_far(): pl.pallas_call(functools.partial(far_kernel, block_len, heads, picks, pla...]
    ppermute x11, starting transfers between devices: 26.5 us -> 27.6 us  [send(): return lax.ppermute(value, 'ctx', perm)]
    dot_general x1, matrix products: 0.74 us -> 1.84 us  [partial_logits(): lax.dot_general(gate_weight, hidden_in, (((0,), (1,)), ((), ())), preferr...]
    ppermute x11, waiting for transfers between devices: 4.4 us -> 3.31 us  [send(): return lax.ppermute(value, 'ctx', perm)]
    ppermute x2 -> x3, starting transfers between devices: 4.37 us -> 3.85 us  [gate_logits(): lax.ppermute(chunk(mine + steps), 'head', [(n, (n + steps) % parts) for n...]
  transfers between devices with their start and end apart: 13 -> 14, of which waited for: 5 -> 3; matrix products, arithmetic and copies ran while one was open for 2% -> 4% of each run, Pallas kernels for 19% -> 20%
where the time goes in v6:
time: 98.1 us; the launch traced here: 97.9 us
  Pallas kernels  58.1 us (59%)
  starting transfers between devices  31.5 us (32%)
  waiting for transfers between devices  3.32 us (3%)
  other arithmetic  2.08 us (2%)
  matrix products  1.84 us (2%)
    pallas_call x1, Pallas kernels, run_far(): pl.pallas_call(functools.partial(far_kernel, block_len, heads, picks, pla...  38.2 us
    ppermute x11, starting transfers between devices, send(): return lax.ppermute(value, 'ctx', perm)  27.6 us
    pallas_call x1, Pallas kernels, run_near(): pl.pallas_call(functools.partial(near_kernel, heads), out_shape=pltpu.HBM...  19.9 us
    ppermute x3, starting transfers between devices, gate_logits(): lax.ppermute(chunk(mine + steps), 'head', [(n, (n + steps) % parts) for n...  3.85 us
    ppermute x11, waiting for transfers between devices, send(): return lax.ppermute(value, 'ctx', perm)  3.31 us
  transfers between devices with their start and end apart: 14, of which 3 were waited for; matrix products, arithmetic and copies ran while one was open for 4% of the time, Pallas kernels for 20%

profile of v6, /device:TPU:1, one launch (start us, length us, event | category | flops | bytes accessed | tf_op | source)
XLA Modules:
  0.0 97.9 jit_solution(16327109931355956551)
XLA Ops:
  0.0 0.0 copy-start
  0.0 1.1 %maximum_bitcast_fusion.own_ref = bf16[512,256]{1,0:T(8,128)(2,1)S(1)} fusion(bf16[512,1,128]{2,0,1:T(8,128)(2,1)} %param.12, bf16[512,1,128]{2,0,1:T(8,128)(2,1)} %param.11), kind=kLoop, calls=%fused_computation.1 | loop fusion | flops 524288 | bytes 524288 | tf_op jit(solution)/shard_map/reshape | solution.py:382
  1.1 2.1 %collective-permute-start.2 = (bf16[512,256]{1,0:T(8,128)(2,1)S(1)}, bf16[512,256]{1,0:T(8,128)(2,1)S(1)}, u32[]{:S(2)}, u32[]{:S(2)}) collective-permute-start(bf16[512,256]{1,0:T(8,128)(2,1)S(1)} %maximum_bitcast_fusion.own_ref), channel_id=1, source_target_pairs={{0,8},{4,36},{8,16},{12,44},{16,24},{20,52},{24,0},{28,60},{32,40}... | collective-permute-start | bytes 786440 | tf_op jit(solution)/shard_map/ppermute | solution.py:260
  3.2 2.5 %collective-permute-start.1 = (bf16[512,256]{1,0:T(8,128)(2,1)S(1)}, bf16[512,256]{1,0:T(8,128)(2,1)S(1)}, u32[]{:S(2)}, u32[]{:S(2)}) collective-permute-start(bf16[512,256]{1,0:T(8,128)(2,1)S(1)} %maximum_bitcast_fusion.own_ref), channel_id=1, source_target_pairs={{0,16},{4,68},{8,24},{12,76},{16,0},{20,84},{24,8},{28,92},{32,48}... | collective-permute-start | bytes 786440 | tf_op jit(solution)/shard_map/ppermute | solution.py:260
  5.7 1.2 %collective-permute-start = (bf16[512,256]{1,0:T(8,128)(2,1)S(1)}, bf16[512,256]{1,0:T(8,128)(2,1)S(1)}, u32[]{:S(2)}, u32[]{:S(2)}) collective-permute-start(bf16[512,256]{1,0:T(8,128)(2,1)S(1)} %maximum_bitcast_fusion.own_ref), channel_id=1, source_target_pairs={{0,24},{4,100},{8,0},{12,108},{16,8},{20,116},{24,16},{28,124},{32... | collective-permute-start | bytes 786440 | tf_op jit(solution)/shard_map/ppermute | solution.py:260
  6.9 4.9 %collective-permute-start.5 = (bf16[512,256]{1,0:T(8,128)(2,1)S(1)}, bf16[512,256]{1,0:T(8,128)(2,1)S(1)}, u32[]{:S(2)}, u32[]{:S(2)}) collective-permute-start(bf16[512,256]{1,0:T(8,128)(2,1)S(1)} %maximum_bitcast_fusion.own_ref), channel_id=1, source_target_pairs={{0,4},{4,8},{8,12},{12,16},{16,20},{20,24},{24,28},{28,32},{32,36}... | collective-permute-start | bytes 786440 | tf_op jit(solution)/shard_map/ppermute | solution.py:260
  11.7 0.0 collective-permute-done.2
  11.8 0.8 collective-permute-done.1
  12.6 0.0 collective-permute-done
  12.6 0.1 pad_maximum_fusion.refs_0_
  12.6 1.4 %collective-permute-start.4 = (bf16[2048,256]{1,0:T(8,128)(2,1)S(1)}, bf16[2048,256]{1,0:T(8,128)(2,1)}, u32[]{:S(2)}, u32[]{:S(2)}) collective-permute-start(bf16[2048,256]{1,0:T(8,128)(2,1)S(1)} %pad_maximum_fusion.refs_0_), channel_id=1, source_target_pairs={{0,32},{4,12},{8,40},{12,20},{16,48},{20,28},{24,56},{28,4},{32,64... | collective-permute-start | bytes 3145736 | tf_op jit(solution)/shard_map/ppermute | solution.py:260
  14.0 2.2 %collective-permute-start.3 = (bf16[2048,256]{1,0:T(8,128)(2,1)S(1)}, bf16[2048,256]{1,0:T(8,128)(2,1)}, u32[]{:S(2)}, u32[]{:S(2)}) collective-permute-start(bf16[2048,256]{1,0:T(8,128)(2,1)S(1)} %pad_maximum_fusion.refs_0_), channel_id=1, source_target_pairs={{0,96},{4,28},{8,104},{12,4},{16,112},{20,12},{24,120},{28,20},{32... | collective-permute-start | bytes 3145736 | tf_op jit(solution)/shard_map/ppermute | solution.py:260
  16.3 0.0 collective-permute-done.5.previous_ref
  16.3 0.0 copy-start.3
  16.3 19.9 %near.1.win_ref = f32[8192,128]{1,0:T(8,128)} custom-call(s32[1]{0:T(128)} %bitcast.1.index_ref, bf16[8192,128]{1,0:T(8,128)(2,1)} %bitcast.25, bf16[512,256]{1,0:T(8,128)(2,1)S(1)} %collective-permute-done.5.previous_ref, bf16[512,256]{1,0:T(8,128)(2,1)S(1)} %maximum_bitcast_fusion.own_ref), custom_call_target="tpu_custom_call" | custom-call | flops 8589934592 | bytes 6291456 | tf_op jit(solution)/shard_map/near/pallas_call | solution.py:300
  36.2 0.0 copy-start.1
  36.2 0.0 copy-start.2
  36.2 0.0 collective-permute-done.4.refs_3_
  36.2 0.0 collective-permute-done.3.refs_1_
  36.2 1.3 %collective-permute-start.6 = (bf16[2048,256]{1,0:T(8,128)(2,1)S(1)}, bf16[2048,256]{1,0:T(8,128)(2,1)}, u32[]{:S(2)}, u32[]{:S(2)}) collective-permute-start(bf16[2048,256]{1,0:T(8,128)(2,1)S(1)} %pad_maximum_fusion.refs_0_), channel_id=1, source_target_pairs={{0,64},{4,20},{8,72},{12,28},{16,80},{20,4},{24,88},{28,12},{32,96... | collective-permute-start | bytes 3145736 | tf_op jit(solution)/shard_map/ppermute | solution.py:260
  37.5 0.1 select_reduce_fusion
  37.6 0.5 broadcast.288
  38.1 0.0 copy-done.3
  38.1 0.7 reduce.3
  38.8 0.1 reshape.130.pick_ref
  38.9 0.0 copy-done
  38.9 1.8 %fusion.17 = f32[512,192]{0,1:T(8,128)S(1)} fusion(bf16[512,1792]{1,0:T(8,128)(2,1)S(1)} %copy-done, bf16[1792,192]{0,1:T(8,128)(2,1)} %param.9), kind=kOutput, calls=%fused_computation.73 | convolution fusion | flops 352321536 | bytes 2916352 | tf_op jit(solution)/shard_map/dot_general | solution.py:238
  40.8 2.8 %collective-permute-start.9 = (f32[48,512]{1,0:T(8,128)S(1)}, f32[48,512]{1,0:T(8,128)S(1)}, u32[]{:S(2)}, u32[]{:S(2)}) collective-permute-start(f32[48,512]{1,0:T(8,128)S(1)} %get-tuple-element.33), channel_id=1, source_target_pairs={{0,3},{1,0},{2,1},{3,2},{4,7},{5,4},{6,5},{7,6},{8,11},{9,8},{10,9... | collective-permute-start | bytes 294920 | tf_op jit(solution)/shard_map/ppermute | solution.py:252
  43.6 0.3 collective-permute-start.8
  44.0 0.7 collective-permute-start.7
  44.7 0.0 copy-done.1
  44.7 0.0 copy-done.2
  44.7 6.2 %collective-permute-start.10 = (bf16[2048,256]{1,0:T(8,128)(2,1)S(1)}, bf16[2048,256]{1,0:T(8,128)(2,1)}, u32[]{:S(2)}, u32[]{:S(2)}) collective-permute-start(bf16[2048,256]{1,0:T(8,128)(2,1)S(1)} %pad_maximum_fusion.refs_0_), channel_id=1, source_target_pairs={{0,4},{4,0},{8,12},{12,8},{16,20},{20,16},{24,28},{28,24},{32,36},... | collective-permute-start | bytes 3145736 | tf_op jit(solution)/shard_map/ppermute | solution.py:260
  50.9 0.0 collective-permute-done.9
  50.9 0.5 collective-permute-start.11
  51.4 0.0 collective-permute-done.8
  51.4 4.0 %collective-permute-start.13 = (bf16[2048,256]{1,0:T(8,128)(2,1)}, bf16[2048,256]{1,0:T(8,128)(2,1)}, u32[]{:S(2)}, u32[]{:S(2)}) collective-permute-start(bf16[2048,256]{1,0:T(8,128)(2,1)} %collective-permute-done.4.refs_3_), channel_id=1, source_target_pairs={{0,4},{4,0},{8,12},{12,8},{16,20},{20,16},{24,28},{28,24},{32,36},... | collective-permute-start | bytes 3145736 | tf_op jit(solution)/shard_map/ppermute | solution.py:260
  55.4 0.0 collective-permute-done.7
  55.5 0.1 reshape.131
  55.6 0.0 collective-permute-done.6.refs_2_
  55.6 1.4 %collective-permute-start.12 = (bf16[2048,256]{1,0:T(8,128)(2,1)}, bf16[2048,256]{1,0:T(8,128)(2,1)S(1)}, u32[]{:S(2)}, u32[]{:S(2)}) collective-permute-start(bf16[2048,256]{1,0:T(8,128)(2,1)} %collective-permute-done.6.refs_2_), channel_id=1, source_target_pairs={{0,4},{4,0},{8,12},{12,8},{16,20},{20,16},{24,28},{28,24},{32,36},... | collective-permute-start | bytes 3145736 | tf_op jit(solution)/shard_map/ppermute | solution.py:260
  57.0 0.0 collective-permute-done.10.refs_4_
  57.0 0.0 collective-permute-done.11.refs_5_
  57.0 1.0 %collective-permute-done.13.refs_7_ = bf16[2048,256]{1,0:T(8,128)(2,1)} collective-permute-done((bf16[2048,256]{1,0:T(8,128)(2,1)}, bf16[2048,256]{1,0:T(8,128)(2,1)}, u32[]{:S(2)}, u32[]{:S(2)}) %collective-permute-start.13) | collective-permute-done | bytes 1048608 | tf_op jit(solution)/shard_map/ppermute | solution.py:260
  58.0 1.5 %collective-permute-done.12.refs_6_ = bf16[2048,256]{1,0:T(8,128)(2,1)S(1)} collective-permute-done((bf16[2048,256]{1,0:T(8,128)(2,1)}, bf16[2048,256]{1,0:T(8,128)(2,1)S(1)}, u32[]{:S(2)}, u32[]{:S(2)}) %collective-permute-start.12) | collective-permute-done | bytes 1048608 | tf_op jit(solution)/shard_map/ppermute | solution.py:260
  59.5 38.2 %far.1 = bf16[8192,128]{1,0:T(8,128)(2,1)} custom-call(s32[128]{0:T(128)S(1)} %reshape.130.pick_ref, s32[128]{0:T(128)S(1)} %fusion.16.row_ref, s32[1]{0:T(128)} %bitcast.1.index_ref, bf16[8192,128]{1,0:T(8,128)(2,1)} %bitcast.26, f32[8,3,16,64]{3,2,1,0:T(8,128)S(1)} %bitcast.23, f32[8192,128]{1,0:T(8,128)} %near.1.win_ref, s32[1,256]{1,0:T(1,128)S(1)} %bitcast.24, ...), custom_call_target="tpu_custom_call" | custom-call | flops 10737418240 | bytes 20971520 | tf_op jit(solution)/shard_map/far/pallas_call | solution.py:330
  (6 shorter events, 0.2 us)
Async XLA Ops:
  0.0 38.9 %copy-start = (bf16[512,1792]{1,0:T(8,128)(2,1)S(1)}, bf16[512,1792]{1,0:T(8,128)(2,1)}, u32[]{:S(2)}) copy-start(bf16[512,1792]{1,0:T(8,128)(2,1)} %param.8) | copy-start | bytes 5505028
  1.1 10.6 %collective-permute-start.2 = (bf16[512,256]{1,0:T(8,128)(2,1)S(1)}, bf16[512,256]{1,0:T(8,128)(2,1)S(1)}, u32[]{:S(2)}, u32[]{:S(2)}) collective-permute-start(bf16[512,256]{1,0:T(8,128)(2,1)S(1)} %maximum_bitcast_fusion.own_ref), channel_id=1, source_target_pairs={{0,8},{4,36},{8,16},{12,44},{16,24},{20,52},{24,0},{28,60},{32,40}... | collective-permute-start | bytes 786440 | tf_op jit(solution)/shard_map/ppermute | solution.py:260
  3.2 9.3 %collective-permute-start.1 = (bf16[512,256]{1,0:T(8,128)(2,1)S(1)}, bf16[512,256]{1,0:T(8,128)(2,1)S(1)}, u32[]{:S(2)}, u32[]{:S(2)}) collective-permute-start(bf16[512,256]{1,0:T(8,128)(2,1)S(1)} %maximum_bitcast_fusion.own_ref), channel_id=1, source_target_pairs={{0,16},{4,68},{8,24},{12,76},{16,0},{20,84},{24,8},{28,92},{32,48}... | collective-permute-start | bytes 786440 | tf_op jit(solution)/shard_map/ppermute | solution.py:260
  5.7 6.9 %collective-permute-start = (bf16[512,256]{1,0:T(8,128)(2,1)S(1)}, bf16[512,256]{1,0:T(8,128)(2,1)S(1)}, u32[]{:S(2)}, u32[]{:S(2)}) collective-permute-start(bf16[512,256]{1,0:T(8,128)(2,1)S(1)} %maximum_bitcast_fusion.own_ref), channel_id=1, source_target_pairs={{0,24},{4,100},{8,0},{12,108},{16,8},{20,116},{24,16},{28,124},{32... | collective-permute-start | bytes 786440 | tf_op jit(solution)/shard_map/ppermute | solution.py:260
  6.9 9.4 %collective-permute-start.5 = (bf16[512,256]{1,0:T(8,128)(2,1)S(1)}, bf16[512,256]{1,0:T(8,128)(2,1)S(1)}, u32[]{:S(2)}, u32[]{:S(2)}) collective-permute-start(bf16[512,256]{1,0:T(8,128)(2,1)S(1)} %maximum_bitcast_fusion.own_ref), channel_id=1, source_target_pairs={{0,4},{4,8},{8,12},{12,16},{16,20},{20,24},{24,28},{28,32},{32,36}... | collective-permute-start | bytes 786440 | tf_op jit(solution)/shard_map/ppermute | solution.py:260
  12.6 23.5 %collective-permute-start.4 = (bf16[2048,256]{1,0:T(8,128)(2,1)S(1)}, bf16[2048,256]{1,0:T(8,128)(2,1)}, u32[]{:S(2)}, u32[]{:S(2)}) collective-permute-start(bf16[2048,256]{1,0:T(8,128)(2,1)S(1)} %pad_maximum_fusion.refs_0_), channel_id=1, source_target_pairs={{0,32},{4,12},{8,40},{12,20},{16,48},{20,28},{24,56},{28,4},{32,64... | collective-permute-start | bytes 3145736 | tf_op jit(solution)/shard_map/ppermute | solution.py:260
  14.0 22.1 %collective-permute-start.3 = (bf16[2048,256]{1,0:T(8,128)(2,1)S(1)}, bf16[2048,256]{1,0:T(8,128)(2,1)}, u32[]{:S(2)}, u32[]{:S(2)}) collective-permute-start(bf16[2048,256]{1,0:T(8,128)(2,1)S(1)} %pad_maximum_fusion.refs_0_), channel_id=1, source_target_pairs={{0,96},{4,28},{8,104},{12,4},{16,112},{20,12},{24,120},{28,20},{32... | collective-permute-start | bytes 3145736 | tf_op jit(solution)/shard_map/ppermute | solution.py:260
  16.3 21.9 %copy-start.3 = (s32[8,1,16]{2,1,0:T(1,128)S(1)}, s32[8,1,16]{2,1,0:T(1,128)}, u32[]{:S(2)}) copy-start(s32[8,1,16]{2,1,0:T(1,128)} %param.15) | copy-start | bytes 1540
  36.2 8.5 %copy-start.1 = (f32[64,128]{1,0:T(8,128)S(1)}, f32[64,128]{1,0:T(8,128)}, u32[]{:S(2)}) copy-start(f32[64,128]{1,0:T(8,128)} %param.14) | copy-start | bytes 98308
  36.2 8.5 %copy-start.2 = (f32[64,128]{1,0:T(8,128)S(1)}, f32[64,128]{1,0:T(8,128)}, u32[]{:S(2)}) copy-start(f32[64,128]{1,0:T(8,128)} %param.13) | copy-start | bytes 98308
  36.2 19.4 %collective-permute-start.6 = (bf16[2048,256]{1,0:T(8,128)(2,1)S(1)}, bf16[2048,256]{1,0:T(8,128)(2,1)}, u32[]{:S(2)}, u32[]{:S(2)}) collective-permute-start(bf16[2048,256]{1,0:T(8,128)(2,1)S(1)} %pad_maximum_fusion.refs_0_), channel_id=1, source_target_pairs={{0,64},{4,20},{8,72},{12,28},{16,80},{20,4},{24,88},{28,12},{32,96... | collective-permute-start | bytes 3145736 | tf_op jit(solution)/shard_map/ppermute | solution.py:260
  40.8 10.1 %collective-permute-start.9 = (f32[48,512]{1,0:T(8,128)S(1)}, f32[48,512]{1,0:T(8,128)S(1)}, u32[]{:S(2)}, u32[]{:S(2)}) collective-permute-start(f32[48,512]{1,0:T(8,128)S(1)} %get-tuple-element.33), channel_id=1, source_target_pairs={{0,3},{1,0},{2,1},{3,2},{4,7},{5,4},{6,5},{7,6},{8,11},{9,8},{10,9... | collective-permute-start | bytes 294920 | tf_op jit(solution)/shard_map/ppermute | solution.py:252
  43.6 7.8 %collective-permute-start.8 = (f32[48,512]{1,0:T(8,128)S(1)}, f32[48,512]{1,0:T(8,128)S(1)}, u32[]{:S(2)}, u32[]{:S(2)}) collective-permute-start(f32[48,512]{1,0:T(8,128)S(1)} %get-tuple-element.34), channel_id=1, source_target_pairs={{0,2},{1,3},{2,0},{3,1},{4,6},{5,7},{6,4},{7,5},{8,10},{9,11},{10,... | collective-permute-start | bytes 294920 | tf_op jit(solution)/shard_map/ppermute | solution.py:252
  44.0 11.4 %collective-permute-start.7 = (f32[48,512]{1,0:T(8,128)S(1)}, f32[48,512]{1,0:T(8,128)S(1)}, u32[]{:S(2)}, u32[]{:S(2)}) collective-permute-start(f32[48,512]{1,0:T(8,128)S(1)} %get-tuple-element.35), channel_id=1, source_target_pairs={{0,1},{1,2},{2,3},{3,0},{4,5},{5,6},{6,7},{7,4},{8,9},{9,10},{10,1... | collective-permute-start | bytes 294920 | tf_op jit(solution)/shard_map/ppermute | solution.py:252
  44.7 12.3 %collective-permute-start.10 = (bf16[2048,256]{1,0:T(8,128)(2,1)S(1)}, bf16[2048,256]{1,0:T(8,128)(2,1)}, u32[]{:S(2)}, u32[]{:S(2)}) collective-permute-start(bf16[2048,256]{1,0:T(8,128)(2,1)S(1)} %pad_maximum_fusion.refs_0_), channel_id=1, source_target_pairs={{0,4},{4,0},{8,12},{12,8},{16,20},{20,16},{24,28},{28,24},{32,36},... | collective-permute-start | bytes 3145736 | tf_op jit(solution)/shard_map/ppermute | solution.py:260
  50.9 6.1 %collective-permute-start.11 = (bf16[2048,256]{1,0:T(8,128)(2,1)}, bf16[2048,256]{1,0:T(8,128)(2,1)}, u32[]{:S(2)}, u32[]{:S(2)}) collective-permute-start(bf16[2048,256]{1,0:T(8,128)(2,1)} %collective-permute-done.3.refs_1_), channel_id=1, source_target_pairs={{0,4},{4,0},{8,12},{12,8},{16,20},{20,16},{24,28},{28,24},{32,36},... | collective-permute-start | bytes 3145736 | tf_op jit(solution)/shard_map/ppermute | solution.py:260
  51.4 6.6 %collective-permute-start.13 = (bf16[2048,256]{1,0:T(8,128)(2,1)}, bf16[2048,256]{1,0:T(8,128)(2,1)}, u32[]{:S(2)}, u32[]{:S(2)}) collective-permute-start(bf16[2048,256]{1,0:T(8,128)(2,1)} %collective-permute-done.4.refs_3_), channel_id=1, source_target_pairs={{0,4},{4,0},{8,12},{12,8},{16,20},{20,16},{24,28},{28,24},{32,36},... | collective-permute-start | bytes 3145736 | tf_op jit(solution)/shard_map/ppermute | solution.py:260
  55.6 3.9 %collective-permute-start.12 = (bf16[2048,256]{1,0:T(8,128)(2,1)}, bf16[2048,256]{1,0:T(8,128)(2,1)S(1)}, u32[]{:S(2)}, u32[]{:S(2)}) collective-permute-start(bf16[2048,256]{1,0:T(8,128)(2,1)} %collective-permute-done.6.refs_2_), channel_id=1, source_target_pairs={{0,4},{4,0},{8,12},{12,8},{16,20},{20,16},{24,28},{28,24},{32,36},... | collective-permute-start | bytes 3145736 | tf_op jit(solution)/shard_map/ppermute | solution.py:260

commit v7 on v6

--- a/solution.py
+++ b/solution.py
@@ -394,7 +394,10 @@
         jnp.where(placed[None, :] == slots[:, None], block_ids[None, :], 0), axis=1, dtype=jnp.int32
     ).reshape(1, total_blocks)
 
-    near = functools.partial(run_near, index, queries, previous, key_value, heads_here)
+    early, chosen, source_rows, ids_by_slot, compress_w = lax.optimization_barrier(
+        (index, chosen, source_rows, ids_by_slot, compress_w)
+    )
+    near = functools.partial(run_near, early, queries, previous, key_value, heads_here)
 
     def late_inputs(win):
         after, _ = lax.optimization_barrier((hidden_in, win))

time: 98.1 us -> 102 us (1.040)
  other arithmetic: 2.08 us -> 4.14 us
  local copies, waits for them, and re-layouts: 0.77 us -> 2.25 us
    concatenate x1, other arithmetic: 0.07 us -> 1.18 us  [gather_pieces(): line = jnp.concatenate(line, axis=0)]
  transfers between devices with their start and end apart: 14 -> 14, of which waited for: 3 -> 3; matrix products, arithmetic and copies ran while one was open for 4% -> 6% of each run, Pallas kernels for 20% -> 20%
where the time goes in v7:
time: 102 us; the launch traced here: 101 us
  Pallas kernels  58.1 us (57%)
  starting transfers between devices  31.5 us (31%)
  other arithmetic  4.14 us (4%)
  waiting for transfers between devices  3.13 us (3%)
  local copies, waits for them, and re-layouts  2.25 us (2%)
  matrix products  1.84 us (2%)
    pallas_call x1, Pallas kernels, run_far(): pl.pallas_call(functools.partial(far_kernel, block_len, heads, picks, pla...  38.2 us
    ppermute x11, starting transfers between devices, send(): return lax.ppermute(value, 'ctx', perm)  27.7 us
    pallas_call x1, Pallas kernels, run_near(): pl.pallas_call(functools.partial(near_kernel, heads), out_shape=pltpu.HBM...  19.9 us
    ppermute x3, starting transfers between devices, gate_logits(): lax.ppermute(chunk(mine + steps), 'head', [(n, (n + steps) % parts) for n...  3.77 us
    ppermute x11, waiting for transfers between devices, send(): return lax.ppermute(value, 'ctx', perm)  3.12 us
  transfers between devices with their start and end apart: 14, of which 3 were waited for; matrix products, arithmetic and copies ran while one was open for 6% of the time, Pallas kernels for 20%

profile of v7, /device:TPU:1, one launch (start us, length us, event | category | flops | bytes accessed | tf_op | source)
XLA Modules:
  0.0 101.3 jit_solution(9737702943597463076)
XLA Ops:
  0.0 0.0 copy-start
  0.0 0.0 copy-start.6
  0.0 1.1 %maximum_bitcast_fusion.own_ref = bf16[512,256]{1,0:T(8,128)(2,1)S(1)} fusion(bf16[512,1,128]{2,0,1:T(8,128)(2,1)} %param.12, bf16[512,1,128]{2,0,1:T(8,128)(2,1)} %param.11), kind=kLoop, calls=%fused_computation.1 | loop fusion | flops 524288 | bytes 524288 | tf_op jit(solution)/shard_map/reshape | solution.py:382
  1.2 2.1 %collective-permute-start.2 = (bf16[512,256]{1,0:T(8,128)(2,1)S(1)}, bf16[512,256]{1,0:T(8,128)(2,1)S(1)}, u32[]{:S(2)}, u32[]{:S(2)}) collective-permute-start(bf16[512,256]{1,0:T(8,128)(2,1)S(1)} %maximum_bitcast_fusion.own_ref), channel_id=1, source_target_pairs={{0,8},{4,36},{8,16},{12,44},{16,24},{20,52},{24,0},{28,60},{32,40}... | collective-permute-start | bytes 786440 | tf_op jit(solution)/shard_map/ppermute | solution.py:260
  3.3 2.5 %collective-permute-start.1 = (bf16[512,256]{1,0:T(8,128)(2,1)S(1)}, bf16[512,256]{1,0:T(8,128)(2,1)S(1)}, u32[]{:S(2)}, u32[]{:S(2)}) collective-permute-start(bf16[512,256]{1,0:T(8,128)(2,1)S(1)} %maximum_bitcast_fusion.own_ref), channel_id=1, source_target_pairs={{0,16},{4,68},{8,24},{12,76},{16,0},{20,84},{24,8},{28,92},{32,48}... | collective-permute-start | bytes 786440 | tf_op jit(solution)/shard_map/ppermute | solution.py:260
  5.7 1.2 %collective-permute-start = (bf16[512,256]{1,0:T(8,128)(2,1)S(1)}, bf16[512,256]{1,0:T(8,128)(2,1)}, u32[]{:S(2)}, u32[]{:S(2)}) collective-permute-start(bf16[512,256]{1,0:T(8,128)(2,1)S(1)} %maximum_bitcast_fusion.own_ref), channel_id=1, source_target_pairs={{0,24},{4,100},{8,0},{12,108},{16,8},{20,116},{24,16},{28,124},{32... | collective-permute-start | bytes 786440 | tf_op jit(solution)/shard_map/ppermute | solution.py:260
  6.9 4.9 %collective-permute-start.5 = (bf16[512,256]{1,0:T(8,128)(2,1)S(1)}, bf16[512,256]{1,0:T(8,128)(2,1)S(1)}, u32[]{:S(2)}, u32[]{:S(2)}) collective-permute-start(bf16[512,256]{1,0:T(8,128)(2,1)S(1)} %maximum_bitcast_fusion.own_ref), channel_id=1, source_target_pairs={{0,4},{4,8},{8,12},{12,16},{16,20},{20,24},{24,28},{28,32},{32,36}... | collective-permute-start | bytes 786440 | tf_op jit(solution)/shard_map/ppermute | solution.py:260
  11.8 0.1 select_reduce_fusion
  11.9 0.0 collective-permute-done.2
  12.0 0.0 copy-start.1
  12.0 0.6 collective-permute-done.1
  12.6 0.1 copy-done.1
  12.7 0.7 copy-done.2
  13.4 0.0 collective-permute-done
  13.4 1.2 %pad_maximum_fusion.refs_0_ = bf16[2048,256]{1,0:T(8,128)(2,1)S(1)} fusion(bf16[512,256]{1,0:T(8,128)(2,1)} %copy-done.1, bf16[512,256]{1,0:T(8,128)(2,1)} %copy-done.2, bf16[512,256]{1,0:T(8,128)(2,1)} %collective-permute-done, bf16[512,256]{1,0:T(8,128)(2,1)S(1)} %maximum_bitcast_fusion.own_ref), kind=kLoop, calls=%fused_computation | loop fusion | flops 4194304 | bytes 2097152 | tf_op jit(solution)/shard_map/concatenate | solution.py:271
  14.5 1.3 %collective-permute-start.4 = (bf16[2048,256]{1,0:T(8,128)(2,1)S(1)}, bf16[2048,256]{1,0:T(8,128)(2,1)}, u32[]{:S(2)}, u32[]{:S(2)}) collective-permute-start(bf16[2048,256]{1,0:T(8,128)(2,1)S(1)} %pad_maximum_fusion.refs_0_), channel_id=1, source_target_pairs={{0,32},{4,12},{8,40},{12,20},{16,48},{20,28},{24,56},{28,4},{32,64... | collective-permute-start | bytes 3145736 | tf_op jit(solution)/shard_map/ppermute | solution.py:260
  15.9 2.2 %collective-permute-start.3 = (bf16[2048,256]{1,0:T(8,128)(2,1)S(1)}, bf16[2048,256]{1,0:T(8,128)(2,1)}, u32[]{:S(2)}, u32[]{:S(2)}) collective-permute-start(bf16[2048,256]{1,0:T(8,128)(2,1)S(1)} %pad_maximum_fusion.refs_0_), channel_id=1, source_target_pairs={{0,96},{4,28},{8,104},{12,4},{16,112},{20,12},{24,120},{28,20},{32... | collective-permute-start | bytes 3145736 | tf_op jit(solution)/shard_map/ppermute | solution.py:260
  18.1 0.0 copy-done.4
  18.1 0.0 copy-done.5
  18.1 0.5 broadcast.288
  18.6 0.7 reduce.3
  19.3 0.1 reshape.129.pick_ref
  19.4 0.0 collective-permute-done.5.previous_ref
  19.4 19.9 %near.1.win_ref = f32[8192,128]{1,0:T(8,128)} custom-call(s32[1]{0:T(128)} %bitcast.1.index_ref, bf16[8192,128]{1,0:T(8,128)(2,1)} %bitcast.25, bf16[512,256]{1,0:T(8,128)(2,1)S(1)} %collective-permute-done.5.previous_ref, bf16[512,256]{1,0:T(8,128)(2,1)S(1)} %maximum_bitcast_fusion.own_ref), custom_call_target="tpu_custom_call" | custom-call | flops 8589934592 | bytes 6291456 | tf_op jit(solution)/shard_map/near/pallas_call | solution.py:300
  39.3 0.0 collective-permute-done.4.refs_3_
  39.3 0.0 collective-permute-done.3.refs_1_
  39.3 1.3 %collective-permute-start.6 = (bf16[2048,256]{1,0:T(8,128)(2,1)S(1)}, bf16[2048,256]{1,0:T(8,128)(2,1)}, u32[]{:S(2)}, u32[]{:S(2)}) collective-permute-start(bf16[2048,256]{1,0:T(8,128)(2,1)S(1)} %pad_maximum_fusion.refs_0_), channel_id=1, source_target_pairs={{0,64},{4,20},{8,72},{12,28},{16,80},{20,4},{24,88},{28,12},{32,96... | collective-permute-start | bytes 3145736 | tf_op jit(solution)/shard_map/ppermute | solution.py:260
  40.6 0.0 copy-done
  40.6 1.8 %fusion.17 = f32[512,192]{0,1:T(8,128)S(1)} fusion(bf16[512,1792]{1,0:T(8,128)(2,1)S(1)} %copy-done, bf16[1792,192]{0,1:T(8,128)(2,1)} %param.9), kind=kOutput, calls=%fused_computation.73 | convolution fusion | flops 352321536 | bytes 2916352 | tf_op jit(solution)/shard_map/dot_general | solution.py:238
  42.4 0.7 dynamic-slice_bitcast_fusion
  43.1 2.7 %collective-permute-start.9 = (f32[48,512]{1,0:T(8,128)}, f32[48,512]{1,0:T(8,128)S(1)}, u32[]{:S(2)}, u32[]{:S(2)}) collective-permute-start(f32[48,512]{1,0:T(8,128)} %get-tuple-element.43), channel_id=1, source_target_pairs={{0,3},{1,0},{2,1},{3,2},{4,7},{5,4},{6,5},{7,6},{8,11},{9,8},{10,9... | collective-permute-start | bytes 294920 | tf_op jit(solution)/shard_map/ppermute | solution.py:252
  45.9 0.4 collective-permute-start.8
  46.2 0.7 collective-permute-start.7
  46.9 6.2 %collective-permute-start.10 = (bf16[2048,256]{1,0:T(8,128)(2,1)S(1)}, bf16[2048,256]{1,0:T(8,128)(2,1)}, u32[]{:S(2)}, u32[]{:S(2)}) collective-permute-start(bf16[2048,256]{1,0:T(8,128)(2,1)S(1)} %pad_maximum_fusion.refs_0_), channel_id=1, source_target_pairs={{0,4},{4,0},{8,12},{12,8},{16,20},{20,16},{24,28},{28,24},{32,36},... | collective-permute-start | bytes 3145736 | tf_op jit(solution)/shard_map/ppermute | solution.py:260
  53.1 0.0 collective-permute-done.9
  53.1 1.0 %collective-permute-start.11 = (bf16[2048,256]{1,0:T(8,128)(2,1)}, bf16[2048,256]{1,0:T(8,128)(2,1)}, u32[]{:S(2)}, u32[]{:S(2)}) collective-permute-start(bf16[2048,256]{1,0:T(8,128)(2,1)} %collective-permute-done.3.refs_1_), channel_id=1, source_target_pairs={{0,4},{4,0},{8,12},{12,8},{16,20},{20,16},{24,28},{28,24},{32,36},... | collective-permute-start | bytes 3145736 | tf_op jit(solution)/shard_map/ppermute | solution.py:260
  54.1 0.0 collective-permute-done.8
  54.1 3.8 %collective-permute-start.13 = (bf16[2048,256]{1,0:T(8,128)(2,1)}, bf16[2048,256]{1,0:T(8,128)(2,1)}, u32[]{:S(2)}, u32[]{:S(2)}) collective-permute-start(bf16[2048,256]{1,0:T(8,128)(2,1)} %collective-permute-done.4.refs_3_), channel_id=1, source_target_pairs={{0,4},{4,0},{8,12},{12,8},{16,20},{20,16},{24,28},{28,24},{32,36},... | collective-permute-start | bytes 3145736 | tf_op jit(solution)/shard_map/ppermute | solution.py:260
  57.9 0.0 collective-permute-done.7
  57.9 1.0 fusion.1
  58.9 0.1 reshape.132
  59.0 0.0 collective-permute-done.6.refs_2_
  59.0 1.3 %collective-permute-start.12 = (bf16[2048,256]{1,0:T(8,128)(2,1)}, bf16[2048,256]{1,0:T(8,128)(2,1)S(1)}, u32[]{:S(2)}, u32[]{:S(2)}) collective-permute-start(bf16[2048,256]{1,0:T(8,128)(2,1)} %collective-permute-done.6.refs_2_), channel_id=1, source_target_pairs={{0,4},{4,0},{8,12},{12,8},{16,20},{20,16},{24,28},{28,24},{32,36},... | collective-permute-start | bytes 3145736 | tf_op jit(solution)/shard_map/ppermute | solution.py:260
  60.4 0.0 collective-permute-done.10.refs_4_
  60.4 0.0 collective-permute-done.11.refs_5_
  60.4 0.1 collective-permute-done.13.refs_7_
  60.5 2.3 %collective-permute-done.12.refs_6_ = bf16[2048,256]{1,0:T(8,128)(2,1)S(1)} collective-permute-done((bf16[2048,256]{1,0:T(8,128)(2,1)}, bf16[2048,256]{1,0:T(8,128)(2,1)S(1)}, u32[]{:S(2)}, u32[]{:S(2)}) %collective-permute-start.12) | collective-permute-done | bytes 1048608 | tf_op jit(solution)/shard_map/ppermute | solution.py:260
  62.9 38.2 %far.1 = bf16[8192,128]{1,0:T(8,128)(2,1)} custom-call(s32[128]{0:T(128)S(1)} %reshape.129.pick_ref, s32[128]{0:T(128)S(1)} %fusion.16.row_ref, s32[1]{0:T(128)} %bitcast.1.index_ref, bf16[8192,128]{1,0:T(8,128)(2,1)} %bitcast.26, f32[8,3,16,64]{3,2,1,0:T(8,128)S(1)} %bitcast.23, f32[8192,128]{1,0:T(8,128)} %near.1.win_ref, s32[1,256]{1,0:T(1,128)S(1)} %bitcast.24, ...), custom_call_target="tpu_custom_call" | custom-call | flops 10737418240 | bytes 20971520 | tf_op jit(solution)/shard_map/far/pallas_call | solution.py:330
  (10 shorter events, 0.1 us)
Async XLA Ops:
  0.0 40.6 %copy-start = (bf16[512,1792]{1,0:T(8,128)(2,1)S(1)}, bf16[512,1792]{1,0:T(8,128)(2,1)}, u32[]{:S(2)}) copy-start(bf16[512,1792]{1,0:T(8,128)(2,1)} %param.8) | copy-start | bytes 5505028
  0.0 18.1 %copy-start.4 = (f32[64,128]{1,0:T(8,128)S(1)}, f32[64,128]{1,0:T(8,128)}, u32[]{:S(2)}) copy-start(f32[64,128]{1,0:T(8,128)} %param.14) | copy-start | bytes 98308
  0.0 18.1 %copy-start.5 = (f32[64,128]{1,0:T(8,128)S(1)}, f32[64,128]{1,0:T(8,128)}, u32[]{:S(2)}) copy-start(f32[64,128]{1,0:T(8,128)} %param.13) | copy-start | bytes 98308
  0.0 18.6 %copy-start.6 = (s32[8,1,16]{2,1,0:T(1,128)S(1)}, s32[8,1,16]{2,1,0:T(1,128)}, u32[]{:S(2)}) copy-start(s32[8,1,16]{2,1,0:T(1,128)} %param.15) | copy-start | bytes 1540
  1.2 10.8 %collective-permute-start.2 = (bf16[512,256]{1,0:T(8,128)(2,1)S(1)}, bf16[512,256]{1,0:T(8,128)(2,1)S(1)}, u32[]{:S(2)}, u32[]{:S(2)}) collective-permute-start(bf16[512,256]{1,0:T(8,128)(2,1)S(1)} %maximum_bitcast_fusion.own_ref), channel_id=1, source_target_pairs={{0,8},{4,36},{8,16},{12,44},{16,24},{20,52},{24,0},{28,60},{32,40}... | collective-permute-start | bytes 786440 | tf_op jit(solution)/shard_map/ppermute | solution.py:260
  3.3 9.3 %collective-permute-start.1 = (bf16[512,256]{1,0:T(8,128)(2,1)S(1)}, bf16[512,256]{1,0:T(8,128)(2,1)S(1)}, u32[]{:S(2)}, u32[]{:S(2)}) collective-permute-start(bf16[512,256]{1,0:T(8,128)(2,1)S(1)} %maximum_bitcast_fusion.own_ref), channel_id=1, source_target_pairs={{0,16},{4,68},{8,24},{12,76},{16,0},{20,84},{24,8},{28,92},{32,48}... | collective-permute-start | bytes 786440 | tf_op jit(solution)/shard_map/ppermute | solution.py:260
  5.7 7.6 %collective-permute-start = (bf16[512,256]{1,0:T(8,128)(2,1)S(1)}, bf16[512,256]{1,0:T(8,128)(2,1)}, u32[]{:S(2)}, u32[]{:S(2)}) collective-permute-start(bf16[512,256]{1,0:T(8,128)(2,1)S(1)} %maximum_bitcast_fusion.own_ref), channel_id=1, source_target_pairs={{0,24},{4,100},{8,0},{12,108},{16,8},{20,116},{24,16},{28,124},{32... | collective-permute-start | bytes 786440 | tf_op jit(solution)/shard_map/ppermute | solution.py:260
  6.9 12.5 %collective-permute-start.5 = (bf16[512,256]{1,0:T(8,128)(2,1)S(1)}, bf16[512,256]{1,0:T(8,128)(2,1)S(1)}, u32[]{:S(2)}, u32[]{:S(2)}) collective-permute-start(bf16[512,256]{1,0:T(8,128)(2,1)S(1)} %maximum_bitcast_fusion.own_ref), channel_id=1, source_target_pairs={{0,4},{4,8},{8,12},{12,16},{16,20},{20,24},{24,28},{28,32},{32,36}... | collective-permute-start | bytes 786440 | tf_op jit(solution)/shard_map/ppermute | solution.py:260
  12.0 0.7 copy-start.1
  12.7 0.7 copy-start.2
  14.5 24.7 %collective-permute-start.4 = (bf16[2048,256]{1,0:T(8,128)(2,1)S(1)}, bf16[2048,256]{1,0:T(8,128)(2,1)}, u32[]{:S(2)}, u32[]{:S(2)}) collective-permute-start(bf16[2048,256]{1,0:T(8,128)(2,1)S(1)} %pad_maximum_fusion.refs_0_), channel_id=1, source_target_pairs={{0,32},{4,12},{8,40},{12,20},{16,48},{20,28},{24,56},{28,4},{32,64... | collective-permute-start | bytes 3145736 | tf_op jit(solution)/shard_map/ppermute | solution.py:260
  15.9 23.4 %collective-permute-start.3 = (bf16[2048,256]{1,0:T(8,128)(2,1)S(1)}, bf16[2048,256]{1,0:T(8,128)(2,1)}, u32[]{:S(2)}, u32[]{:S(2)}) collective-permute-start(bf16[2048,256]{1,0:T(8,128)(2,1)S(1)} %pad_maximum_fusion.refs_0_), channel_id=1, source_target_pairs={{0,96},{4,28},{8,104},{12,4},{16,112},{20,12},{24,120},{28,20},{32... | collective-permute-start | bytes 3145736 | tf_op jit(solution)/shard_map/ppermute | solution.py:260
  39.3 19.7 %collective-permute-start.6 = (bf16[2048,256]{1,0:T(8,128)(2,1)S(1)}, bf16[2048,256]{1,0:T(8,128)(2,1)}, u32[]{:S(2)}, u32[]{:S(2)}) collective-permute-start(bf16[2048,256]{1,0:T(8,128)(2,1)S(1)} %pad_maximum_fusion.refs_0_), channel_id=1, source_target_pairs={{0,64},{4,20},{8,72},{12,28},{16,80},{20,4},{24,88},{28,12},{32,96... | collective-permute-start | bytes 3145736 | tf_op jit(solution)/shard_map/ppermute | solution.py:260
  43.1 9.9 %collective-permute-start.9 = (f32[48,512]{1,0:T(8,128)}, f32[48,512]{1,0:T(8,128)S(1)}, u32[]{:S(2)}, u32[]{:S(2)}) collective-permute-start(f32[48,512]{1,0:T(8,128)} %get-tuple-element.43), channel_id=1, source_target_pairs={{0,3},{1,0},{2,1},{3,2},{4,7},{5,4},{6,5},{7,6},{8,11},{9,8},{10,9... | collective-permute-start | bytes 294920 | tf_op jit(solution)/shard_map/ppermute | solution.py:252
  45.9 8.3 %collective-permute-start.8 = (f32[48,512]{1,0:T(8,128)}, f32[48,512]{1,0:T(8,128)S(1)}, u32[]{:S(2)}, u32[]{:S(2)}) collective-permute-start(f32[48,512]{1,0:T(8,128)} %get-tuple-element.44), channel_id=1, source_target_pairs={{0,2},{1,3},{2,0},{3,1},{4,6},{5,7},{6,4},{7,5},{8,10},{9,11},{10,... | collective-permute-start | bytes 294920 | tf_op jit(solution)/shard_map/ppermute | solution.py:252
  46.2 11.7 %collective-permute-start.7 = (f32[48,512]{1,0:T(8,128)}, f32[48,512]{1,0:T(8,128)}, u32[]{:S(2)}, u32[]{:S(2)}) collective-permute-start(f32[48,512]{1,0:T(8,128)} %get-tuple-element.45), channel_id=1, source_target_pairs={{0,1},{1,2},{2,3},{3,0},{4,5},{5,6},{6,7},{7,4},{8,9},{9,10},{10,1... | collective-permute-start | bytes 294920 | tf_op jit(solution)/shard_map/ppermute | solution.py:252
  46.9 13.4 %collective-permute-start.10 = (bf16[2048,256]{1,0:T(8,128)(2,1)S(1)}, bf16[2048,256]{1,0:T(8,128)(2,1)}, u32[]{:S(2)}, u32[]{:S(2)}) collective-permute-start(bf16[2048,256]{1,0:T(8,128)(2,1)S(1)} %pad_maximum_fusion.refs_0_), channel_id=1, source_target_pairs={{0,4},{4,0},{8,12},{12,8},{16,20},{20,16},{24,28},{28,24},{32,36},... | collective-permute-start | bytes 3145736 | tf_op jit(solution)/shard_map/ppermute | solution.py:260
  53.1 7.3 %collective-permute-start.11 = (bf16[2048,256]{1,0:T(8,128)(2,1)}, bf16[2048,256]{1,0:T(8,128)(2,1)}, u32[]{:S(2)}, u32[]{:S(2)}) collective-permute-start(bf16[2048,256]{1,0:T(8,128)(2,1)} %collective-permute-done.3.refs_1_), channel_id=1, source_target_pairs={{0,4},{4,0},{8,12},{12,8},{16,20},{20,16},{24,28},{28,24},{32,36},... | collective-permute-start | bytes 3145736 | tf_op jit(solution)/shard_map/ppermute | solution.py:260
  54.1 3.8 %copy-start.3 = (f32[48,512]{1,0:T(8,128)}, f32[48,512]{1,0:T(8,128)S(1)}, u32[]{:S(2)}) copy-start(f32[48,512]{1,0:T(8,128)S(1)} %collective-permute-done.8) | copy-start | bytes 294916
  54.1 6.4 %collective-permute-start.13 = (bf16[2048,256]{1,0:T(8,128)(2,1)}, bf16[2048,256]{1,0:T(8,128)(2,1)}, u32[]{:S(2)}, u32[]{:S(2)}) collective-permute-start(bf16[2048,256]{1,0:T(8,128)(2,1)} %collective-permute-done.4.refs_3_), channel_id=1, source_target_pairs={{0,4},{4,0},{8,12},{12,8},{16,20},{20,16},{24,28},{28,24},{32,36},... | collective-permute-start | bytes 3145736 | tf_op jit(solution)/shard_map/ppermute | solution.py:260
  59.0 3.8 %collective-permute-start.12 = (bf16[2048,256]{1,0:T(8,128)(2,1)}, bf16[2048,256]{1,0:T(8,128)(2,1)S(1)}, u32[]{:S(2)}, u32[]{:S(2)}) collective-permute-start(bf16[2048,256]{1,0:T(8,128)(2,1)} %collective-permute-done.6.refs_2_), channel_id=1, source_target_pairs={{0,4},{4,0},{8,12},{12,8},{16,20},{20,16},{24,28},{28,24},{32,36},... | collective-permute-start | bytes 3145736 | tf_op jit(solution)/shard_map/ppermute | solution.py:260
